TPU v7x, 32 devices: a whole 2x2x4 slice. The times are simulated.
32 devices in a mesh: users: 16 (over z, y, core), heads: 2 (over x).
Axes of the slice: x: 2, y: 2, z: 4, core: 2. Of those that a mesh axis runs over, the one named last changes fastest.
Arguments:
- sessions: bfloat16 [8192, 4096], P(('users', 'heads')), parts along dimension 0, may hold values from -16 to 16
- input_weight: bfloat16 [3, 4096, 2048], P(None, None, 'heads'), may hold values from -1 to 1
- output_weight: bfloat16 [2048, 4096], P('heads'), may hold values from -0.359375 to 0.359375
- session_counts: int32 [32], P('users'), parts along dimension 0, may hold values from 1 to 384, 512 in all
Outputs:
- attended: bfloat16 [8192, 4096], P(('users', 'heads')), parts along dimension 0
There are 16 independent parts, one for each index of `users`. A program takes and returns all parts, laid end to end along the dimension named above; an argument that names none is the same for every part. Nothing has to cross between parts.
Inputs may be any that keep to these rules, and one draw needn't show every extreme that they name: `session_counts`: the 2 counts sum to 512.
All inputs are finite; a program needn't handle non-finite values.
Results may differ from a plain program's by a relative error of at most 0.015.
Values may be sent and summed in bfloat16 or wider, within the bound.
No kernel may reach another device: no remote copies, remote signals or barrier semaphores. Data moves between devices by JAX's collectives and lax.ppermute only.
A program may use at most 128 MiB of HBM per device.

v0:
```python
import jax
import jax.numpy as jnp
from jax import lax
from jax.sharding import PartitionSpec as P

HD = 128


def permitted(total, counts):
    positions = jnp.arange(total, dtype=jnp.int32)
    ends = jnp.cumsum(counts)
    row_user = jnp.sum((positions[:, None] >= ends[None, :]).astype(jnp.int32), axis=1)
    same_user = row_user[:, None] == row_user[None, :]
    return jnp.logical_and(same_user, positions[:, None] >= positions[None, :])


def attend(packed, allowed):
    total = packed.shape[1]
    width = packed.shape[2]
    block = min(512, total)
    count = total // block
    queries = packed[0].reshape(count, block, width // HD, HD)
    key_rows = packed[1].reshape(total, width // HD, HD)
    values = packed[2].reshape(total, width // HD, HD)
    masks = allowed.reshape(count, block, total)

    def one_block(pair):
        query_block, mask_block = pair
        scores = jnp.einsum(
            "qhe,khe->hqk", query_block, key_rows, preferred_element_type=jnp.float32
        ) * HD ** (-0.5)
        scores = jnp.where(mask_block[None], scores, -1e30)
        highest = jnp.max(scores, axis=2, keepdims=True)
        raised = jnp.where(mask_block[None], jnp.exp(scores - highest), 0.0)
        attn_probs = (raised / jnp.sum(raised, axis=2, keepdims=True)).astype(jnp.bfloat16)
        mixed = jnp.einsum("hqk,khe->qhe", attn_probs, values, preferred_element_type=jnp.float32)
        return mixed.astype(jnp.bfloat16).reshape(block, width)

    blocks_out = lax.map(one_block, (queries, masks))
    return blocks_out.reshape(total, width)


def per_device(sessions, input_weight, output_weight, session_counts):
    packed = jnp.einsum(
        "nd,cde->cne",
        lax.all_gather(sessions, "heads", axis=0, tiled=True),
        input_weight,
        preferred_element_type=jnp.float32,
    ).astype(jnp.bfloat16)
    total = packed.shape[1]
    allowed = permitted(total, session_counts)
    mixed = attend(packed, allowed)
    return lax.psum_scatter(
        jnp.dot(mixed, output_weight, preferred_element_type=jnp.float32).astype(jnp.bfloat16),
        "heads",
        scatter_dimension=0,
        tiled=True,
    )


def solution(mesh):
    in_specs = (P(("users", "heads"), None), P(None, None, "heads"), P("heads", None), P("users"))
    out_specs = P(("users", "heads"), None)
    return jax.shard_map(
        per_device, mesh=mesh, in_specs=in_specs, out_specs=out_specs, check_vma=False
    )
```

profile of v0, /device:TPU:0, one launch (start us, length us, event | category | flops | bytes accessed | tf_op | source)
XLA Modules:
  0.0 167.7 jit_solution(7120729407783168606)
XLA Ops:
  6.5 0.0 all-gather.2.cloned.1.call-start
  6.5 0.7 all-gather.2.cloned.1.call-update
  7.3 0.0 reduce-scatter.2.cloned.1.call-start
  7.3 0.8 reduce-window.8
  8.1 0.1 fusion.14
  8.2 0.2 fusion.11
  8.4 59.9 %all-gather.2.cloned.1.call-done = bf16[512,4096]{1,0:T(8,128)(2,1)} async-done(((bf16[256,4096]{1,0:T(8,128)(2,1)}), bf16[512,4096]{1,0:T(8,128)(2,1)}) %all-gather.2.cloned.1.call-update) | async-done | bytes 4194320 | tf_op jit(solution)/shard_map/all_gather | solution.py:46
  68.4 18.2 %convert_bitcast_fusion = bf16[3,512,1024]{1,2,0:T(8,128)(2,1)S(1)} fusion(bf16[3,4096,1024]{2,1,0:T(8,128)(2,1)} %param.5, bf16[512,4096]{1,0:T(8,128)(2,1)} %all-gather.2.cloned.1.call-done), kind=kOutput, calls=%fused_computation.12 | convolution fusion | flops 12886474752 | bytes 32505856 | tf_op jit(solution)/shard_map/nd,cde->cne/dot_general | solution.py:44
  86.6 0.2 fusion.17
  86.8 5.9 %fusion.18 = (f32[8,512]{1,0:T(8,128)S(1)}, f32[8,512,512]{1,2,0:T(8,128)}) fusion(pred[512,512]{0,1:T(8,128)(4,1)S(1)} %fusion.11, bf16[512,8,128]{0,2,1:T(8,128)(2,1)S(1)} %bitcast.25, bf16[512,8,128]{0,2,1:T(8,128)(2,1)S(1)} %bitcast.24), kind=kOutput, calls=%fused_computation.22 | convolution fusion | flops 547357184 | bytes 10764288 | tf_op jit(solution)/shard_map/while/body/eval_jaxpr/sub | solution.py:34
  92.7 4.1 %fusion.10 = bf16[8,128,512]{2,1,0:T(8,128)(2,1)S(1)} fusion(bf16[512,8,128]{0,2,1:T(8,128)(2,1)S(1)} %bitcast.23, f32[8,512,512]{1,2,0:T(8,128)} %get-tuple-element.26, f32[8,512]{1,0:T(8,128)S(1)} %get-tuple-element.24), kind=kOutput, calls=%fused_computation.13 | convolution fusion | flops 541589504 | bytes 10502144 | tf_op jit(solution)/shard_map/while/body/eval_jaxpr/hqk,khe->qhe/dot_general | solution.py:36
  96.8 9.5 %convolution_convert_fusion = bf16[512,4096]{1,0:T(8,128)(2,1)} fusion(bf16[512,1024]{0,1:T(8,128)(2,1)S(1)} %bitcast.28, bf16[1024,4096]{1,0:T(8,128)(2,1)} %param.6), kind=kOutput, calls=%fused_computation.5 | convolution fusion | flops 4297064448 | bytes 13631488 | tf_op jit(solution)/shard_map/dot_general | solution.py:54
  106.3 0.0 reduce-scatter.2.cloned.1.call-update
  106.4 54.5 %reduce-scatter.2.cloned.1.call-done = bf16[256,4096]{1,0:T(8,128)(2,1)} async-done(((bf16[512,4096]{1,0:T(8,128)(2,1)}), bf16[256,4096]{1,0:T(8,128)(2,1)}) %reduce-scatter.2.cloned.1.call-update) | async-done | bytes 2097168 | tf_op jit(solution)/shard_map/reduce_scatter | solution.py:53
Async XLA Ops:
  6.5 61.8 %all-gather.2.cloned.1.call-start = ((), (), s32[]{:S(2)}) async-start(), calls=%async_computation.1 | async-start | bytes 6291456 | tf_op jit(solution)/shard_map/all_gather | solution.py:46
  7.3 153.6 %reduce-scatter.2.cloned.1.call-start = ((), (), s32[]{:S(2)}) async-start(), calls=%async_computation.2 | async-start | bytes 6291456 | tf_op jit(solution)/shard_map/reduce_scatter | solution.py:53
Sparse Core Ops, SparseCore 0:
  8.9 59.4 all-gather.1
  106.5 54.3 reduce-scatter.1
where the time goes:
time: 168 us
  waiting for transfers between devices  115 us (68%)
  matrix products  37.8 us (22%)
  between operations  13.4 us (8%)
    all_gather x1, waiting for transfers between devices, per_device(): lax.all_gather(sessions, 'heads', axis=0, tiled=True)  59.9 us
    reduce_scatter x1, waiting for transfers between devices, per_device(): lax.psum_scatter(jnp.dot(mixed, output_weight, preferred_element_type=jnp...  54.5 us
    dot_general x1, matrix products, per_device(): jnp.einsum('nd,cde->cne', lax.all_gather(sessions, 'heads', axis=0, tiled...  18.2 us
    dot_general x1, matrix products, per_device(): jnp.dot(mixed, output_weight, preferred_element_type=jnp.float32)  9.48 us
    sub x1, matrix products, one_block(): raised = jnp.where(mask_block[None], jnp.exp(scores - highest), 0.0)  5.92 us
    dot_general x1, matrix products, one_block(): jnp.einsum('hqk,khe->qhe', attn_probs, values, preferred_element_type=jnp...  4.11 us
  transfers between devices with their start and end apart: 2, of which 2 were waited for; matrix products, arithmetic and copies ran while one was open for 1% of the time, Pallas kernels for 0%

commit v1 on v0

--- a/solution.py
+++ b/solution.py
@@ -1,9 +1,15 @@
+import functools
 import jax
 import jax.numpy as jnp
+import numpy as np
 from jax import lax
+from jax.experimental import pallas as pl
+from jax.experimental.pallas import tpu as pltpu
 from jax.sharding import PartitionSpec as P
 
+
 HD = 128
+PAIR = 2 * HD
 
 
 def permitted(total, counts):
@@ -40,7 +46,7 @@
     return blocks_out.reshape(total, width)
 
 
-def per_device(sessions, input_weight, output_weight, session_counts):
+def gather_and_scatter(sessions, input_weight, output_weight, session_counts):
     packed = jnp.einsum(
         "nd,cde->cne",
         lax.all_gather(sessions, "heads", axis=0, tiled=True),
@@ -58,9 +64,391 @@
     )
 
 
+def chip_ring(mesh):
+    column = mesh.devices.reshape(mesh.shape["users"], -1)[:, 0]
+    by_chip = {}
+    for user, device in enumerate(column):
+        key = getattr(device, "coords", None)
+        key = (user // 2,) if key is None else tuple(key)
+        by_chip.setdefault(key, []).append(user)
+    if any(len(users) != 2 for users in by_chip.values()):
+        by_chip = {(i,): [2 * i, 2 * i + 1] for i in range(len(column) // 2)}
+    keys = list(by_chip)
+
+    def near(a, b):
+        return sum(abs(i - j) for i, j in zip(a, b)) == 1
+
+    budget = [20000]
+
+    def extend(path, left):
+        budget[0] -= 1
+        if budget[0] < 0:
+            return None
+        if not left:
+            return path if near(path[-1], path[0]) else None
+        for key in sorted(k for k in left if near(k, path[-1])):
+            found = extend(path + [key], left - {key})
+            if found:
+                return found
+        return None
+
+    order = extend([keys[0]], frozenset(keys[1:])) or keys
+    return [tuple(by_chip[key]) for key in order]
+
+
+def dot32(a, b):
+    return jnp.dot(a, b, preferred_element_type=jnp.float32)
+
+
+def scores_of(q, k):
+    return lax.dot_general(q, k, (((1,), (1,)), ((), ())), preferred_element_type=jnp.float32)
+
+
+def mask_of(counts_ref, query_base, key_base, rows):
+    i = query_base + lax.broadcasted_iota(jnp.int32, (rows, 1), 0)
+    first = jnp.zeros((rows, 1), jnp.int32)
+    end = jnp.int32(0)
+    for u in range(counts_ref.shape[0]):
+        end = end + counts_ref[u]
+        first = jnp.where(i >= end, end, first)
+    j = key_base + lax.broadcasted_iota(jnp.int32, (rows, rows), 1)
+    return jnp.logical_and(j <= i, j >= first)
+
+
+def head_out(q, k_a, v_a, mask_a, k_b, v_b, mask_b):
+    scale = HD ** (-0.5)
+    s_a = jnp.where(mask_a, scores_of(q, k_a) * scale, -1e30)
+    s_b = jnp.where(mask_b, scores_of(q, k_b) * scale, -1e30)
+    top = jnp.maximum(jnp.max(s_a, axis=1, keepdims=True), jnp.max(s_b, axis=1, keepdims=True))
+    p_a = jnp.exp(s_a - top)
+    p_b = jnp.exp(s_b - top)
+    total = jnp.sum(p_a, axis=1, keepdims=True) + jnp.sum(p_b, axis=1, keepdims=True)
+    out = dot32(p_a.astype(jnp.bfloat16), v_a) + dot32(p_b.astype(jnp.bfloat16), v_b)
+    return (out / total).astype(jnp.bfloat16)
+
+
+def streamed(x, weight, kinds, offset, total, out_type):
+    rows, depth = x.shape
+    width = weight.shape[2]
+    wide = min(2 * PAIR, width)
+    across = width // wide
+    n = len(kinds) * across
+    first = kinds[0]
+
+    def body(x_ref, w_hbm, *refs):
+        o_ref, buf, sem = refs[-3:]
+
+        def load(s):
+            src = w_hbm.at[first + s // across, pl.ds(offset, depth), pl.ds(s % across * wide, wide)]
+            return pltpu.make_async_copy(src, buf.at[s], sem.at[s])
+
+        for s in range(n):
+            load(s).start()
+
+        @pl.loop(0, n)
+        def _(s):
+            pltpu.make_async_copy(
+                w_hbm.at[0, pl.ds(0, depth), pl.ds(0, wide)], buf.at[s], sem.at[s]
+            ).wait()
+            at = pl.ds(pl.multiple_of(lax.rem(s, across) * wide, wide), wide)
+            part = dot32(x_ref[...], buf[s])
+            if total is not None:
+                part = refs[0][s // across, :, at] + part
+            o_ref[s // across, :, at] = part.astype(out_type)
+
+    operands = (x, weight) if total is None else (x, weight, total)
+    vmem = pl.BlockSpec(memory_space=pltpu.VMEM)
+    return pl.pallas_call(
+        body,
+        in_specs=[vmem, pl.BlockSpec(memory_space=pl.ANY)] + [vmem] * (total is not None),
+        out_specs=vmem,
+        out_shape=jax.ShapeDtypeStruct((len(kinds), rows, width), out_type),
+        scratch_shapes=[
+            pltpu.VMEM((n, depth, wide), jnp.bfloat16),
+            pltpu.SemaphoreType.DMA((n,)),
+        ],
+        cost_estimate=pl.CostEstimate(
+            flops=2 * rows * depth * len(kinds) * width,
+            bytes_accessed=2 * (rows * depth + len(kinds) * depth * width),
+            transcendentals=0,
+        ),
+    )(*operands)
+
+
+def finish_guests(place, counts, x, weight, offset, total, own, first_pair, pairs):
+    rows, depth = x.shape
+    kinds, _, _ = weight.shape
+    step = offset // depth
+
+    def body(place_ref, counts_ref, x_ref, w_ref, t_ref, own_ref, mixed_ref, kv_ref):
+        mine = place_ref[0] * rows
+        other = (1 - place_ref[0]) * rows
+        mask_a = mask_of(counts_ref, other, mine, rows)
+        mask_b = mask_of(counts_ref, other, other, rows)
+        q, k, v = [
+            (t_ref[c] + dot32(x_ref[...], w_ref[c])).astype(jnp.bfloat16) for c in range(3)
+        ]
+        kv_ref[0] = k
+        kv_ref[1] = v
+        for h in range(2):
+            at = slice(h * HD, (h + 1) * HD)
+            mixed_ref[:, at] = head_out(
+                q[:, at], own_ref[0, :, at], own_ref[1, :, at], mask_a, k[:, at], v[:, at], mask_b
+            )
+
+    n = pairs
+    return pl.pallas_call(
+        body,
+        grid_spec=pltpu.PrefetchScalarGridSpec(
+            num_scalar_prefetch=2,
+            grid=(n,),
+            in_specs=[
+                pl.BlockSpec((rows, depth), lambda p, *_: (0, 0)),
+                pl.BlockSpec((kinds, depth, PAIR), lambda p, *_: (0, step, first_pair + p)),
+                pl.BlockSpec((kinds, rows, PAIR), lambda p, *_: (0, 0, first_pair + p)),
+                pl.BlockSpec((2, rows, PAIR), lambda p, *_: (0, 0, first_pair + p)),
+            ],
+            out_specs=[
+                pl.BlockSpec((rows, PAIR), lambda p, *_: (0, p)),
+                pl.BlockSpec((2, rows, PAIR), lambda p, *_: (0, 0, p)),
+            ],
+        ),
+        out_shape=[
+            jax.ShapeDtypeStruct((rows, n * PAIR), jnp.bfloat16),
+            jax.ShapeDtypeStruct((2, rows, n * PAIR), jnp.bfloat16),
+        ],
+        cost_estimate=pl.CostEstimate(
+            flops=2 * rows * depth * kinds * n * PAIR + 8 * rows * rows * n * PAIR,
+            bytes_accessed=2 * kinds * depth * n * PAIR + 12 * kinds * rows * n * PAIR,
+            transcendentals=4 * rows * rows * n,
+        ),
+    )(place, counts, x, weight, total, own)
+
+
+def attend_own(place, counts, own_q, own_kv, kv, first_pair, pairs):
+    rows = own_q.shape[1]
+
+    def body(place_ref, counts_ref, q_ref, own_ref, kv_ref, mixed_ref):
+        mine = place_ref[0] * rows
+        other = (1 - place_ref[0]) * rows
+        mask_a = mask_of(counts_ref, mine, mine, rows)
+        mask_b = mask_of(counts_ref, mine, other, rows)
+        for h in range(2):
+            at = slice(h * HD, (h + 1) * HD)
+            mixed_ref[:, at] = head_out(
+                q_ref[0, :, at], own_ref[0, :, at], own_ref[1, :, at], mask_a,
+                kv_ref[0, :, at], kv_ref[1, :, at], mask_b,
+            )
+
+    return pl.pallas_call(
+        body,
+        grid_spec=pltpu.PrefetchScalarGridSpec(
+            num_scalar_prefetch=2,
+            grid=(pairs,),
+            in_specs=[
+                pl.BlockSpec((1, rows, PAIR), lambda p, *_: (0, 0, first_pair + p)),
+                pl.BlockSpec((2, rows, PAIR), lambda p, *_: (0, 0, first_pair + p)),
+                pl.BlockSpec((2, rows, PAIR), lambda p, *_: (0, 0, p)),
+            ],
+            out_specs=pl.BlockSpec((rows, PAIR), lambda p, *_: (0, p)),
+        ),
+        out_shape=jax.ShapeDtypeStruct((rows, pairs * PAIR), jnp.bfloat16),
+        cost_estimate=pl.CostEstimate(
+            flops=8 * rows * rows * pairs * PAIR,
+            bytes_accessed=12 * rows * pairs * PAIR,
+            transcendentals=4 * rows * rows * pairs,
+        ),
+    )(place, counts, own_q, own_kv, kv)
+
+
+def out_own(mixed_list, weight):
+    rows = mixed_list[0].shape[0]
+    depth, width = weight.shape
+    wide = 4 * PAIR
+
+    def body(*refs):
+        w_ref, o_ref = refs[-2:]
+        at, part = 0, None
+        for ref in refs[:-2]:
+            d = ref.shape[1]
+            term = dot32(ref[...], w_ref[at:at + d, :])
+            part = term if part is None else part + term
+            at += d
+        o_ref[...] = part
+
+    return pl.pallas_call(
+        body,
+        grid=(width // wide,),
+        in_specs=[pl.BlockSpec(m.shape, lambda n: (0, 0)) for m in mixed_list]
+        + [pl.BlockSpec((depth, wide), lambda n: (0, n))],
+        out_specs=pl.BlockSpec((rows, wide), lambda n: (0, n)),
+        out_shape=jax.ShapeDtypeStruct((rows, width), jnp.float32),
+        cost_estimate=pl.CostEstimate(
+            flops=2 * rows * depth * width,
+            bytes_accessed=2 * depth * width + 4 * rows * width,
+            transcendentals=0,
+        ),
+    )(*mixed_list, weight)
+
+
+def out_other(slots, mixed, row_offset, pieces, total, last):
+    rows, depth = mixed.shape
+    width = total.shape[1]
+    wide = pieces[0].shape[-1]
+    flat = []
+    for i, array in enumerate(pieces):
+        flat += [(i, s) for s in range(array.shape[0])]
+    n = len(flat)
+    out_type = jnp.bfloat16 if last else jnp.float32
+
+    def body(slots_ref, mixed_ref, total_hbm, *refs):
+        piece_refs, out_hbm = refs[:len(pieces)], refs[len(pieces)]
+        w_buf, t_buf, o_buf, w_sem, t_sem, o_sem = refs[len(pieces) + 1:]
+
+        def column(s):
+            return pl.ds(pl.multiple_of(slots_ref[s] * wide, wide), wide)
+
+        def loads(s):
+            i, at = flat[s]
+            src = piece_refs[i].at[at, pl.ds(row_offset, depth), :]
+            return (
+                pltpu.make_async_copy(src, w_buf.at[s], w_sem.at[s]),
+                pltpu.make_async_copy(total_hbm.at[:, column(s)], t_buf.at[s], t_sem.at[s]),
+            )
+
+        def store(s):
+            return pltpu.make_async_copy(o_buf.at[s], out_hbm.at[:, column(s)], o_sem.at[s])
+
+        for s in range(n):
+            for copy in loads(s):
+                copy.start()
+        for s in range(n):
+            for copy in loads(s):
+                copy.wait()
+            o_buf[s] = (t_buf[s] + dot32(mixed_ref[...], w_buf[s])).astype(out_type)
+            store(s).start()
+        for s in range(n):
+            store(s).wait()
+
+    return pl.pallas_call(
+        body,
+        grid_spec=pltpu.PrefetchScalarGridSpec(
+            num_scalar_prefetch=1,
+            grid=(1,),
+            in_specs=[
+                pl.BlockSpec(mixed.shape, lambda i, *_: (0, 0)),
+                pl.BlockSpec(memory_space=pl.ANY),
+            ]
+            + [pl.BlockSpec(memory_space=pl.ANY)] * len(pieces),
+            out_specs=pl.BlockSpec(memory_space=pl.ANY),
+            scratch_shapes=[
+                pltpu.VMEM((n, depth, wide), jnp.bfloat16),
+                pltpu.VMEM((n, rows, wide), jnp.float32),
+                pltpu.VMEM((n, rows, wide), out_type),
+                pltpu.SemaphoreType.DMA((n,)),
+                pltpu.SemaphoreType.DMA((n,)),
+                pltpu.SemaphoreType.DMA((n,)),
+            ],
+        ),
+        out_shape=jax.ShapeDtypeStruct((rows, width), out_type),
+        cost_estimate=pl.CostEstimate(
+            flops=2 * rows * depth * width,
+            bytes_accessed=2 * depth * width + 6 * rows * width,
+            transcendentals=0,
+        ),
+    )(slots, mixed, total, *pieces)
+
+
+def two_halves(ring, sessions, input_weight, output_weight, session_counts):
+    users = 2 * len(ring)
+    chips = len(ring)
+    _, model = sessions.shape
+    width = input_weight.shape[2]
+    pairs = width // PAIR
+    place = lax.axis_index("heads").astype(jnp.int32)[None]
+    user = lax.axis_index("users")
+
+    across = [(0, 1), (1, 0)]
+    beside = [(a, b) for pair in ring for a, b in (pair, pair[::-1])]
+    around = []
+    for i in range(chips):
+        around.append((ring[i][0], ring[(i + 1) % chips][0]))
+        around.append((ring[i][1], ring[(i - 1) % chips][1]))
+
+    full = (chips - 1) // 2
+    half = chips % 2 == 0
+    table = np.zeros((users, users), np.int32)
+    for i in range(chips):
+        for core in range(2):
+            held = [(i, core), (i, 1 - core)]
+            for k in range(1, full + 1):
+                for c in (core, 1 - core):
+                    source = (i - k) % chips if c == 0 else (i + k) % chips
+                    held += [(source, c), (source, 1 - c)]
+            if half:
+                far = (i + chips // 2) % chips
+                held += [(far, core), (far, 1 - core)]
+            table[ring[i][core]] = [2 * a + b for a, b in held]
+    slots = jnp.asarray(table)[user]
+    piece_width = model // users
+    start = slots[0] * piece_width
+    piece = lax.dynamic_slice_in_dim(output_weight, start, piece_width, 1)
+
+    crossed = lax.ppermute(piece, "heads", across)
+    sizes = [model // 2, model // 4, model // 8, model // 8]
+    offsets = np.cumsum([0] + sizes)[:-1].tolist()
+    guests = [lax.ppermute(sessions[:, o:o + s], "heads", across) for o, s in zip(offsets, sizes)]
+
+    partner = lax.ppermute(crossed, "users", beside)
+    stack = jnp.stack([crossed, partner])
+    pieces = [stack]
+    moving = stack
+    for _ in range(full):
+        moving = lax.ppermute(moving, "users", around)
+        pieces += [moving, lax.ppermute(moving, "users", beside)]
+    if half:
+        far = lax.ppermute(moving[:1], "users", around)
+        pieces += [far, lax.ppermute(far, "users", beside)]
+
+    own_q = streamed(sessions, input_weight, (0,), 0, None, jnp.bfloat16)
+    own_kv = streamed(sessions, input_weight, (1, 2), 0, None, jnp.bfloat16)
+    total = None
+    for i in range(len(sizes) - 1):
+        total = streamed(
+            guests[i], input_weight, (0, 1, 2), offsets[i], total,
+            jnp.float32,
+        )
+    groups = [(0, pairs // 2), (pairs // 2, pairs - pairs // 2)]
+    groups = [g for g in groups if g[1]]
+    mixed_far, mixed_own = [], []
+    for first, n in groups:
+        mixed, kv = finish_guests(
+            place, session_counts, guests[-1], input_weight,
+            offsets[-1], total, own_kv, first, n,
+        )
+        mixed_far.append(lax.ppermute(mixed, "heads", across))
+        mixed_own.append(attend_own(place, session_counts, own_q, own_kv, kv, first, n))
+    out = out_own(mixed_own, output_weight)
+    for i, (first, n) in enumerate(groups):
+        out = out_other(
+            slots, mixed_far[i], first * PAIR, pieces, out,
+            i == len(groups) - 1,
+        )
+    return out
+
+
 def solution(mesh):
     in_specs = (P(("users", "heads"), None), P(None, None, "heads"), P("heads", None), P("users"))
     out_specs = P(("users", "heads"), None)
+    if mesh.shape["heads"] == 2 and mesh.shape["users"] % 2 == 0 and mesh.shape["users"] > 2:
+        per_device = functools.partial(two_halves, chip_ring(mesh))
+
+        def layer(*args):
+            return per_device(*args)
+
+        return jax.shard_map(
+            layer, mesh=mesh, in_specs=in_specs, out_specs=out_specs, check_vma=False
+        )
     return jax.shard_map(
-        per_device, mesh=mesh, in_specs=in_specs, out_specs=out_specs, check_vma=False
+        gather_and_scatter, mesh=mesh, in_specs=in_specs, out_specs=out_specs, check_vma=False
     )

time: 168 us -> 178 us (1.060)
  Pallas kernels: 0 us -> 82.1 us
  waiting for transfers between devices: 115 us -> 68.2 us
  matrix products: 37.8 us -> 0 us
  starting transfers between devices: 0.04 us -> 16.7 us
  between operations: 13.4 us -> 0.24 us
  local copies, waits for them, and re-layouts: 0.2 us -> 10.1 us
    pallas_call x0 -> x12, Pallas kernels: none -> 82.1 us  [the longest x5 39.9 us: streamed(): pl.pallas_call(body, in_specs=[vmem, pl.BlockSpec(memory_space=pl.ANY)] +...]
    ppermute x0 -> x16, waiting for transfers between devices: none -> 68.2 us  [the longest x4 28.3 us: two_halves(): lax.ppermute(sessions[:, o:o + s], 'heads', across)]
    all_gather x1 -> x0, waiting for transfers between devices: 59.9 us -> none  [per_device(): lax.all_gather(sessions, 'heads', axis=0, tiled=True)]
    reduce_scatter x1 -> x0, waiting for transfers between devices: 54.5 us -> none  [per_device(): lax.psum_scatter(jnp.dot(mixed, output_weight, preferred_element_type=jnp...]
    dot_general x3 -> x0, matrix products: 31.8 us -> none  [the longest x1 18.2 us: per_device(): jnp.einsum('nd,cde->cne', lax.all_gather(sessions, 'heads', axis=0, tiled...]
    ppermute x0 -> x16, starting transfers between devices: none -> 16.7 us  [the longest x3 5.53 us: two_halves(): moving = lax.ppermute(moving, 'users', around)]
    sub x1 -> x0, matrix products: 5.92 us -> none  [one_block(): raised = jnp.where(mask_block[None], jnp.exp(scores - highest), 0.0)]
    slice x1 -> x4, local copies, waits for them, and re-layouts: 0.2 us -> 4.65 us  [the longest x3 2.77 us: two_halves(): sessions[:, o:o + s]]
  transfers between devices with their start and end apart: 2 -> 16, of which waited for: 2 -> 5; matrix products, arithmetic and copies ran while one was open for 1% -> 3% of each run, Pallas kernels for 0% -> 42%
where the time goes in v1:
time: 178 us; the launch traced here: 177 us
  Pallas kernels  82.1 us (46%)
  waiting for transfers between devices  68.2 us (38%)
  starting transfers between devices  16.7 us (9%)
  local copies, waits for them, and re-layouts  10.1 us (6%)
    pallas_call x5, Pallas kernels, streamed(): pl.pallas_call(body, in_specs=[vmem, pl.BlockSpec(memory_space=pl.ANY)] +...  39.9 us
    ppermute x4, waiting for transfers between devices, two_halves(): lax.ppermute(sessions[:, o:o + s], 'heads', across)  28.3 us
    ppermute x3, waiting for transfers between devices, two_halves(): moving = lax.ppermute(moving, 'users', around)  26.1 us
    pallas_call x2, Pallas kernels, out_other(): pl.pallas_call(body, grid_spec=pltpu.PrefetchScalarGridSpec(num_scalar_pr...  16.8 us
    ppermute x1, waiting for transfers between devices, two_halves(): crossed = lax.ppermute(piece, 'heads', across)  11.9 us
    pallas_call x2, Pallas kernels, finish_guests(): pl.pallas_call(body, grid_spec=pltpu.PrefetchScalarGridSpec(num_scalar_pr...  10.1 us
    pallas_call x2, Pallas kernels, attend_own(): pl.pallas_call(body, grid_spec=pltpu.PrefetchScalarGridSpec(num_scalar_pr...  8.18 us
    pallas_call x1, Pallas kernels, out_own(): pl.pallas_call(body, grid=(width // wide,), in_specs=[pl.BlockSpec(m.shap...  7.16 us
  transfers between devices with their start and end apart: 16, of which 5 were waited for; matrix products, arithmetic and copies ran while one was open for 3% of the time, Pallas kernels for 42%

profile of v1, /device:TPU:0, one launch (start us, length us, event | category | flops | bytes accessed | tf_op | source)
XLA Modules:
  0.0 177.4 jit_solution(4489439603618564308)
XLA Ops:
  0.0 1.3 constant_dynamic-slice_fusion.1
  1.4 1.1 constant_dynamic-slice_fusion
  2.4 3.0 %collective-permute-start.6 = (bf16[1024,256]{1,0:T(8,128)(2,1)S(1)}, bf16[1024,256]{1,0:T(8,128)(2,1)S(1)}, u32[]{:S(2)}, u32[]{:S(2)}) collective-permute-start(bf16[1024,256]{1,0:T(8,128)(2,1)S(1)} %constant_dynamic-slice_fusion), channel_id=1, source_target_pairs={{0,1},{1,0},{2,3},{3,2},{4,5},{5,4},{6,7},{7,6},{8,9},{9,8},{10,11... | collective-permute-start | bytes 1572872 | tf_op jit(solution)/shard_map/ppermute | solution.py:397
  5.5 11.9 %collective-permute-done.6 = bf16[1024,256]{1,0:T(8,128)(2,1)S(1)} collective-permute-done((bf16[1024,256]{1,0:T(8,128)(2,1)S(1)}, bf16[1024,256]{1,0:T(8,128)(2,1)S(1)}, u32[]{:S(2)}, u32[]{:S(2)}) %collective-permute-start.6) | collective-permute-done | bytes 524320 | tf_op jit(solution)/shard_map/ppermute | solution.py:397
  17.4 1.9 %collective-permute-done.7 = bf16[1024,256]{1,0:T(8,128)(2,1)S(1)} collective-permute-done((bf16[1024,256]{1,0:T(8,128)(2,1)S(1)}, bf16[1024,256]{1,0:T(8,128)(2,1)S(1)}, u32[]{:S(2)}, u32[]{:S(2)}) %collective-permute-start.7) | collective-permute-done | bytes 524320 | tf_op jit(solution)/shard_map/ppermute | solution.py:402
  19.4 1.9 %collective-permute-start.8 = (bf16[2,1024,256]{2,1,0:T(8,128)(2,1)S(1)}, bf16[2,1024,256]{2,1,0:T(8,128)(2,1)S(1)}, u32[]{:S(2)}, u32[]{:S(2)}) collective-permute-start(bf16[2,1024,256]{2,1,0:T(8,128)(2,1)S(1)} %pad_maximum_fusion.refs_0_), channel_id=1, source_target_pairs={{0,8},{2,6},{8,16},{10,2},{16,24},{18,10},{24,28},{26,18},{28,20},... | collective-permute-start | bytes 3145736 | tf_op jit(solution)/shard_map/ppermute | solution.py:407
  21.3 13.0 %collective-permute-done.8.refs_1_ = bf16[2,1024,256]{2,1,0:T(8,128)(2,1)S(1)} collective-permute-done((bf16[2,1024,256]{2,1,0:T(8,128)(2,1)S(1)}, bf16[2,1024,256]{2,1,0:T(8,128)(2,1)S(1)}, u32[]{:S(2)}, u32[]{:S(2)}) %collective-permute-start.8) | collective-permute-done | bytes 1048608 | tf_op jit(solution)/shard_map/ppermute | solution.py:407
  34.3 1.0 copy-done.2
  35.3 1.8 %collective-permute-start.10 = (bf16[2,1024,256]{2,1,0:T(8,128)(2,1)S(1)}, bf16[2,1024,256]{2,1,0:T(8,128)(2,1)}, u32[]{:S(2)}, u32[]{:S(2)}) collective-permute-start(bf16[2,1024,256]{2,1,0:T(8,128)(2,1)S(1)} %collective-permute-done.8.refs_1_), channel_id=1, source_target_pairs={{0,8},{2,6},{8,16},{10,2},{16,24},{18,10},{24,28},{26,18},{28,20},... | collective-permute-start | bytes 3145736 | tf_op jit(solution)/shard_map/ppermute | solution.py:407
  37.1 13.1 %collective-permute-done.10.refs_3_ = bf16[2,1024,256]{2,1,0:T(8,128)(2,1)} collective-permute-done((bf16[2,1024,256]{2,1,0:T(8,128)(2,1)S(1)}, bf16[2,1024,256]{2,1,0:T(8,128)(2,1)}, u32[]{:S(2)}, u32[]{:S(2)}) %collective-permute-start.10) | collective-permute-done | bytes 1048608 | tf_op jit(solution)/shard_map/ppermute | solution.py:407
  50.2 1.8 %collective-permute-start.12 = (bf16[2,1024,256]{2,1,0:T(8,128)(2,1)}, bf16[2,1024,256]{2,1,0:T(8,128)(2,1)}, u32[]{:S(2)}, u32[]{:S(2)}) collective-permute-start(bf16[2,1024,256]{2,1,0:T(8,128)(2,1)} %collective-permute-done.10.refs_3_), channel_id=1, source_target_pairs={{0,8},{2,6},{8,16},{10,2},{16,24},{18,10},{24,28},{26,18},{28,20},... | collective-permute-start | bytes 3145736 | tf_op jit(solution)/shard_map/ppermute | solution.py:407
  52.0 1.0 slice.22
  53.0 1.5 collective-permute-start.3
  54.5 0.9 slice.21
  56.8 1.5 collective-permute-start
  58.8 9.9 %shard_map.58.own_ref = bf16[2,256,1024]{2,1,0:T(8,128)(2,1)} custom-call(bf16[256,4096]{1,0:T(8,128)(2,1)} %x_ref.3, bf16[3,4096,1024]{2,1,0:T(8,128)(2,1)} %w_hbm.9), custom_call_target="tpu_custom_call" | custom-call | flops 4294967296 | bytes 18874368 | tf_op jit(solution)/shard_map/pallas_call | solution.py:161
  68.8 1.9 %slice.25 = bf16[1,1024,256]{2,1,0:T(8,128)(2,1)} slice(bf16[2,1024,256]{2,1,0:T(8,128)(2,1)} %collective-permute-done.12.refs_5_), slice={[0:1], [0:1024], [0:256]} | slice | bytes 1048576 | tf_op jit(solution)/shard_map/slice | solution.py:410
  70.7 28.3 %collective-permute-done.1.x_ref = bf16[256,512]{1,0:T(8,128)(2,1)} collective-permute-done((bf16[256,512]{1,0:T(8,128)(2,1)}, bf16[256,512]{1,0:T(8,128)(2,1)}, u32[]{:S(2)}, u32[]{:S(2)}) %collective-permute-start.1) | collective-permute-done | bytes 262176 | tf_op jit(solution)/shard_map/ppermute | solution.py:400
  99.3 1.5 collective-permute-start.13
  100.8 8.7 %shard_map.55.refs_0_ = f32[3,256,1024]{2,1,0:T(8,128)} custom-call(bf16[256,2048]{1,0:T(8,128)(2,1)} %collective-permute-done.3.x_ref, bf16[3,4096,1024]{2,1,0:T(8,128)(2,1)} %w_hbm.9), custom_call_target="tpu_custom_call" | custom-call | flops 3221225472 | bytes 13631488 | tf_op jit(solution)/shard_map/pallas_call | solution.py:161
  109.6 7.6 %shard_map.56.refs_0_ = f32[3,256,1024]{2,1,0:T(8,128)} custom-call(bf16[256,1024]{1,0:T(8,128)(2,1)} %collective-permute-done.2.x_ref, bf16[3,4096,1024]{2,1,0:T(8,128)(2,1)} %w_hbm.9, f32[3,256,1024]{2,1,0:T(8,128)} %shard_map.55.refs_0_), custom_call_target="tpu_custom_call" | custom-call | flops 1610612736 | bytes 6815744 | tf_op jit(solution)/shard_map/pallas_call | solution.py:161
  117.2 6.5 %shard_map.57.t_ref = f32[3,256,1024]{2,1,0:T(8,128)} custom-call(bf16[256,512]{1,0:T(8,128)(2,1)} %collective-permute-done.1.x_ref, bf16[3,4096,1024]{2,1,0:T(8,128)(2,1)} %w_hbm.9, f32[3,256,1024]{2,1,0:T(8,128)} %shard_map.56.refs_0_), custom_call_target="tpu_custom_call" | custom-call | flops 805306368 | bytes 3407872 | tf_op jit(solution)/shard_map/pallas_call | solution.py:161
  124.6 5.1 %shard_map.60 = (bf16[256,512]{1,0:T(8,128)(2,1)}, bf16[2,256,512]{2,1,0:T(8,128)(2,1)}) custom-call(s32[1]{0:T(128)} %bitcast.1.place_ref, s32[2]{0:T(128)} %counts_ref.7, bf16[256,512]{1,0:T(8,128)(2,1)} %copy-done.6, bf16[3,4096,1024]{2,1,0:T(8,128)(2,1)} %w_hbm.9, f32[3,256,1024]{2,1,0:T(8,128)} %shard_map.57.t_ref, bf16[2,256,1024]{2,1,0:T(8,128)(2,1)} %shard_map.58.own_ref), custom_call_target="tpu_custom_call" | custom-call | flops 671088640 | bytes 6291456 | tf_op jit(solution)/shard_map/pallas_call | solution.py:200
  129.6 1.5 collective-permute-start.5
  131.1 7.1 %shard_map.61.q_ref = bf16[1,256,1024]{2,1,0:T(8,128)(2,1)} custom-call(bf16[256,4096]{1,0:T(8,128)(2,1)} %x_ref.3, bf16[3,4096,1024]{2,1,0:T(8,128)(2,1)} %w_hbm.9), custom_call_target="tpu_custom_call" | custom-call | flops 2147483648 | bytes 10485760 | tf_op jit(solution)/shard_map/pallas_call | solution.py:161
  138.2 4.1 %shard_map.62.refs_0_ = bf16[256,512]{1,0:T(8,128)(2,1)} custom-call(s32[1]{0:T(128)} %bitcast.1.place_ref, s32[2]{0:T(128)} %counts_ref.7, bf16[1,256,1024]{2,1,0:T(8,128)(2,1)} %shard_map.61.q_ref, bf16[2,256,1024]{2,1,0:T(8,128)(2,1)} %shard_map.58.own_ref, bf16[2,256,512]{2,1,0:T(8,128)(2,1)} %get-tuple-element.11.kv_ref), custom_call_target="tpu_custom_call" | custom-call | flops 268435456 | bytes 1572864 | tf_op jit(solution)/shard_map/pallas_call | solution.py:243
  142.3 5.1 %shard_map.59 = (bf16[256,512]{1,0:T(8,128)(2,1)}, bf16[2,256,512]{2,1,0:T(8,128)(2,1)}) custom-call(s32[1]{0:T(128)} %bitcast.1.place_ref, s32[2]{0:T(128)} %counts_ref.7, bf16[256,512]{1,0:T(8,128)(2,1)} %copy-done.6, bf16[3,4096,1024]{2,1,0:T(8,128)(2,1)} %w_hbm.9, f32[3,256,1024]{2,1,0:T(8,128)} %shard_map.57.t_ref, bf16[2,256,1024]{2,1,0:T(8,128)(2,1)} %shard_map.58.own_ref), custom_call_target="tpu_custom_call" | custom-call | flops 671088640 | bytes 6291456 | tf_op jit(solution)/shard_map/pallas_call | solution.py:200
  147.4 4.1 %shard_map.63.refs_1_ = bf16[256,512]{1,0:T(8,128)(2,1)} custom-call(s32[1]{0:T(128)} %bitcast.1.place_ref, s32[2]{0:T(128)} %counts_ref.7, bf16[1,256,1024]{2,1,0:T(8,128)(2,1)} %shard_map.61.q_ref, bf16[2,256,1024]{2,1,0:T(8,128)(2,1)} %shard_map.58.own_ref, bf16[2,256,512]{2,1,0:T(8,128)(2,1)} %get-tuple-element.12.kv_ref), custom_call_target="tpu_custom_call" | custom-call | flops 268435456 | bytes 1572864 | tf_op jit(solution)/shard_map/pallas_call | solution.py:243
  152.1 7.2 %shard_map.64.total_hbm = f32[256,4096]{1,0:T(8,128)} custom-call(bf16[256,512]{1,0:T(8,128)(2,1)} %shard_map.62.refs_0_, bf16[256,512]{1,0:T(8,128)(2,1)} %shard_map.63.refs_1_, bf16[1024,4096]{1,0:T(8,128)(2,1)} %refs_2_.1), custom_call_target="tpu_custom_call" | custom-call | flops 2147483648 | bytes 12582912 | tf_op jit(solution)/shard_map/pallas_call | solution.py:279
  159.3 0.9 copy-done.4
  160.6 8.4 %shard_map.65.total_hbm = f32[256,4096]{1,0:T(8,128)} custom-call(s32[16]{0:T(128)} %get-tuple-element.16.slots_ref, bf16[256,512]{1,0:T(8,128)(2,1)} %copy-done.7, f32[256,4096]{1,0:T(8,128)} %shard_map.64.total_hbm, bf16[2,1024,256]{2,1,0:T(8,128)(2,1)} %copy-done.1, bf16[2,1024,256]{2,1,0:T(8,128)(2,1)} %copy-done.2, bf16[2,1024,256]{2,1,0:T(8,128)(2,1)} %copy-done.4, ...), custom_call_target="tpu_custom_call" | custom-call | flops 1073741824 | bytes 10485760 | tf_op jit(solution)/shard_map/pallas_call | solution.py:333
  169.0 8.3 %shard_map.66 = bf16[256,4096]{1,0:T(8,128)(2,1)} custom-call(s32[16]{0:T(128)} %get-tuple-element.16.slots_ref, bf16[256,512]{1,0:T(8,128)(2,1)} %collective-permute-done.4.mixed_ref, f32[256,4096]{1,0:T(8,128)} %shard_map.65.total_hbm, bf16[2,1024,256]{2,1,0:T(8,128)(2,1)} %copy-done.1, bf16[2,1024,256]{2,1,0:T(8,128)(2,1)} %copy-done.2, ...), custom_call_target="tpu_custom_call" | custom-call | flops 1073741824 | bytes 10485760 | tf_op jit(solution)/shard_map/pallas_call | solution.py:333
  (35 shorter events, 4.2 us)
Async XLA Ops:
  0.0 52.0 %copy-start = (bf16[256,4096]{1,0:T(8,128)(2,1)S(1)}, bf16[256,4096]{1,0:T(8,128)(2,1)}, u32[]{:S(2)}) copy-start(bf16[256,4096]{1,0:T(8,128)(2,1)} %x_ref.3) | copy-start | bytes 6291460
  2.4 15.0 %collective-permute-start.6 = (bf16[1024,256]{1,0:T(8,128)(2,1)S(1)}, bf16[1024,256]{1,0:T(8,128)(2,1)S(1)}, u32[]{:S(2)}, u32[]{:S(2)}) collective-permute-start(bf16[1024,256]{1,0:T(8,128)(2,1)S(1)} %constant_dynamic-slice_fusion), channel_id=1, source_target_pairs={{0,1},{1,0},{2,3},{3,2},{4,5},{5,4},{6,7},{7,6},{8,9},{9,8},{10,11... | collective-permute-start | bytes 1572872 | tf_op jit(solution)/shard_map/ppermute | solution.py:397
  17.4 1.9 %collective-permute-start.7 = (bf16[1024,256]{1,0:T(8,128)(2,1)S(1)}, bf16[1024,256]{1,0:T(8,128)(2,1)S(1)}, u32[]{:S(2)}, u32[]{:S(2)}) collective-permute-start(bf16[1024,256]{1,0:T(8,128)(2,1)S(1)} %collective-permute-done.6), channel_id=1, source_target_pairs={{0,2},{2,0},{8,10},{10,8},{16,18},{18,16},{24,26},{26,24},{28,30},... | collective-permute-start | bytes 1572872 | tf_op jit(solution)/shard_map/ppermute | solution.py:402
  19.4 49.3 %copy-start.1 = (bf16[2,1024,256]{2,1,0:T(8,128)(2,1)}, bf16[2,1024,256]{2,1,0:T(8,128)(2,1)S(1)}, u32[]{:S(2)}) copy-start(bf16[2,1024,256]{2,1,0:T(8,128)(2,1)S(1)} %pad_maximum_fusion.refs_0_) | copy-start | bytes 3145732
  19.4 14.9 %collective-permute-start.8 = (bf16[2,1024,256]{2,1,0:T(8,128)(2,1)S(1)}, bf16[2,1024,256]{2,1,0:T(8,128)(2,1)S(1)}, u32[]{:S(2)}, u32[]{:S(2)}) collective-permute-start(bf16[2,1024,256]{2,1,0:T(8,128)(2,1)S(1)} %pad_maximum_fusion.refs_0_), channel_id=1, source_target_pairs={{0,8},{2,6},{8,16},{10,2},{16,24},{18,10},{24,28},{26,18},{28,20},... | collective-permute-start | bytes 3145736 | tf_op jit(solution)/shard_map/ppermute | solution.py:407
  34.3 1.0 copy-start.2
  35.3 14.9 %collective-permute-start.10 = (bf16[2,1024,256]{2,1,0:T(8,128)(2,1)S(1)}, bf16[2,1024,256]{2,1,0:T(8,128)(2,1)}, u32[]{:S(2)}, u32[]{:S(2)}) collective-permute-start(bf16[2,1024,256]{2,1,0:T(8,128)(2,1)S(1)} %collective-permute-done.8.refs_1_), channel_id=1, source_target_pairs={{0,8},{2,6},{8,16},{10,2},{16,24},{18,10},{24,28},{26,18},{28,20},... | collective-permute-start | bytes 3145736 | tf_op jit(solution)/shard_map/ppermute | solution.py:407
  50.2 18.6 %collective-permute-start.12 = (bf16[2,1024,256]{2,1,0:T(8,128)(2,1)}, bf16[2,1024,256]{2,1,0:T(8,128)(2,1)}, u32[]{:S(2)}, u32[]{:S(2)}) collective-permute-start(bf16[2,1024,256]{2,1,0:T(8,128)(2,1)} %collective-permute-done.10.refs_3_), channel_id=1, source_target_pairs={{0,8},{2,6},{8,16},{10,2},{16,24},{18,10},{24,28},{26,18},{28,20},... | collective-permute-start | bytes 3145736 | tf_op jit(solution)/shard_map/ppermute | solution.py:407
  53.0 46.3 %collective-permute-start.3 = (bf16[256,2048]{1,0:T(8,128)(2,1)}, bf16[256,2048]{1,0:T(8,128)(2,1)}, u32[]{:S(2)}, u32[]{:S(2)}) collective-permute-start(bf16[256,2048]{1,0:T(8,128)(2,1)} %slice.22), channel_id=1, source_target_pairs={{0,1},{1,0},{2,3},{3,2},{4,5},{5,4},{6,7},{7,6},{8,9},{9,8},{10,11... | collective-permute-start | bytes 3145736 | tf_op jit(solution)/shard_map/ppermute | solution.py:400
  55.4 43.6 %collective-permute-start.2 = (bf16[256,1024]{1,0:T(8,128)(2,1)}, bf16[256,1024]{1,0:T(8,128)(2,1)}, u32[]{:S(2)}, u32[]{:S(2)}) collective-permute-start(bf16[256,1024]{1,0:T(8,128)(2,1)} %slice.21), channel_id=1, source_target_pairs={{0,1},{1,0},{2,3},{3,2},{4,5},{5,4},{6,7},{7,6},{8,9},{9,8},{10,11... | collective-permute-start | bytes 1572872 | tf_op jit(solution)/shard_map/ppermute | solution.py:400
  56.8 67.0 %collective-permute-start = (bf16[256,512]{1,0:T(8,128)(2,1)}, bf16[256,512]{1,0:T(8,128)(2,1)S(1)}, u32[]{:S(2)}, u32[]{:S(2)}) collective-permute-start(bf16[256,512]{1,0:T(8,128)(2,1)} %get-tuple-element.14), channel_id=1, source_target_pairs={{0,1},{1,0},{2,3},{3,2},{4,5},{5,4},{6,7},{7,6},{8,9},{9,8},{10,11... | collective-permute-start | bytes 786440 | tf_op jit(solution)/shard_map/ppermute | solution.py:400
  58.3 40.7 %collective-permute-start.1 = (bf16[256,512]{1,0:T(8,128)(2,1)}, bf16[256,512]{1,0:T(8,128)(2,1)}, u32[]{:S(2)}, u32[]{:S(2)}) collective-permute-start(bf16[256,512]{1,0:T(8,128)(2,1)} %get-tuple-element.13), channel_id=1, source_target_pairs={{0,1},{1,0},{2,3},{3,2},{4,5},{5,4},{6,7},{7,6},{8,9},{9,8},{10,11... | collective-permute-start | bytes 786440 | tf_op jit(solution)/shard_map/ppermute | solution.py:400
  58.8 9.9 %copy-start.3 = (bf16[2,1024,256]{2,1,0:T(8,128)(2,1)S(1)}, bf16[2,1024,256]{2,1,0:T(8,128)(2,1)}, u32[]{:S(2)}) copy-start(bf16[2,1024,256]{2,1,0:T(8,128)(2,1)} %copy-done.2) | copy-start | bytes 3145732
  68.8 90.5 %collective-permute-start.9 = (bf16[2,1024,256]{2,1,0:T(8,128)(2,1)S(1)}, bf16[2,1024,256]{2,1,0:T(8,128)(2,1)S(1)}, u32[]{:S(2)}, u32[]{:S(2)}) collective-permute-start(bf16[2,1024,256]{2,1,0:T(8,128)(2,1)S(1)} %copy-done.3), channel_id=1, source_target_pairs={{0,2},{2,0},{8,10},{10,8},{16,18},{18,16},{24,26},{26,24},{28,30},... | collective-permute-start | bytes 3145736 | tf_op jit(solution)/shard_map/ppermute | solution.py:408
  99.0 60.3 %collective-permute-start.11 = (bf16[2,1024,256]{2,1,0:T(8,128)(2,1)}, bf16[2,1024,256]{2,1,0:T(8,128)(2,1)S(1)}, u32[]{:S(2)}, u32[]{:S(2)}) collective-permute-start(bf16[2,1024,256]{2,1,0:T(8,128)(2,1)} %collective-permute-done.10.refs_3_), channel_id=1, source_target_pairs={{0,2},{2,0},{8,10},{10,8},{16,18},{18,16},{24,26},{26,24},{28,30},... | collective-permute-start | bytes 3145736 | tf_op jit(solution)/shard_map/ppermute | solution.py:408
  99.0 24.7 %collective-permute-start.14 = (bf16[1,1024,256]{2,1,0:T(8,128)(2,1)}, bf16[1,1024,256]{2,1,0:T(8,128)(2,1)}, u32[]{:S(2)}, u32[]{:S(2)}) collective-permute-start(bf16[1,1024,256]{2,1,0:T(8,128)(2,1)} %slice.25), channel_id=1, source_target_pairs={{0,8},{2,6},{8,16},{10,2},{16,24},{18,10},{24,28},{26,18},{28,20},... | collective-permute-start | bytes 1572872 | tf_op jit(solution)/shard_map/ppermute | solution.py:410
  99.3 60.0 %collective-permute-start.13 = (bf16[2,1024,256]{2,1,0:T(8,128)(2,1)}, bf16[2,1024,256]{2,1,0:T(8,128)(2,1)}, u32[]{:S(2)}, u32[]{:S(2)}) collective-permute-start(bf16[2,1024,256]{2,1,0:T(8,128)(2,1)} %collective-permute-done.12.refs_5_), channel_id=1, source_target_pairs={{0,2},{2,0},{8,10},{10,8},{16,18},{18,16},{24,26},{26,24},{28,30},... | collective-permute-start | bytes 3145736 | tf_op jit(solution)/shard_map/ppermute | solution.py:408
  123.7 35.5 %collective-permute-start.15 = (bf16[1,1024,256]{2,1,0:T(8,128)(2,1)}, bf16[1,1024,256]{2,1,0:T(8,128)(2,1)}, u32[]{:S(2)}, u32[]{:S(2)}) collective-permute-start(bf16[1,1024,256]{2,1,0:T(8,128)(2,1)} %collective-permute-done.14.refs_7_), channel_id=1, source_target_pairs={{0,2},{2,0},{8,10},{10,8},{16,18},{18,16},{24,26},{26,24},{28,30},... | collective-permute-start | bytes 1572872 | tf_op jit(solution)/shard_map/ppermute | solution.py:411
  123.8 0.7 copy-start.6
  129.6 21.9 %collective-permute-start.5 = (bf16[256,512]{1,0:T(8,128)(2,1)}, bf16[256,512]{1,0:T(8,128)(2,1)S(1)}, u32[]{:S(2)}, u32[]{:S(2)}) collective-permute-start(bf16[256,512]{1,0:T(8,128)(2,1)} %get-tuple-element.10), channel_id=1, source_target_pairs={{0,1},{1,0},{2,3},{3,2},{4,5},{5,4},{6,7},{7,6},{8,9},{9,8},{10,11... | collective-permute-start | bytes 786440 | tf_op jit(solution)/shard_map/ppermute | solution.py:429
  151.5 7.8 %copy-start.7 = (bf16[256,512]{1,0:T(8,128)(2,1)}, bf16[256,512]{1,0:T(8,128)(2,1)S(1)}, u32[]{:S(2)}) copy-start(bf16[256,512]{1,0:T(8,128)(2,1)S(1)} %collective-permute-done.5.mixed_ref) | copy-start | bytes 786436
  151.5 17.5 %collective-permute-start.4 = (bf16[256,512]{1,0:T(8,128)(2,1)}, bf16[256,512]{1,0:T(8,128)(2,1)}, u32[]{:S(2)}, u32[]{:S(2)}) collective-permute-start(bf16[256,512]{1,0:T(8,128)(2,1)} %get-tuple-element.9), channel_id=1, source_target_pairs={{0,1},{1,0},{2,3},{3,2},{4,5},{5,4},{6,7},{7,6},{8,9},{9,8},{10,11... | collective-permute-start | bytes 786440 | tf_op jit(solution)/shard_map/ppermute | solution.py:429
  159.3 1.0 copy-start.4
  159.3 1.3 copy-start.5

commit v2 on v0

--- a/solution.py
+++ b/solution.py
@@ -1,7 +1,12 @@
+import functools
 import jax
 import jax.numpy as jnp
+import numpy as np
 from jax import lax
+from jax.experimental import pallas as pl
+from jax.experimental.pallas import tpu as pltpu
 from jax.sharding import PartitionSpec as P
+
 
 HD = 128
 
@@ -40,7 +45,7 @@
     return blocks_out.reshape(total, width)
 
 
-def per_device(sessions, input_weight, output_weight, session_counts):
+def gather_and_scatter(sessions, input_weight, output_weight, session_counts):
     packed = jnp.einsum(
         "nd,cde->cne",
         lax.all_gather(sessions, "heads", axis=0, tiled=True),
@@ -58,9 +63,408 @@
     )
 
 
+def chip_ring(mesh):
+    column = mesh.devices.reshape(mesh.shape["users"], -1)[:, 0]
+    by_chip = {}
+    for user, device in enumerate(column):
+        key = getattr(device, "coords", None)
+        key = (user // 2,) if key is None else tuple(key)
+        by_chip.setdefault(key, []).append(user)
+    if any(len(users) != 2 for users in by_chip.values()):
+        by_chip = {(i,): [2 * i, 2 * i + 1] for i in range(len(column) // 2)}
+    keys = list(by_chip)
+
+    def near(a, b):
+        return sum(abs(i - j) for i, j in zip(a, b)) == 1
+
+    budget = [20000]
+
+    def extend(path, left):
+        budget[0] -= 1
+        if budget[0] < 0:
+            return None
+        if not left:
+            return path if near(path[-1], path[0]) else None
+        for key in sorted(k for k in left if near(k, path[-1])):
+            found = extend(path + [key], left - {key})
+            if found:
+                return found
+        return None
+
+    order = extend([keys[0]], frozenset(keys[1:])) or keys
+    return [tuple(by_chip[key]) for key in order]
+
+
+def dot32(a, b):
+    return jnp.dot(a, b, preferred_element_type=jnp.float32)
+
+
+def scores_of(q, k):
+    return lax.dot_general(q, k, (((1,), (1,)), ((), ())), preferred_element_type=jnp.float32)
+
+
+LOG2E = 1.4426950408889634
+VMEM = pl.BlockSpec(memory_space=pltpu.VMEM)
+SMEM = pl.BlockSpec(memory_space=pltpu.SMEM)
+HBM = pl.BlockSpec(memory_space=pltpu.HBM)
+
+
+def call(
+    body, in_specs, out_shape, operands, flops, scratch=(), aliases=None, out_specs=None, mib=8
+):
+    spaces = {id(VMEM): pltpu.VMEM, id(HBM): pltpu.HBM}
+    operands = [
+        pltpu.with_memory_space_constraint(x, spaces[id(spec)]) if id(spec) in spaces else x
+        for spec, x in zip(in_specs, operands)
+    ]
+    return pl.pallas_call(
+        body,
+        in_specs=in_specs,
+        out_specs=out_specs if out_specs is not None else jax.tree.map(lambda _: VMEM, out_shape),
+        out_shape=out_shape,
+        scratch_shapes=list(scratch),
+        input_output_aliases=aliases or {},
+        compiler_params=pltpu.CompilerParams(vmem_limit_bytes=mib << 20),
+        cost_estimate=pl.CostEstimate(flops=flops, bytes_accessed=1 << 20, transcendentals=0),
+    )(*operands)
+
+
+def load_piece(user, place, output_weight, piece_width):
+    depth = output_weight.shape[0]
+
+    def body(user_ref, place_ref, w_hbm, o_ref, sem):
+        at = pl.ds(pl.multiple_of(user_ref[0] * piece_width, piece_width), piece_width)
+        copy = pltpu.make_async_copy(w_hbm.at[:, at], o_ref, sem)
+        copy.start()
+        copy.wait()
+
+    return call(
+        body, [SMEM, SMEM, HBM], pltpu.VMEM((depth, piece_width), jnp.bfloat16),
+        (user, place, output_weight), 0, [pltpu.SemaphoreType.DMA(())],
+    )
+
+
+def load_rows(sessions, sizes):
+    rows = sessions.shape[0]
+    offsets = np.cumsum([0] + sizes)[:-1].tolist()
+    n = len(sizes)
+
+    def body(x_hbm, *refs):
+        outs, sem = refs[:-1], refs[-1]
+        copies = []
+        for i in range(n):
+            src = x_hbm.at[:, pl.ds(offsets[i], sizes[i])]
+            copies.append(pltpu.make_async_copy(src, outs[i], sem.at[i]))
+        for copy in copies:
+            copy.start()
+        for copy in copies:
+            copy.wait()
+
+    return call(
+        body, [HBM], [pltpu.VMEM((rows, s), jnp.bfloat16) for s in sizes],
+        (sessions,), 0, [pltpu.SemaphoreType.DMA((n,))],
+    )
+
+
+def project(parts, weight, kinds, wide):
+    rows = parts[0].shape[0]
+    _, depth, width = weight.shape
+    across = width // wide
+    n = len(kinds) * across
+    first = kinds[0]
+
+    def body(*refs):
+        x_refs, (w_hbm, o_ref, buf, sem) = refs[:len(parts)], refs[len(parts):]
+
+        def load(s):
+            src = w_hbm.at[first + s // across, :, pl.ds(s % across * wide, wide)]
+            return pltpu.make_async_copy(src, buf.at[s], sem.at[s])
+
+        for s in range(n):
+            load(s).start()
+
+        @pl.loop(0, n)
+        def _(s):
+            pltpu.make_async_copy(w_hbm.at[0, :, pl.ds(0, wide)], buf.at[s], sem.at[s]).wait()
+            at, total = 0, None
+            for x_ref in x_refs:
+                d = x_ref.shape[1]
+                term = dot32(x_ref[...], buf[s, at:at + d, :])
+                total = term if total is None else total + term
+                at += d
+            cols = pl.ds(pl.multiple_of(lax.rem(s, across) * wide, wide), wide)
+            o_ref[s // across, :, cols] = total.astype(jnp.bfloat16)
+
+    return call(
+        body, [VMEM] * len(parts) + [HBM],
+        [
+            pltpu.VMEM((len(kinds), rows, width), jnp.bfloat16),
+            pltpu.VMEM((n, depth, wide), jnp.bfloat16),
+        ],
+        (*parts, weight), 2 * rows * depth * len(kinds) * width,
+        [pltpu.SemaphoreType.DMA((n,))],
+    )
+
+
+def project_part(x, weights, offset, total):
+    rows, depth = x.shape
+    blocks = sum(w.shape[0] for w in weights)
+    wide = weights[0].shape[2]
+    across = blocks // 3
+
+    def body(x_ref, *refs):
+        w_refs, o_ref = refs[:len(weights)], refs[-1]
+        base = 0
+        for w_ref in w_refs:
+            n = w_ref.shape[0]
+
+            @pl.loop(0, n)
+            def _(s, w_ref=w_ref, base=base):
+                t = s + base
+                at = pl.ds(pl.multiple_of(lax.rem(t, across) * wide, wide), wide)
+                part = dot32(x_ref[...], w_ref[s, offset:offset + depth, :])
+                if total is not None:
+                    part = refs[len(weights)][t // across, :, at] + part
+                o_ref[t // across, :, at] = part
+
+            base += n
+
+    operands = (x, *weights) + (() if total is None else (total,))
+    return call(
+        body, [VMEM] * len(operands),
+        pltpu.VMEM((3, rows, across * wide), jnp.float32), operands,
+        2 * rows * depth * blocks * wide,
+        aliases={} if total is None else {len(operands) - 1: 0},
+    )
+
+
+def biases(place, counts, rows):
+    def body(place_ref, counts_ref, o_ref):
+        mine = place_ref[0] * rows
+        other = (1 - place_ref[0]) * rows
+        for n, (query, key) in enumerate(((mine, mine), (mine, other), (other, mine), (other, other))):
+            i = query + lax.broadcasted_iota(jnp.int32, (rows, 1), 0)
+            first = jnp.zeros((rows, 1), jnp.int32)
+            end = jnp.int32(0)
+            for u in range(counts_ref.shape[0]):
+                end = end + counts_ref[u]
+                first = jnp.where(i >= end, end, first)
+            j = key + lax.broadcasted_iota(jnp.int32, (rows, rows), 1)
+            allowed = jnp.logical_and(j <= i, j >= first)
+            o_ref[n] = jnp.where(allowed, 0.0, -1e30)
+
+    return call(body, [SMEM, SMEM], pltpu.VMEM((4, rows, rows), jnp.float32), (place, counts), 0)
+
+
+def head_out(q, keys, values, masks):
+    scores = [scores_of(q, k) * (HD ** (-0.5) * LOG2E) + b for k, b in zip(keys, masks)]
+    top = functools.reduce(jnp.maximum, [jnp.max(s, axis=1, keepdims=True) for s in scores])
+    raised = [jnp.exp2(s - top) for s in scores]
+    total = sum(jnp.sum(p, axis=1, keepdims=True) for p in raised)
+    out = sum(dot32(p.astype(jnp.bfloat16), v) for p, v in zip(raised, values))
+    return (out / total).astype(jnp.bfloat16)
+
+
+def finish(x, weights, offset, total, own_k, own_v, bias, g):
+    rows, depth = x.shape
+    wide = weights[0].shape[2]
+    across = total.shape[2] // wide
+    cols = slice(g * wide, (g + 1) * wide)
+    where = [(i, s) for i, w in enumerate(weights) for s in range(w.shape[0])]
+
+    def body(x_ref, *refs):
+        w_refs = refs[:len(weights)]
+        t_ref, k_ref, v_ref, bias_ref, mixed_ref, kv_ref = refs[len(weights):]
+        packed = []
+        for c in range(3):
+            i, s = where[c * across + g]
+            part = dot32(x_ref[...], w_refs[i][s, offset:offset + depth, :])
+            packed.append((t_ref[c, :, cols] + part).astype(jnp.bfloat16))
+        q, k, v = packed
+        kv_ref[0] = k
+        kv_ref[1] = v
+        for h in range(wide // HD):
+            at = slice(h * HD, (h + 1) * HD)
+            there = slice(g * wide + h * HD, g * wide + (h + 1) * HD)
+            mixed_ref[:, at] = head_out(
+                q[:, at], (k[:, at], k_ref[0, :, there]), (v[:, at], v_ref[0, :, there]),
+                (bias_ref[3], bias_ref[2]),
+            )
+
+    operands = (x, *weights, total, own_k, own_v, bias)
+    return call(
+        body, [VMEM] * len(operands),
+        [pltpu.VMEM((rows, wide), jnp.bfloat16), pltpu.VMEM((2, rows, wide), jnp.bfloat16)],
+        operands, 6 * rows * depth * wide + 8 * rows * rows * wide,
+    )
+
+
+def own_out(own_q, own_k, own_v, kvs, bias, weight):
+    _, rows, width = own_q.shape
+    model = weight.shape[1]
+    wide = kvs[0].shape[2]
+    step = min(512, model)
+    n = model // step
+
+    def body(q_ref, k_ref, v_ref, *refs):
+        kv_refs = refs[:len(kvs)]
+        bias_ref, w_hbm, o_ref, buf, mixed, sem = refs[len(kvs):]
+
+        def load(s):
+            return pltpu.make_async_copy(w_hbm.at[:, pl.ds(s * step, step)], buf.at[s], sem.at[s])
+
+        for s in range(n):
+            load(s).start()
+        for h in range(width // HD):
+            at = slice(h * HD, (h + 1) * HD)
+            kv_ref, here = kv_refs[h * HD // wide], slice(h * HD % wide, h * HD % wide + HD)
+            mixed[:, at] = head_out(
+                q_ref[0, :, at], (k_ref[0, :, at], kv_ref[0, :, here]),
+                (v_ref[0, :, at], kv_ref[1, :, here]), (bias_ref[0], bias_ref[1]),
+            )
+
+        @pl.loop(0, n)
+        def _(s):
+            pltpu.make_async_copy(w_hbm.at[:, pl.ds(0, step)], buf.at[s], sem.at[s]).wait()
+            cols = pl.ds(pl.multiple_of(s * step, step), step)
+            o_ref[:, cols] = dot32(mixed[...], buf[s])
+
+    return call(
+        body, [VMEM] * (3 + len(kvs)) + [VMEM, HBM],
+        pltpu.VMEM((rows, model), jnp.float32), (own_q, own_k, own_v, *kvs, bias, weight),
+        2 * rows * width * model + 8 * rows * rows * width,
+        [
+            pltpu.VMEM((n, width, step), jnp.bfloat16),
+            pltpu.VMEM((rows, width), jnp.bfloat16),
+            pltpu.SemaphoreType.DMA((n,)),
+        ],
+        mib=6 + (2 * width * model >> 20),
+    )
+
+
+def other_out(user, table, mixed, row_offset, pieces, total, last):
+    rows, depth = mixed.shape
+    model = total.shape[1]
+    wide = pieces[0].shape[-1]
+    n = len(pieces)
+
+    def body(user_ref, table_ref, mixed_ref, total_ref, *refs):
+        piece_refs, o_ref = refs[:len(pieces)], refs[len(pieces)]
+
+        def columns(s):
+            return pl.ds(pl.multiple_of(table_ref[user_ref[0] * n + s] * wide, wide), wide)
+
+        if last:
+            buf, sem = refs[len(pieces) + 1:]
+
+            def store(s):
+                return pltpu.make_async_copy(buf.at[s], o_ref.at[:, columns(s)], sem.at[s])
+
+        for s in range(n):
+            part = dot32(mixed_ref[...], piece_refs[s][row_offset:row_offset + depth, :])
+            part = total_ref[:, columns(s)] + part
+            if last:
+                buf[s] = part.astype(jnp.bfloat16)
+                store(s).start()
+            else:
+                o_ref[:, columns(s)] = part
+        if last:
+            for s in range(n):
+                store(s).wait()
+
+    operands = (user, table, mixed, total, *pieces)
+    return call(
+        body, [SMEM, SMEM] + [VMEM] * (2 + len(pieces)),
+        jax.ShapeDtypeStruct((rows, model), jnp.bfloat16) if last else pltpu.VMEM((rows, model), jnp.float32),
+        operands, 2 * rows * depth * model,
+        [pltpu.VMEM((n, rows, wide), jnp.bfloat16), pltpu.SemaphoreType.DMA((n,))] if last else (),
+        aliases={} if last else {3: 0},
+        out_specs=HBM if last else VMEM,
+    )
+
+
+def two_halves(ring, sessions, input_weight, output_weight, session_counts):
+    users = 2 * len(ring)
+    chips = len(ring)
+    rows, model = sessions.shape
+    width = input_weight.shape[2]
+    wide = min(512, width)
+    place = lax.axis_index("heads").astype(jnp.int32)[None]
+    user = lax.axis_index("users").astype(jnp.int32)[None]
+
+    across = [(0, 1), (1, 0)]
+    beside = [(a, b) for pair in ring for a, b in (pair, pair[::-1])]
+    around = []
+    for i in range(chips):
+        around.append((ring[i][0], ring[(i + 1) % chips][0]))
+        around.append((ring[i][1], ring[(i - 1) % chips][1]))
+
+    full = (chips - 1) // 2
+    half = chips % 2 == 0
+    table = np.zeros((users, users), np.int32)
+    for i in range(chips):
+        for core in range(2):
+            held = [(i, core), (i, 1 - core)]
+            for k in range(1, full + 1):
+                for c in (core, 1 - core):
+                    source = (i - k) % chips if c == 0 else (i + k) % chips
+                    held += [(source, c), (source, 1 - c)]
+            if half:
+                far = (i + chips // 2) % chips
+                held += [(far, core), (far, 1 - core)]
+            table[ring[i][core]] = [ring[a][b] for a, b in held]
+    table = jnp.asarray(table.reshape(-1))
+
+    sizes = [model // 2, model // 4, model // 8, model // 8]
+    offsets = np.cumsum([0] + sizes)[:-1].tolist()
+    piece = load_piece(user, place, output_weight, model // users)
+    parts = load_rows(sessions, sizes)
+
+    crossed = lax.ppermute(piece, "heads", across)
+    guests = [lax.ppermute(x, "heads", across) for x in parts]
+
+    near, far = crossed, lax.ppermute(crossed, "users", beside)
+    pieces = [near, far]
+    for _ in range(full):
+        near = lax.ppermute(near, "users", around)
+        far = lax.ppermute(far, "users", around)
+        pieces += [near, far]
+        pieces += [lax.ppermute(near, "users", beside), lax.ppermute(far, "users", beside)]
+    if half:
+        near = lax.ppermute(near, "users", around)
+        pieces += [near, lax.ppermute(near, "users", beside)]
+
+    own_q, w_q = project(parts, input_weight, (0,), wide)
+    own_k, w_k = project(parts, input_weight, (1,), wide)
+    own_v, w_v = project(parts, input_weight, (2,), wide)
+    weights = (w_q, w_k, w_v)
+    bias = biases(place, session_counts, rows)
+    total = None
+    for i in range(len(sizes) - 1):
+        total = project_part(guests[i], weights, offsets[i], total)
+    mixed_far, kvs = [], []
+    for g in range(width // wide):
+        mixed, kv = finish(guests[-1], weights, offsets[-1], total, own_k, own_v, bias, g)
+        mixed_far.append(lax.ppermute(mixed, "heads", across))
+        kvs.append(kv)
+    out = own_out(own_q, own_k, own_v, kvs, bias, output_weight)
+    for g, mixed in enumerate(mixed_far):
+        out = other_out(user, table, mixed, g * wide, pieces, out, g == len(mixed_far) - 1)
+    return out
+
+
 def solution(mesh):
     in_specs = (P(("users", "heads"), None), P(None, None, "heads"), P("heads", None), P("users"))
     out_specs = P(("users", "heads"), None)
+    if mesh.shape["heads"] == 2 and mesh.shape["users"] % 2 == 0 and mesh.shape["users"] > 2:
+        per_device = functools.partial(two_halves, chip_ring(mesh))
+
+        def layer(*args):
+            return per_device(*args)
+
+        return jax.shard_map(
+            layer, mesh=mesh, in_specs=in_specs, out_specs=out_specs, check_vma=False
+        )
     return jax.shard_map(
-        per_device, mesh=mesh, in_specs=in_specs, out_specs=out_specs, check_vma=False
-    )
+        gather_and_scatter, mesh=mesh, in_specs=in_specs, out_specs=out_specs, check_vma=False
+    )

time: 168 us -> 94.8 us (0.56)
  waiting for transfers between devices: 115 us -> 28.6 us
  Pallas kernels: 0 us -> 41.7 us
  matrix products: 37.8 us -> 0 us
  starting transfers between devices: 0.04 us -> 23.9 us
  between operations: 13.4 us -> 0.36 us
    all_gather x1 -> x0, waiting for transfers between devices: 59.9 us -> none  [per_device(): lax.all_gather(sessions, 'heads', axis=0, tiled=True)]
    reduce_scatter x1 -> x0, waiting for transfers between devices: 54.5 us -> none  [per_device(): lax.psum_scatter(jnp.dot(mixed, output_weight, preferred_element_type=jnp...]
    pallas_call x0 -> x14, Pallas kernels: none -> 41.7 us  [call(): pl.pallas_call(body, in_specs=in_specs, out_specs=out_specs if out_specs...]
    dot_general x3 -> x0, matrix products: 31.8 us -> none  [the longest x1 18.2 us: per_device(): jnp.einsum('nd,cde->cne', lax.all_gather(sessions, 'heads', axis=0, tiled...]
    ppermute x0 -> x22, waiting for transfers between devices: none -> 28.6 us  [the longest x1 11.9 us: two_halves(): crossed = lax.ppermute(piece, 'heads', across)]
    ppermute x0 -> x22, starting transfers between devices: none -> 23.9 us  [the longest x4 6.85 us: two_halves(): near = lax.ppermute(near, 'users', around)]
    sub x1 -> x0, matrix products: 5.92 us -> none  [one_block(): raised = jnp.where(mask_block[None], jnp.exp(scores - highest), 0.0)]
  transfers between devices with their start and end apart: 2 -> 22, of which waited for: 2 -> 7; matrix products, arithmetic and copies ran while one was open for 1% -> 0% of each run, Pallas kernels for 0% -> 40%
where the time goes in v2:
time: 94.8 us; the launch traced here: 94.6 us
  Pallas kernels  41.7 us (44%)
  waiting for transfers between devices  28.6 us (30%)
  starting transfers between devices  23.9 us (25%)
    pallas_call x14, Pallas kernels, call(): pl.pallas_call(body, in_specs=in_specs, out_specs=out_specs if out_specs...  41.7 us
    ppermute x1, waiting for transfers between devices, two_halves(): crossed = lax.ppermute(piece, 'heads', across)  11.9 us
    ppermute x4, waiting for transfers between devices, two_halves(): guests = [lax.ppermute(x, 'heads', across) for x in parts]  7.23 us
    ppermute x4, starting transfers between devices, two_halves(): near = lax.ppermute(near, 'users', around)  6.85 us
    ppermute x2, waiting for transfers between devices, two_halves(): mixed_far.append(lax.ppermute(mixed, 'heads', across))  6.37 us
    ppermute x4, starting transfers between devices, two_halves(): guests = [lax.ppermute(x, 'heads', across) for x in parts]  5.07 us
    ppermute x3, starting transfers between devices, two_halves(): far = lax.ppermute(far, 'users', around)  4.73 us
    ppermute x2, starting transfers between devices, two_halves(): mixed_far.append(lax.ppermute(mixed, 'heads', across))  3.12 us
  transfers between devices with their start and end apart: 22, of which 7 were waited for; matrix products, arithmetic and copies ran while one was open for 0% of the time, Pallas kernels for 40%

profile of v2, /device:TPU:0, one launch (start us, length us, event | category | flops | bytes accessed | tf_op | source)
XLA Modules:
  0.0 94.6 jit_solution(9075499388612182123)
XLA Ops:
  0.0 1.0 %shard_map.66 = bf16[1024,256]{1,0:T(8,128)(2,1)S(1)} custom-call(s32[1]{0:T(128)} %bitcast.user_ref, s32[1]{0:T(128)} %bitcast.1.place_ref, bf16[1024,4096]{1,0:T(8,128)(2,1)} %w_hbm.1), custom_call_target="tpu_custom_call" | custom-call | bytes 1048576 | tf_op jit(solution)/shard_map/pallas_call | solution.py:120
  1.1 3.0 %collective-permute-start.6 = (bf16[1024,256]{1,0:T(8,128)(2,1)S(1)}, bf16[1024,256]{1,0:T(8,128)(2,1)S(1)}, u32[]{:S(2)}, u32[]{:S(2)}) collective-permute-start(bf16[1024,256]{1,0:T(8,128)(2,1)S(1)} %shard_map.66), channel_id=1, source_target_pairs={{0,1},{1,0},{2,3},{3,2},{4,5},{5,4},{6,7},{7,6},{8,9},{9,8},{10,11... | collective-permute-start | bytes 1572872 | tf_op jit(solution)/shard_map/ppermute | solution.py:423
  4.1 11.9 %collective-permute-done.6.refs_0_ = bf16[1024,256]{1,0:T(8,128)(2,1)S(1)} collective-permute-done((bf16[1024,256]{1,0:T(8,128)(2,1)S(1)}, bf16[1024,256]{1,0:T(8,128)(2,1)S(1)}, u32[]{:S(2)}, u32[]{:S(2)}) %collective-permute-start.6) | collective-permute-done | bytes 524320 | tf_op jit(solution)/shard_map/ppermute | solution.py:423
  16.0 1.8 %collective-permute-start.8 = (bf16[1024,256]{1,0:T(8,128)(2,1)S(1)}, bf16[1024,256]{1,0:T(8,128)(2,1)S(1)}, u32[]{:S(2)}, u32[]{:S(2)}) collective-permute-start(bf16[1024,256]{1,0:T(8,128)(2,1)S(1)} %collective-permute-done.6.refs_0_), channel_id=1, source_target_pairs={{0,8},{2,6},{8,16},{10,2},{16,24},{18,10},{24,28},{26,18},{28,20},... | collective-permute-start | bytes 1572872 | tf_op jit(solution)/shard_map/ppermute | solution.py:429
  17.8 1.5 %shard_map.55 = (bf16[256,2048]{1,0:T(8,128)(2,1)S(1)}, bf16[256,1024]{1,0:T(8,128)(2,1)S(1)}, bf16[256,512]{1,0:T(8,128)(2,1)S(1)}, bf16[256,512]{1,0:T(8,128)(2,1)S(1)}) custom-call(bf16[256,4096]{1,0:T(8,128)(2,1)} %x_hbm.1), custom_call_target="tpu_custom_call" | custom-call | bytes 1048576 | tf_op jit(solution)/shard_map/pallas_call | solution.py:120
  19.4 1.6 %collective-permute-start.3 = (bf16[256,2048]{1,0:T(8,128)(2,1)S(1)}, bf16[256,2048]{1,0:T(8,128)(2,1)S(1)}, u32[]{:S(2)}, u32[]{:S(2)}) collective-permute-start(bf16[256,2048]{1,0:T(8,128)(2,1)S(1)} %get-tuple-element.20.refs_0_), channel_id=1, source_target_pairs={{0,1},{1,0},{2,3},{3,2},{4,5},{5,4},{6,7},{7,6},{8,9},{9,8},{10,11... | collective-permute-start | bytes 3145736 | tf_op jit(solution)/shard_map/ppermute | solution.py:424
  21.5 1.5 %collective-permute-start.1 = (bf16[256,512]{1,0:T(8,128)(2,1)S(1)}, bf16[256,512]{1,0:T(8,128)(2,1)S(1)}, u32[]{:S(2)}, u32[]{:S(2)}) collective-permute-start(bf16[256,512]{1,0:T(8,128)(2,1)S(1)} %get-tuple-element.22.refs_2_), channel_id=1, source_target_pairs={{0,1},{1,0},{2,3},{3,2},{4,5},{5,4},{6,7},{7,6},{8,9},{9,8},{10,11... | collective-permute-start | bytes 786440 | tf_op jit(solution)/shard_map/ppermute | solution.py:424
  23.0 2.2 %collective-permute-done.8.refs_2_ = bf16[1024,256]{1,0:T(8,128)(2,1)S(1)} collective-permute-done((bf16[1024,256]{1,0:T(8,128)(2,1)S(1)}, bf16[1024,256]{1,0:T(8,128)(2,1)S(1)}, u32[]{:S(2)}, u32[]{:S(2)}) %collective-permute-start.8) | collective-permute-done | bytes 524320 | tf_op jit(solution)/shard_map/ppermute | solution.py:429
  25.2 1.8 %collective-permute-start.12 = (bf16[1024,256]{1,0:T(8,128)(2,1)S(1)}, bf16[1024,256]{1,0:T(8,128)(2,1)S(1)}, u32[]{:S(2)}, u32[]{:S(2)}) collective-permute-start(bf16[1024,256]{1,0:T(8,128)(2,1)S(1)} %collective-permute-done.8.refs_2_), channel_id=1, source_target_pairs={{0,8},{2,6},{8,16},{10,2},{16,24},{18,10},{24,28},{26,18},{28,20},... | collective-permute-start | bytes 1572872 | tf_op jit(solution)/shard_map/ppermute | solution.py:429
  27.0 1.6 %collective-permute-start.9 = (bf16[1024,256]{1,0:T(8,128)(2,1)S(1)}, bf16[1024,256]{1,0:T(8,128)(2,1)S(1)}, u32[]{:S(2)}, u32[]{:S(2)}) collective-permute-start(bf16[1024,256]{1,0:T(8,128)(2,1)S(1)} %collective-permute-done.7.refs_1_), channel_id=1, source_target_pairs={{0,8},{2,6},{8,16},{10,2},{16,24},{18,10},{24,28},{26,18},{28,20},... | collective-permute-start | bytes 1572872 | tf_op jit(solution)/shard_map/ppermute | solution.py:430
  28.6 4.7 %shard_map.57 = (bf16[1,256,1024]{2,1,0:T(8,128)(2,1)S(1)}, bf16[2,4096,512]{2,1,0:T(8,128)(2,1)S(1)}) custom-call(bf16[256,2048]{1,0:T(8,128)(2,1)S(1)} %get-tuple-element.20.refs_0_, bf16[256,1024]{1,0:T(8,128)(2,1)S(1)} %get-tuple-element.21.refs_1_, bf16[256,512]{1,0:T(8,128)(2,1)S(1)} %get-tuple-element.22.refs_2_, ...), custom_call_target="tpu_custom_call" | custom-call | flops 2147483648 | bytes 1048576 | tf_op jit(solution)/shard_map/pallas_call | solution.py:120
  33.3 4.7 %shard_map.58 = (bf16[1,256,1024]{2,1,0:T(8,128)(2,1)S(1)}, bf16[2,4096,512]{2,1,0:T(8,128)(2,1)S(1)}) custom-call(bf16[256,2048]{1,0:T(8,128)(2,1)S(1)} %get-tuple-element.20.refs_0_, bf16[256,1024]{1,0:T(8,128)(2,1)S(1)} %get-tuple-element.21.refs_1_, bf16[256,512]{1,0:T(8,128)(2,1)S(1)} %get-tuple-element.22.refs_2_, ...), custom_call_target="tpu_custom_call" | custom-call | flops 2147483648 | bytes 1048576 | tf_op jit(solution)/shard_map/pallas_call | solution.py:120
  38.9 4.7 %shard_map.56 = (bf16[1,256,1024]{2,1,0:T(8,128)(2,1)S(1)}, bf16[2,4096,512]{2,1,0:T(8,128)(2,1)S(1)}) custom-call(bf16[256,2048]{1,0:T(8,128)(2,1)S(1)} %get-tuple-element.20.refs_0_, bf16[256,1024]{1,0:T(8,128)(2,1)S(1)} %get-tuple-element.21.refs_1_, bf16[256,512]{1,0:T(8,128)(2,1)S(1)} %get-tuple-element.22.refs_2_, ...), custom_call_target="tpu_custom_call" | custom-call | flops 2147483648 | bytes 1048576 | tf_op jit(solution)/shard_map/pallas_call | solution.py:120
  43.6 1.9 %collective-permute-done.3.x_ref = bf16[256,2048]{1,0:T(8,128)(2,1)S(1)} collective-permute-done((bf16[256,2048]{1,0:T(8,128)(2,1)S(1)}, bf16[256,2048]{1,0:T(8,128)(2,1)S(1)}, u32[]{:S(2)}, u32[]{:S(2)}) %collective-permute-start.3) | collective-permute-done | bytes 1048608 | tf_op jit(solution)/shard_map/ppermute | solution.py:424
  45.5 1.5 %collective-permute-start = (bf16[256,512]{1,0:T(8,128)(2,1)S(1)}, bf16[256,512]{1,0:T(8,128)(2,1)S(1)}, u32[]{:S(2)}, u32[]{:S(2)}) collective-permute-start(bf16[256,512]{1,0:T(8,128)(2,1)S(1)} %get-tuple-element.19.refs_3_), channel_id=1, source_target_pairs={{0,1},{1,0},{2,3},{3,2},{4,5},{5,4},{6,7},{7,6},{8,9},{9,8},{10,11... | collective-permute-start | bytes 786440 | tf_op jit(solution)/shard_map/ppermute | solution.py:424
  47.0 1.6 %collective-permute-start.16 = (bf16[1024,256]{1,0:T(8,128)(2,1)S(1)}, bf16[1024,256]{1,0:T(8,128)(2,1)S(1)}, u32[]{:S(2)}, u32[]{:S(2)}) collective-permute-start(bf16[1024,256]{1,0:T(8,128)(2,1)S(1)} %collective-permute-done.12.refs_6_), channel_id=1, source_target_pairs={{0,8},{2,6},{8,16},{10,2},{16,24},{18,10},{24,28},{26,18},{28,20},... | collective-permute-start | bytes 1572872 | tf_op jit(solution)/shard_map/ppermute | solution.py:429
  48.6 1.6 %collective-permute-start.13 = (bf16[1024,256]{1,0:T(8,128)(2,1)S(1)}, bf16[1024,256]{1,0:T(8,128)(2,1)S(1)}, u32[]{:S(2)}, u32[]{:S(2)}) collective-permute-start(bf16[1024,256]{1,0:T(8,128)(2,1)S(1)} %collective-permute-done.9.refs_3_), channel_id=1, source_target_pairs={{0,8},{2,6},{8,16},{10,2},{16,24},{18,10},{24,28},{26,18},{28,20},... | collective-permute-start | bytes 1572872 | tf_op jit(solution)/shard_map/ppermute | solution.py:430
  50.1 4.2 %shard_map.59.refs_3_ = f32[3,256,1024]{2,1,0:T(8,128)S(1)} custom-call(bf16[256,2048]{1,0:T(8,128)(2,1)S(1)} %collective-permute-done.3.x_ref, bf16[2,4096,512]{2,1,0:T(8,128)(2,1)S(1)} %get-tuple-element.23.refs_0_, bf16[2,4096,512]{2,1,0:T(8,128)(2,1)S(1)} %get-tuple-element.24.refs_1_, bf16[2,4096,512]{2,1,0:T(8,128)(2,1)S(1)} %get-tuple-element.25.refs_2_), custom_call_target="tpu_custom_call" | custom-call | flops 3221225472 | bytes 1048576 | tf_op jit(solution)/shard_map/pallas_call | solution.py:120
  54.4 2.3 %collective-permute-done.2.x_ref = bf16[256,1024]{1,0:T(8,128)(2,1)S(1)} collective-permute-done((bf16[256,1024]{1,0:T(8,128)(2,1)S(1)}, bf16[256,1024]{1,0:T(8,128)(2,1)S(1)}, u32[]{:S(2)}, u32[]{:S(2)}) %collective-permute-start.2) | collective-permute-done | bytes 524320 | tf_op jit(solution)/shard_map/ppermute | solution.py:424
  56.7 2.6 %shard_map.60.refs_3_ = f32[3,256,1024]{2,1,0:T(8,128)S(1)} custom-call(bf16[256,1024]{1,0:T(8,128)(2,1)S(1)} %collective-permute-done.2.x_ref, bf16[2,4096,512]{2,1,0:T(8,128)(2,1)S(1)} %get-tuple-element.23.refs_0_, bf16[2,4096,512]{2,1,0:T(8,128)(2,1)S(1)} %get-tuple-element.24.refs_1_, ...), custom_call_target="tpu_custom_call", output_to_operand_aliasing={{}: (4, {})} | custom-call | flops 1610612736 | bytes 1048576 | tf_op jit(solution)/shard_map/pallas_call | solution.py:120
  59.4 3.0 %collective-permute-done.1.x_ref = bf16[256,512]{1,0:T(8,128)(2,1)S(1)} collective-permute-done((bf16[256,512]{1,0:T(8,128)(2,1)S(1)}, bf16[256,512]{1,0:T(8,128)(2,1)S(1)}, u32[]{:S(2)}, u32[]{:S(2)}) %collective-permute-start.1) | collective-permute-done | bytes 262176 | tf_op jit(solution)/shard_map/ppermute | solution.py:424
  62.3 1.8 %shard_map.61.refs_3_ = f32[3,256,1024]{2,1,0:T(8,128)S(1)} custom-call(bf16[256,512]{1,0:T(8,128)(2,1)S(1)} %collective-permute-done.1.x_ref, bf16[2,4096,512]{2,1,0:T(8,128)(2,1)S(1)} %get-tuple-element.23.refs_0_, bf16[2,4096,512]{2,1,0:T(8,128)(2,1)S(1)} %get-tuple-element.24.refs_1_, ...), custom_call_target="tpu_custom_call", output_to_operand_aliasing={{}: (4, {})} | custom-call | flops 805306368 | bytes 1048576 | tf_op jit(solution)/shard_map/pallas_call | solution.py:120
  64.3 1.6 %collective-permute-start.20 = (bf16[1024,256]{1,0:T(8,128)(2,1)S(1)}, bf16[1024,256]{1,0:T(8,128)(2,1)S(1)}, u32[]{:S(2)}, u32[]{:S(2)}) collective-permute-start(bf16[1024,256]{1,0:T(8,128)(2,1)S(1)} %collective-permute-done.16.refs_10_), channel_id=1, source_target_pairs={{0,8},{2,6},{8,16},{10,2},{16,24},{18,10},{24,28},{26,18},{28,20},... | collective-permute-start | bytes 1572872 | tf_op jit(solution)/shard_map/ppermute | solution.py:434
  65.9 1.6 %collective-permute-start.17 = (bf16[1024,256]{1,0:T(8,128)(2,1)S(1)}, bf16[1024,256]{1,0:T(8,128)(2,1)S(1)}, u32[]{:S(2)}, u32[]{:S(2)}) collective-permute-start(bf16[1024,256]{1,0:T(8,128)(2,1)S(1)} %collective-permute-done.13.refs_7_), channel_id=1, source_target_pairs={{0,8},{2,6},{8,16},{10,2},{16,24},{18,10},{24,28},{26,18},{28,20},... | collective-permute-start | bytes 1572872 | tf_op jit(solution)/shard_map/ppermute | solution.py:430
  67.5 1.8 %shard_map.64 = (bf16[256,512]{1,0:T(8,128)(2,1)S(1)}, bf16[2,256,512]{2,1,0:T(8,128)(2,1)S(1)}) custom-call(bf16[256,512]{1,0:T(8,128)(2,1)S(1)} %collective-permute-done.x_ref, bf16[2,4096,512]{2,1,0:T(8,128)(2,1)S(1)} %get-tuple-element.23.refs_0_, bf16[2,4096,512]{2,1,0:T(8,128)(2,1)S(1)} %get-tuple-element.24.refs_1_, ...), custom_call_target="tpu_custom_call" | custom-call | flops 671088640 | bytes 1048576 | tf_op jit(solution)/shard_map/pallas_call | solution.py:120
  69.3 1.6 %collective-permute-start.5 = (bf16[256,512]{1,0:T(8,128)(2,1)S(1)}, bf16[256,512]{1,0:T(8,128)(2,1)S(1)}, u32[]{:S(2)}, u32[]{:S(2)}) collective-permute-start(bf16[256,512]{1,0:T(8,128)(2,1)S(1)} %get-tuple-element.29), channel_id=1, source_target_pairs={{0,1},{1,0},{2,3},{3,2},{4,5},{5,4},{6,7},{7,6},{8,9},{9,8},{10,11... | collective-permute-start | bytes 786440 | tf_op jit(solution)/shard_map/ppermute | solution.py:448
  70.8 6.4 %collective-permute-done.5.mixed_ref = bf16[256,512]{1,0:T(8,128)(2,1)S(1)} collective-permute-done((bf16[256,512]{1,0:T(8,128)(2,1)S(1)}, bf16[256,512]{1,0:T(8,128)(2,1)S(1)}, u32[]{:S(2)}, u32[]{:S(2)}) %collective-permute-start.5) | collective-permute-done | bytes 262176 | tf_op jit(solution)/shard_map/ppermute | solution.py:448
  79.1 1.8 %shard_map.63 = (bf16[256,512]{1,0:T(8,128)(2,1)S(1)}, bf16[2,256,512]{2,1,0:T(8,128)(2,1)S(1)}) custom-call(bf16[256,512]{1,0:T(8,128)(2,1)S(1)} %collective-permute-done.x_ref, bf16[2,4096,512]{2,1,0:T(8,128)(2,1)S(1)} %get-tuple-element.23.refs_0_, bf16[2,4096,512]{2,1,0:T(8,128)(2,1)S(1)} %get-tuple-element.24.refs_1_, ...), custom_call_target="tpu_custom_call" | custom-call | flops 671088640 | bytes 1048576 | tf_op jit(solution)/shard_map/pallas_call | solution.py:120
  80.9 1.6 %collective-permute-start.4 = (bf16[256,512]{1,0:T(8,128)(2,1)S(1)}, bf16[256,512]{1,0:T(8,128)(2,1)S(1)}, u32[]{:S(2)}, u32[]{:S(2)}) collective-permute-start(bf16[256,512]{1,0:T(8,128)(2,1)S(1)} %get-tuple-element.28), channel_id=1, source_target_pairs={{0,1},{1,0},{2,3},{3,2},{4,5},{5,4},{6,7},{7,6},{8,9},{9,8},{10,11... | collective-permute-start | bytes 786440 | tf_op jit(solution)/shard_map/ppermute | solution.py:448
  82.5 7.1 %shard_map.65.total_ref = f32[256,4096]{1,0:T(8,128)S(1)} custom-call(bf16[1,256,1024]{2,1,0:T(8,128)(2,1)S(1)} %get-tuple-element.30.q_ref, bf16[1,256,1024]{2,1,0:T(8,128)(2,1)S(1)} %get-tuple-element.26.refs_4_.k_ref, bf16[1,256,1024]{2,1,0:T(8,128)(2,1)S(1)} %get-tuple-element.27.refs_5_.v_ref, bf16[2,256,512]{2,1,0:T(8,128)(2,1)S(1)} %get-tuple-element.31.refs_0_, ...), custom_call_target="tpu_custom_call" | custom-call | flops 2684354560 | bytes 1048576 | tf_op jit(solution)/shard_map/pallas_call | solution.py:120
  89.7 2.1 %shard_map.67.total_ref = f32[256,4096]{1,0:T(8,128)S(1)} custom-call(s32[1]{0:T(128)} %bitcast.user_ref, s32[256]{0:T(256)S(1)} %copy-done, bf16[256,512]{1,0:T(8,128)(2,1)S(1)} %collective-permute-done.5.mixed_ref, f32[256,4096]{1,0:T(8,128)S(1)} %shard_map.65.total_ref, ...), custom_call_target="tpu_custom_call", output_to_operand_aliasing={{}: (3, {})} | custom-call | flops 1073741824 | bytes 1048576 | tf_op jit(solution)/shard_map/pallas_call | solution.py:120
  91.8 2.7 %shard_map.68 = bf16[256,4096]{1,0:T(8,128)(2,1)} custom-call(s32[1]{0:T(128)} %bitcast.user_ref, s32[256]{0:T(256)S(1)} %copy-done, bf16[256,512]{1,0:T(8,128)(2,1)S(1)} %collective-permute-done.4.mixed_ref, f32[256,4096]{1,0:T(8,128)S(1)} %shard_map.67.total_ref, bf16[1024,256]{1,0:T(8,128)(2,1)S(1)} %collective-permute-done.6.refs_0_, ...), custom_call_target="tpu_custom_call" | custom-call | flops 1073741824 | bytes 1048576 | tf_op jit(solution)/shard_map/pallas_call | solution.py:120
  (30 shorter events, 3.3 us)
Async XLA Ops:
  1.1 15.0 %collective-permute-start.6 = (bf16[1024,256]{1,0:T(8,128)(2,1)S(1)}, bf16[1024,256]{1,0:T(8,128)(2,1)S(1)}, u32[]{:S(2)}, u32[]{:S(2)}) collective-permute-start(bf16[1024,256]{1,0:T(8,128)(2,1)S(1)} %shard_map.66), channel_id=1, source_target_pairs={{0,1},{1,0},{2,3},{3,2},{4,5},{5,4},{6,7},{7,6},{8,9},{9,8},{10,11... | collective-permute-start | bytes 1572872 | tf_op jit(solution)/shard_map/ppermute | solution.py:423
  16.0 9.2 %collective-permute-start.8 = (bf16[1024,256]{1,0:T(8,128)(2,1)S(1)}, bf16[1024,256]{1,0:T(8,128)(2,1)S(1)}, u32[]{:S(2)}, u32[]{:S(2)}) collective-permute-start(bf16[1024,256]{1,0:T(8,128)(2,1)S(1)} %collective-permute-done.6.refs_0_), channel_id=1, source_target_pairs={{0,8},{2,6},{8,16},{10,2},{16,24},{18,10},{24,28},{26,18},{28,20},... | collective-permute-start | bytes 1572872 | tf_op jit(solution)/shard_map/ppermute | solution.py:429
  17.8 9.2 %collective-permute-start.7 = (bf16[1024,256]{1,0:T(8,128)(2,1)S(1)}, bf16[1024,256]{1,0:T(8,128)(2,1)S(1)}, u32[]{:S(2)}, u32[]{:S(2)}) collective-permute-start(bf16[1024,256]{1,0:T(8,128)(2,1)S(1)} %collective-permute-done.6.refs_0_), channel_id=1, source_target_pairs={{0,2},{2,0},{8,10},{10,8},{16,18},{18,16},{24,26},{26,24},{28,30},... | collective-permute-start | bytes 1572872 | tf_op jit(solution)/shard_map/ppermute | solution.py:426
  19.4 26.1 %collective-permute-start.3 = (bf16[256,2048]{1,0:T(8,128)(2,1)S(1)}, bf16[256,2048]{1,0:T(8,128)(2,1)S(1)}, u32[]{:S(2)}, u32[]{:S(2)}) collective-permute-start(bf16[256,2048]{1,0:T(8,128)(2,1)S(1)} %get-tuple-element.20.refs_0_), channel_id=1, source_target_pairs={{0,1},{1,0},{2,3},{3,2},{4,5},{5,4},{6,7},{7,6},{8,9},{9,8},{10,11... | collective-permute-start | bytes 3145736 | tf_op jit(solution)/shard_map/ppermute | solution.py:424
  20.9 35.8 %collective-permute-start.2 = (bf16[256,1024]{1,0:T(8,128)(2,1)S(1)}, bf16[256,1024]{1,0:T(8,128)(2,1)S(1)}, u32[]{:S(2)}, u32[]{:S(2)}) collective-permute-start(bf16[256,1024]{1,0:T(8,128)(2,1)S(1)} %get-tuple-element.21.refs_1_), channel_id=1, source_target_pairs={{0,1},{1,0},{2,3},{3,2},{4,5},{5,4},{6,7},{7,6},{8,9},{9,8},{10,11... | collective-permute-start | bytes 1572872 | tf_op jit(solution)/shard_map/ppermute | solution.py:424
  21.5 40.9 %collective-permute-start.1 = (bf16[256,512]{1,0:T(8,128)(2,1)S(1)}, bf16[256,512]{1,0:T(8,128)(2,1)S(1)}, u32[]{:S(2)}, u32[]{:S(2)}) collective-permute-start(bf16[256,512]{1,0:T(8,128)(2,1)S(1)} %get-tuple-element.22.refs_2_), channel_id=1, source_target_pairs={{0,1},{1,0},{2,3},{3,2},{4,5},{5,4},{6,7},{7,6},{8,9},{9,8},{10,11... | collective-permute-start | bytes 786440 | tf_op jit(solution)/shard_map/ppermute | solution.py:424
  25.2 21.8 %collective-permute-start.12 = (bf16[1024,256]{1,0:T(8,128)(2,1)S(1)}, bf16[1024,256]{1,0:T(8,128)(2,1)S(1)}, u32[]{:S(2)}, u32[]{:S(2)}) collective-permute-start(bf16[1024,256]{1,0:T(8,128)(2,1)S(1)} %collective-permute-done.8.refs_2_), channel_id=1, source_target_pairs={{0,8},{2,6},{8,16},{10,2},{16,24},{18,10},{24,28},{26,18},{28,20},... | collective-permute-start | bytes 1572872 | tf_op jit(solution)/shard_map/ppermute | solution.py:429
  27.0 21.5 %collective-permute-start.9 = (bf16[1024,256]{1,0:T(8,128)(2,1)S(1)}, bf16[1024,256]{1,0:T(8,128)(2,1)S(1)}, u32[]{:S(2)}, u32[]{:S(2)}) collective-permute-start(bf16[1024,256]{1,0:T(8,128)(2,1)S(1)} %collective-permute-done.7.refs_1_), channel_id=1, source_target_pairs={{0,8},{2,6},{8,16},{10,2},{16,24},{18,10},{24,28},{26,18},{28,20},... | collective-permute-start | bytes 1572872 | tf_op jit(solution)/shard_map/ppermute | solution.py:430
  33.3 4.8 %copy-start.1 = (s32[2]{0:T(128)S(1)}, s32[2]{0:T(128)}, u32[]{:S(2)}) copy-start(s32[2]{0:T(128)} %counts_ref.1) | copy-start | bytes 28
  45.5 22.0 %collective-permute-start = (bf16[256,512]{1,0:T(8,128)(2,1)S(1)}, bf16[256,512]{1,0:T(8,128)(2,1)S(1)}, u32[]{:S(2)}, u32[]{:S(2)}) collective-permute-start(bf16[256,512]{1,0:T(8,128)(2,1)S(1)} %get-tuple-element.19.refs_3_), channel_id=1, source_target_pairs={{0,1},{1,0},{2,3},{3,2},{4,5},{5,4},{6,7},{7,6},{8,9},{9,8},{10,11... | collective-permute-start | bytes 786440 | tf_op jit(solution)/shard_map/ppermute | solution.py:424
  47.0 17.3 %collective-permute-start.16 = (bf16[1024,256]{1,0:T(8,128)(2,1)S(1)}, bf16[1024,256]{1,0:T(8,128)(2,1)S(1)}, u32[]{:S(2)}, u32[]{:S(2)}) collective-permute-start(bf16[1024,256]{1,0:T(8,128)(2,1)S(1)} %collective-permute-done.12.refs_6_), channel_id=1, source_target_pairs={{0,8},{2,6},{8,16},{10,2},{16,24},{18,10},{24,28},{26,18},{28,20},... | collective-permute-start | bytes 1572872 | tf_op jit(solution)/shard_map/ppermute | solution.py:429
  48.6 17.3 %collective-permute-start.13 = (bf16[1024,256]{1,0:T(8,128)(2,1)S(1)}, bf16[1024,256]{1,0:T(8,128)(2,1)S(1)}, u32[]{:S(2)}, u32[]{:S(2)}) collective-permute-start(bf16[1024,256]{1,0:T(8,128)(2,1)S(1)} %collective-permute-done.9.refs_3_), channel_id=1, source_target_pairs={{0,8},{2,6},{8,16},{10,2},{16,24},{18,10},{24,28},{26,18},{28,20},... | collective-permute-start | bytes 1572872 | tf_op jit(solution)/shard_map/ppermute | solution.py:430
  56.7 20.5 %collective-permute-start.10 = (bf16[1024,256]{1,0:T(8,128)(2,1)S(1)}, bf16[1024,256]{1,0:T(8,128)(2,1)S(1)}, u32[]{:S(2)}, u32[]{:S(2)}) collective-permute-start(bf16[1024,256]{1,0:T(8,128)(2,1)S(1)} %collective-permute-done.8.refs_2_), channel_id=1, source_target_pairs={{0,2},{2,0},{8,10},{10,8},{16,18},{18,16},{24,26},{26,24},{28,30},... | collective-permute-start | bytes 1572872 | tf_op jit(solution)/shard_map/ppermute | solution.py:432
  64.2 13.6 %collective-permute-start.14 = (bf16[1024,256]{1,0:T(8,128)(2,1)S(1)}, bf16[1024,256]{1,0:T(8,128)(2,1)S(1)}, u32[]{:S(2)}, u32[]{:S(2)}) collective-permute-start(bf16[1024,256]{1,0:T(8,128)(2,1)S(1)} %collective-permute-done.12.refs_6_), channel_id=1, source_target_pairs={{0,2},{2,0},{8,10},{10,8},{16,18},{18,16},{24,26},{26,24},{28,30},... | collective-permute-start | bytes 1572872 | tf_op jit(solution)/shard_map/ppermute | solution.py:432
  64.3 13.6 %collective-permute-start.20 = (bf16[1024,256]{1,0:T(8,128)(2,1)S(1)}, bf16[1024,256]{1,0:T(8,128)(2,1)S(1)}, u32[]{:S(2)}, u32[]{:S(2)}) collective-permute-start(bf16[1024,256]{1,0:T(8,128)(2,1)S(1)} %collective-permute-done.16.refs_10_), channel_id=1, source_target_pairs={{0,8},{2,6},{8,16},{10,2},{16,24},{18,10},{24,28},{26,18},{28,20},... | collective-permute-start | bytes 1572872 | tf_op jit(solution)/shard_map/ppermute | solution.py:434
  65.9 13.2 %collective-permute-start.17 = (bf16[1024,256]{1,0:T(8,128)(2,1)S(1)}, bf16[1024,256]{1,0:T(8,128)(2,1)S(1)}, u32[]{:S(2)}, u32[]{:S(2)}) collective-permute-start(bf16[1024,256]{1,0:T(8,128)(2,1)S(1)} %collective-permute-done.13.refs_7_), channel_id=1, source_target_pairs={{0,8},{2,6},{8,16},{10,2},{16,24},{18,10},{24,28},{26,18},{28,20},... | collective-permute-start | bytes 1572872 | tf_op jit(solution)/shard_map/ppermute | solution.py:430
  69.3 7.9 %collective-permute-start.5 = (bf16[256,512]{1,0:T(8,128)(2,1)S(1)}, bf16[256,512]{1,0:T(8,128)(2,1)S(1)}, u32[]{:S(2)}, u32[]{:S(2)}) collective-permute-start(bf16[256,512]{1,0:T(8,128)(2,1)S(1)} %get-tuple-element.29), channel_id=1, source_target_pairs={{0,1},{1,0},{2,3},{3,2},{4,5},{5,4},{6,7},{7,6},{8,9},{9,8},{10,11... | collective-permute-start | bytes 786440 | tf_op jit(solution)/shard_map/ppermute | solution.py:448
  77.2 3.7 %collective-permute-start.11 = (bf16[1024,256]{1,0:T(8,128)(2,1)S(1)}, bf16[1024,256]{1,0:T(8,128)(2,1)S(1)}, u32[]{:S(2)}, u32[]{:S(2)}) collective-permute-start(bf16[1024,256]{1,0:T(8,128)(2,1)S(1)} %collective-permute-done.9.refs_3_), channel_id=1, source_target_pairs={{0,2},{2,0},{8,10},{10,8},{16,18},{18,16},{24,26},{26,24},{28,30},... | collective-permute-start | bytes 1572872 | tf_op jit(solution)/shard_map/ppermute | solution.py:432
  77.2 12.4 %collective-permute-start.18 = (bf16[1024,256]{1,0:T(8,128)(2,1)S(1)}, bf16[1024,256]{1,0:T(8,128)(2,1)S(1)}, u32[]{:S(2)}, u32[]{:S(2)}) collective-permute-start(bf16[1024,256]{1,0:T(8,128)(2,1)S(1)} %collective-permute-done.16.refs_10_), channel_id=1, source_target_pairs={{0,2},{2,0},{8,10},{10,8},{16,18},{18,16},{24,26},{26,24},{28,30},... | collective-permute-start | bytes 1572872 | tf_op jit(solution)/shard_map/ppermute | solution.py:432
  77.7 11.9 %collective-permute-start.15 = (bf16[1024,256]{1,0:T(8,128)(2,1)S(1)}, bf16[1024,256]{1,0:T(8,128)(2,1)S(1)}, u32[]{:S(2)}, u32[]{:S(2)}) collective-permute-start(bf16[1024,256]{1,0:T(8,128)(2,1)S(1)} %collective-permute-done.13.refs_7_), channel_id=1, source_target_pairs={{0,2},{2,0},{8,10},{10,8},{16,18},{18,16},{24,26},{26,24},{28,30},... | collective-permute-start | bytes 1572872 | tf_op jit(solution)/shard_map/ppermute | solution.py:432
  77.8 11.8 %collective-permute-start.21 = (bf16[1024,256]{1,0:T(8,128)(2,1)S(1)}, bf16[1024,256]{1,0:T(8,128)(2,1)S(1)}, u32[]{:S(2)}, u32[]{:S(2)}) collective-permute-start(bf16[1024,256]{1,0:T(8,128)(2,1)S(1)} %collective-permute-done.20.refs_14_), channel_id=1, source_target_pairs={{0,2},{2,0},{8,10},{10,8},{16,18},{18,16},{24,26},{26,24},{28,30},... | collective-permute-start | bytes 1572872 | tf_op jit(solution)/shard_map/ppermute | solution.py:435
  79.1 10.6 %collective-permute-start.19 = (bf16[1024,256]{1,0:T(8,128)(2,1)S(1)}, bf16[1024,256]{1,0:T(8,128)(2,1)S(1)}, u32[]{:S(2)}, u32[]{:S(2)}) collective-permute-start(bf16[1024,256]{1,0:T(8,128)(2,1)S(1)} %collective-permute-done.17.refs_11_), channel_id=1, source_target_pairs={{0,2},{2,0},{8,10},{10,8},{16,18},{18,16},{24,26},{26,24},{28,30},... | collective-permute-start | bytes 1572872 | tf_op jit(solution)/shard_map/ppermute | solution.py:432
  80.9 10.9 %collective-permute-start.4 = (bf16[256,512]{1,0:T(8,128)(2,1)S(1)}, bf16[256,512]{1,0:T(8,128)(2,1)S(1)}, u32[]{:S(2)}, u32[]{:S(2)}) collective-permute-start(bf16[256,512]{1,0:T(8,128)(2,1)S(1)} %get-tuple-element.28), channel_id=1, source_target_pairs={{0,1},{1,0},{2,3},{3,2},{4,5},{5,4},{6,7},{7,6},{8,9},{9,8},{10,11... | collective-permute-start | bytes 786440 | tf_op jit(solution)/shard_map/ppermute | solution.py:448
  82.5 7.2 %copy-start = (s32[256]{0:T(256)S(1)}, s32[256]{0:T(256)}, u32[]{:S(2)}) copy-start(s32[256]{0:T(256)} %constant.10.clone.table_ref) | copy-start | bytes 3076

commit v3 on v2

--- a/solution.py
+++ b/solution.py
@@ -110,7 +110,7 @@
 
 
 def call(
-    body, in_specs, out_shape, operands, flops, scratch=(), aliases=None, out_specs=None, mib=8
+    body, in_specs, out_shape, operands, flops, scratch=(), aliases=None, out_specs=None, mib=2
 ):
     spaces = {id(VMEM): pltpu.VMEM, id(HBM): pltpu.HBM}
     operands = [
@@ -144,16 +144,14 @@
     )
 
 
-def load_rows(sessions, sizes):
-    rows = sessions.shape[0]
-    offsets = np.cumsum([0] + sizes)[:-1].tolist()
-    n = len(sizes)
+def load_rows(sessions, boxes):
+    n = len(boxes)
 
     def body(x_hbm, *refs):
         outs, sem = refs[:-1], refs[-1]
         copies = []
-        for i in range(n):
-            src = x_hbm.at[:, pl.ds(offsets[i], sizes[i])]
+        for i, (r, rows, c, columns) in enumerate(boxes):
+            src = x_hbm.at[pl.ds(r, rows), pl.ds(c, columns)]
             copies.append(pltpu.make_async_copy(src, outs[i], sem.at[i]))
         for copy in copies:
             copy.start()
@@ -161,60 +159,79 @@
             copy.wait()
 
     return call(
-        body, [HBM], [pltpu.VMEM((rows, s), jnp.bfloat16) for s in sizes],
+        body, [HBM],
+        [pltpu.VMEM((rows, columns), jnp.bfloat16) for _, rows, _, columns in boxes],
         (sessions,), 0, [pltpu.SemaphoreType.DMA((n,))],
     )
 
 
-def project(parts, weight, kinds, wide):
+def project(parts, weight, kind, held, ahead):
     rows = parts[0].shape[0]
     _, depth, width = weight.shape
-    across = width // wide
-    n = len(kinds) * across
-    first = kinds[0]
+    wide = min(512, width)
+    n = width // wide
+    fetched = ([] if held is not None else [kind]) + ([] if ahead is None else [ahead])
 
     def body(*refs):
-        x_refs, (w_hbm, o_ref, buf, sem) = refs[:len(parts)], refs[len(parts):]
-
-        def load(s):
-            src = w_hbm.at[first + s // across, :, pl.ds(s % across * wide, wide)]
-            return pltpu.make_async_copy(src, buf.at[s], sem.at[s])
-
-        for s in range(n):
-            load(s).start()
+        x_refs, w_hbm = refs[:len(parts)], refs[len(parts)]
+        bufs = refs[-1 - len(fetched):-1] if fetched else ()
+        sem = refs[-1]
+        o_ref = refs[len(parts) + 1 + (held is not None)]
+        w_ref = refs[len(parts) + 1] if held is not None else bufs[0]
+
+        def load(i, s):
+            src = w_hbm.at[fetched[i], :, pl.ds(s * wide, wide)]
+            return pltpu.make_async_copy(src, bufs[i].at[s], sem.at[i, s])
+
+        for i in range(len(fetched)):
+            for s in range(n):
+                load(i, s).start()
 
         @pl.loop(0, n)
         def _(s):
-            pltpu.make_async_copy(w_hbm.at[0, :, pl.ds(0, wide)], buf.at[s], sem.at[s]).wait()
+            if held is None:
+                pltpu.make_async_copy(w_hbm.at[0, :, pl.ds(0, wide)], w_ref.at[s], sem.at[0, s]).wait()
             at, total = 0, None
             for x_ref in x_refs:
                 d = x_ref.shape[1]
-                term = dot32(x_ref[...], buf[s, at:at + d, :])
+                term = dot32(x_ref[...], w_ref[s, at:at + d, :])
                 total = term if total is None else total + term
                 at += d
-            cols = pl.ds(pl.multiple_of(lax.rem(s, across) * wide, wide), wide)
-            o_ref[s // across, :, cols] = total.astype(jnp.bfloat16)
-
-    return call(
-        body, [VMEM] * len(parts) + [HBM],
-        [
-            pltpu.VMEM((len(kinds), rows, width), jnp.bfloat16),
-            pltpu.VMEM((n, depth, wide), jnp.bfloat16),
-        ],
-        (*parts, weight), 2 * rows * depth * len(kinds) * width,
-        [pltpu.SemaphoreType.DMA((n,))],
-    )
-
-
-def project_part(x, weights, offset, total):
+            cols = pl.ds(pl.multiple_of(s * wide, wide), wide)
+            o_ref[0, :, cols] = total.astype(jnp.bfloat16)
+
+        if ahead is not None:
+            for s in range(n):
+                load(len(fetched) - 1, s).wait()
+
+    operands = (*parts, weight) + (() if held is None else (held,))
+    result, *weights = call(
+        body, [VMEM] * len(parts) + [HBM] + [VMEM] * (held is not None),
+        [pltpu.VMEM((1, rows, width), jnp.bfloat16)]
+        + [pltpu.VMEM((n, depth, wide), jnp.bfloat16)] * len(fetched),
+        operands, 2 * rows * depth * width,
+        [pltpu.SemaphoreType.DMA((max(1, len(fetched)), n))],
+    )
+    return result, weights
+
+
+def project_part(x, weights, offset, total, fetched):
     rows, depth = x.shape
     blocks = sum(w.shape[0] for w in weights)
     wide = weights[0].shape[2]
     across = blocks // 3
 
     def body(x_ref, *refs):
-        w_refs, o_ref = refs[:len(weights)], refs[-1]
+        w_refs, o_ref = refs[:len(weights)], refs[n_in - 1]
         base = 0
+
+        def load(s):
+            src = refs[n_in - 2].at[:, pl.ds(s * step, step)]
+            return pltpu.make_async_copy(src, refs[n_in].at[s], refs[-1].at[s])
+
+        if fetched is not None:
+            for s in range(n_blocks):
+                load(s).start()
         for w_ref in w_refs:
             n = w_ref.shape[0]
 
@@ -229,12 +246,25 @@
 
             base += n
 
+        if fetched is not None:
+            for s in range(n_blocks):
+                load(s).wait()
+
     operands = (x, *weights) + (() if total is None else (total,))
-    return call(
-        body, [VMEM] * len(operands),
-        pltpu.VMEM((3, rows, across * wide), jnp.float32), operands,
-        2 * rows * depth * blocks * wide,
-        aliases={} if total is None else {len(operands) - 1: 0},
+    specs = [VMEM] * len(operands)
+    aliases = {} if total is None else {len(operands) - 1: 0}
+    shapes, scratch = [pltpu.VMEM((3, rows, across * wide), jnp.float32)], []
+    if fetched is not None:
+        step = min(512, fetched.shape[1])
+        n_blocks = fetched.shape[1] // step
+        operands += (fetched,)
+        specs.append(HBM)
+        shapes.append(pltpu.VMEM((n_blocks, fetched.shape[0], step), jnp.bfloat16))
+        scratch.append(pltpu.SemaphoreType.DMA((n_blocks,)))
+    n_in = len(operands)
+    return call(
+        body, specs, shapes, operands, 2 * rows * depth * blocks * wide, scratch,
+        aliases=aliases,
     )
 
 
@@ -256,129 +286,188 @@
     return call(body, [SMEM, SMEM], pltpu.VMEM((4, rows, rows), jnp.float32), (place, counts), 0)
 
 
-def head_out(q, keys, values, masks):
+def softmax_parts(q, keys, values, masks):
     scores = [scores_of(q, k) * (HD ** (-0.5) * LOG2E) + b for k, b in zip(keys, masks)]
     top = functools.reduce(jnp.maximum, [jnp.max(s, axis=1, keepdims=True) for s in scores])
     raised = [jnp.exp2(s - top) for s in scores]
     total = sum(jnp.sum(p, axis=1, keepdims=True) for p in raised)
     out = sum(dot32(p.astype(jnp.bfloat16), v) for p, v in zip(raised, values))
+    return top, total, out
+
+
+def head_out(q, keys, values, masks):
+    _, total, out = softmax_parts(q, keys, values, masks)
     return (out / total).astype(jnp.bfloat16)
 
 
-def finish(x, weights, offset, total, own_k, own_v, bias, g):
-    rows, depth = x.shape
+def finish(place, x, weights, offset, total, own_k, own_v, bias, kv, r, splits):
+    part_rows, depth = x.shape
+    _, rows, width = total.shape
     wide = weights[0].shape[2]
-    across = total.shape[2] // wide
-    cols = slice(g * wide, (g + 1) * wide)
-    where = [(i, s) for i, w in enumerate(weights) for s in range(w.shape[0])]
-
-    def body(x_ref, *refs):
+    across = width // wide
+    here = slice(r * part_rows, (r + 1) * part_rows)
+    known = slice(0, (r + 1) * part_rows)
+
+    def body(place_ref, x_ref, *refs):
         w_refs = refs[:len(weights)]
-        t_ref, k_ref, v_ref, bias_ref, mixed_ref, kv_ref = refs[len(weights):]
-        packed = []
-        for c in range(3):
-            i, s = where[c * across + g]
-            part = dot32(x_ref[...], w_refs[i][s, offset:offset + depth, :])
-            packed.append((t_ref[c, :, cols] + part).astype(jnp.bfloat16))
-        q, k, v = packed
-        kv_ref[0] = k
-        kv_ref[1] = v
-        for h in range(wide // HD):
-            at = slice(h * HD, (h + 1) * HD)
-            there = slice(g * wide + h * HD, g * wide + (h + 1) * HD)
-            mixed_ref[:, at] = head_out(
-                q[:, at], (k[:, at], k_ref[0, :, there]), (v[:, at], v_ref[0, :, there]),
-                (bias_ref[3], bias_ref[2]),
-            )
-
-    operands = (x, *weights, total, own_k, own_v, bias)
-    return call(
-        body, [VMEM] * len(operands),
-        [pltpu.VMEM((rows, wide), jnp.bfloat16), pltpu.VMEM((2, rows, wide), jnp.bfloat16)],
-        operands, 6 * rows * depth * wide + 8 * rows * rows * wide,
-    )
-
-
-def own_out(own_q, own_k, own_v, kvs, bias, weight):
+        t_ref, k_ref, v_ref, bias_ref = refs[len(weights):len(weights) + 4]
+        mixed_refs, kv_ref, q_ref = refs[-2 - splits:-2], refs[-2], refs[-1]
+
+        for c, w_ref in enumerate(w_refs):
+            for g in range(across):
+                cols = slice(g * wide, (g + 1) * wide)
+                part = dot32(x_ref[...], w_ref[g, offset:offset + depth, :])
+                part = (t_ref[c, here, cols] + part).astype(jnp.bfloat16)
+                if c == 0:
+                    q_ref[:, cols] = part
+                else:
+                    kv_ref[c - 1, here, cols] = part
+
+        def heads(with_own):
+            for h in range(width // HD):
+                at = slice(h * HD, (h + 1) * HD)
+                keys, values = [kv_ref[0, known, at]], [kv_ref[1, known, at]]
+                masks = [bias_ref[3, here, known]]
+                if with_own:
+                    keys.append(k_ref[0, :, at])
+                    values.append(v_ref[0, :, at])
+                    masks.append(bias_ref[2, here, :])
+                where = slice(h * HD % piece, h * HD % piece + HD)
+                mixed_refs[h * HD // piece][:, where] = head_out(q_ref[:, at], keys, values, masks)
+
+        pl.when(place_ref[0] == 0)(lambda: heads(True))
+        pl.when(place_ref[0] != 0)(lambda: heads(False))
+
+    piece = width // splits
+    operands = (place, x, *weights, total, own_k, own_v, bias)
+    aliases = {}
+    if kv is not None:
+        aliases = {len(operands): splits}
+        operands += (kv,)
+    specs = [SMEM] + [VMEM] * (len(operands) - 1)
+    shapes = [pltpu.VMEM((part_rows, piece), jnp.bfloat16)] * splits
+    shapes.append(pltpu.VMEM((2, rows, width), jnp.bfloat16))
+    return call(
+        body, specs, shapes, operands,
+        6 * part_rows * depth * width + 8 * part_rows * rows * width,
+        [pltpu.VMEM((part_rows, width), jnp.bfloat16)],
+        aliases=aliases,
+    )
+
+
+def own_start(own_q, own_k, own_v, bias):
     _, rows, width = own_q.shape
-    model = weight.shape[1]
-    wide = kvs[0].shape[2]
-    step = min(512, model)
-    n = model // step
-
-    def body(q_ref, k_ref, v_ref, *refs):
-        kv_refs = refs[:len(kvs)]
-        bias_ref, w_hbm, o_ref, buf, mixed, sem = refs[len(kvs):]
-
-        def load(s):
-            return pltpu.make_async_copy(w_hbm.at[:, pl.ds(s * step, step)], buf.at[s], sem.at[s])
-
-        for s in range(n):
-            load(s).start()
+
+    def body(q_ref, k_ref, v_ref, bias_ref, o_ref):
         for h in range(width // HD):
             at = slice(h * HD, (h + 1) * HD)
-            kv_ref, here = kv_refs[h * HD // wide], slice(h * HD % wide, h * HD % wide + HD)
-            mixed[:, at] = head_out(
-                q_ref[0, :, at], (k_ref[0, :, at], kv_ref[0, :, here]),
-                (v_ref[0, :, at], kv_ref[1, :, here]), (bias_ref[0], bias_ref[1]),
+            o_ref[:, at] = head_out(
+                q_ref[0, :, at], [k_ref[0, :, at]], [v_ref[0, :, at]], [bias_ref[0]]
             )
+
+    return call(
+        body, [VMEM] * 4, pltpu.VMEM((rows, width), jnp.bfloat16),
+        (own_q, own_k, own_v, bias), 4 * rows * rows * width,
+    )
+
+
+def rest_heads(place_ref, q_ref, k_ref, v_ref, alone_ref, kv_ref, bias_ref, out_ref, heads):
+    first = heads[0] * HD
+    there = slice(first, (heads[-1] + 1) * HD)
+
+    @pl.when(place_ref[0] == 0)
+    def _():
+        out_ref[...] = alone_ref[:, there]
+
+    @pl.when(place_ref[0] != 0)
+    def _():
+        for h in heads:
+            at = slice(h * HD, (h + 1) * HD)
+            out_ref[:, h * HD - first:(h + 1) * HD - first] = head_out(
+                q_ref[0, :, at], (k_ref[0, :, at], kv_ref[0, :, at]),
+                (v_ref[0, :, at], kv_ref[1, :, at]), (bias_ref[0], bias_ref[1]),
+            )
+
+
+def own_rest(place, own_q, own_k, own_v, alone, kv, bias):
+    _, rows, width = own_q.shape
+    heads = range(width // HD // 2)
+
+    def body(*refs):
+        rest_heads(*refs, heads)
+
+    return call(
+        body, [SMEM] + [VMEM] * 6, pltpu.VMEM((rows, width // 2), jnp.bfloat16),
+        (place, own_q, own_k, own_v, alone, kv, bias), 2 * rows * rows * width, mib=4,
+    )
+
+
+def own_out(place, own_q, own_k, own_v, alone, kv, bias, half, weight):
+    rows, depth = alone.shape
+    n, _, step = weight.shape
+    heads = range(depth // HD // 2, depth // HD)
+    cut = depth // 2
+
+    def body(*refs):
+        half_ref, w_ref, o_ref, rest = refs[7:]
+        rest_heads(*refs[:7], rest, heads)
 
         @pl.loop(0, n)
         def _(s):
-            pltpu.make_async_copy(w_hbm.at[:, pl.ds(0, step)], buf.at[s], sem.at[s]).wait()
-            cols = pl.ds(pl.multiple_of(s * step, step), step)
-            o_ref[:, cols] = dot32(mixed[...], buf[s])
-
-    return call(
-        body, [VMEM] * (3 + len(kvs)) + [VMEM, HBM],
-        pltpu.VMEM((rows, model), jnp.float32), (own_q, own_k, own_v, *kvs, bias, weight),
-        2 * rows * width * model + 8 * rows * rows * width,
-        [
-            pltpu.VMEM((n, width, step), jnp.bfloat16),
-            pltpu.VMEM((rows, width), jnp.bfloat16),
-            pltpu.SemaphoreType.DMA((n,)),
-        ],
-        mib=6 + (2 * width * model >> 20),
-    )
-
-
-def other_out(user, table, mixed, row_offset, pieces, total, last):
-    rows, depth = mixed.shape
-    model = total.shape[1]
+            part = dot32(half_ref[...], w_ref[s, :cut, :]) + dot32(rest[...], w_ref[s, cut:, :])
+            o_ref[:, pl.ds(pl.multiple_of(s * step, step), step)] = part
+
+    return call(
+        body, [SMEM] + [VMEM] * 8, pltpu.VMEM((rows, n * step), jnp.float32),
+        (place, own_q, own_k, own_v, alone, kv, bias, half, weight), 2 * rows * depth * n * step,
+        [pltpu.VMEM((rows, depth // 2), jnp.bfloat16)],
+        mib=5,
+    )
+
+
+def other_out(user, table, mixed, first, pieces, total, r, out, last):
+    part_rows, depth = mixed.shape
+    rows, model = total.shape
     wide = pieces[0].shape[-1]
     n = len(pieces)
+    here = slice(r * part_rows, (r + 1) * part_rows)
 
     def body(user_ref, table_ref, mixed_ref, total_ref, *refs):
-        piece_refs, o_ref = refs[:len(pieces)], refs[len(pieces)]
+        piece_refs = refs[:n]
 
         def columns(s):
             return pl.ds(pl.multiple_of(table_ref[user_ref[0] * n + s] * wide, wide), wide)
 
-        if last:
-            buf, sem = refs[len(pieces) + 1:]
-
-            def store(s):
-                return pltpu.make_async_copy(buf.at[s], o_ref.at[:, columns(s)], sem.at[s])
+        def store(s):
+            o_ref, buf, sem = refs[-3:]
+            dst = o_ref.at[pl.ds(r * part_rows, part_rows), columns(s)]
+            return pltpu.make_async_copy(buf.at[s], dst, sem.at[s])
 
         for s in range(n):
-            part = dot32(mixed_ref[...], piece_refs[s][row_offset:row_offset + depth, :])
-            part = total_ref[:, columns(s)] + part
+            part = dot32(mixed_ref[...], piece_refs[s][first:first + depth, :])
+            part = total_ref[here, columns(s)] + part
             if last:
-                buf[s] = part.astype(jnp.bfloat16)
+                refs[-2][s] = part.astype(jnp.bfloat16)
                 store(s).start()
             else:
-                o_ref[:, columns(s)] = part
+                refs[-1][here, columns(s)] = part
         if last:
             for s in range(n):
                 store(s).wait()
 
-    operands = (user, table, mixed, total, *pieces)
-    return call(
-        body, [SMEM, SMEM] + [VMEM] * (2 + len(pieces)),
-        jax.ShapeDtypeStruct((rows, model), jnp.bfloat16) if last else pltpu.VMEM((rows, model), jnp.float32),
-        operands, 2 * rows * depth * model,
-        [pltpu.VMEM((n, rows, wide), jnp.bfloat16), pltpu.SemaphoreType.DMA((n,))] if last else (),
-        aliases={} if last else {3: 0},
+    operands = (user, table, mixed, total, *pieces) + (() if out is None else (out,))
+    if last:
+        aliases = {} if out is None else {len(operands) - 1: 0}
+    else:
+        aliases = {3: 0}
+    return call(
+        body,
+        [SMEM, SMEM] + [VMEM] * (2 + n) + [HBM] * (out is not None),
+        jax.ShapeDtypeStruct((rows, model), jnp.bfloat16) if last
+        else pltpu.VMEM((rows, model), jnp.float32),
+        operands, 2 * part_rows * depth * model,
+        [pltpu.VMEM((n, part_rows, wide), jnp.bfloat16), pltpu.SemaphoreType.DMA((n,))] if last else (),
+        aliases=aliases,
         out_specs=HBM if last else VMEM,
     )
 
@@ -387,8 +476,6 @@
     users = 2 * len(ring)
     chips = len(ring)
     rows, model = sessions.shape
-    width = input_weight.shape[2]
-    wide = min(512, width)
     place = lax.axis_index("heads").astype(jnp.int32)[None]
     user = lax.axis_index("users").astype(jnp.int32)[None]
 
@@ -415,13 +502,17 @@
             table[ring[i][core]] = [ring[a][b] for a, b in held]
     table = jnp.asarray(table.reshape(-1))
 
-    sizes = [model // 2, model // 4, model // 8, model // 8]
+    sizes = [model // 2, model // 4, model // 4]
     offsets = np.cumsum([0] + sizes)[:-1].tolist()
+    block = rows // 2
     piece = load_piece(user, place, output_weight, model // users)
-    parts = load_rows(sessions, sizes)
+    boxes = [(0, rows, o, s) for o, s in zip(offsets, sizes)]
+    boxes += [(r * block, block, offsets[-1], sizes[-1]) for r in range(2)]
+    loaded = load_rows(sessions, boxes)
+    parts, sent = loaded[:3], [*loaded[:2], *loaded[3:]]
 
     crossed = lax.ppermute(piece, "heads", across)
-    guests = [lax.ppermute(x, "heads", across) for x in parts]
+    guests = [lax.ppermute(x, "heads", across) for x in sent]
 
     near, far = crossed, lax.ppermute(crossed, "users", beside)
     pieces = [near, far]
@@ -434,23 +525,24 @@
         near = lax.ppermute(near, "users", around)
         pieces += [near, lax.ppermute(near, "users", beside)]
 
-    own_q, w_q = project(parts, input_weight, (0,), wide)
-    own_k, w_k = project(parts, input_weight, (1,), wide)
-    own_v, w_v = project(parts, input_weight, (2,), wide)
+    own_q, (w_q, w_k) = project(parts, input_weight, 0, None, 1)
+    own_k, (w_v,) = project(parts, input_weight, 1, w_k, 2)
+    own_v, _ = project(parts, input_weight, 2, w_v, None)
     weights = (w_q, w_k, w_v)
     bias = biases(place, session_counts, rows)
-    total = None
-    for i in range(len(sizes) - 1):
-        total = project_part(guests[i], weights, offsets[i], total)
-    mixed_far, kvs = [], []
-    for g in range(width // wide):
-        mixed, kv = finish(guests[-1], weights, offsets[-1], total, own_k, own_v, bias, g)
-        mixed_far.append(lax.ppermute(mixed, "heads", across))
-        kvs.append(kv)
-    out = own_out(own_q, own_k, own_v, kvs, bias, output_weight)
-    for g, mixed in enumerate(mixed_far):
-        out = other_out(user, table, mixed, g * wide, pieces, out, g == len(mixed_far) - 1)
-    return out
+    total, = project_part(guests[0], weights, offsets[0], None, None)
+    total, own_weight = project_part(guests[1], weights, offsets[1], total, output_weight)
+    alone = own_start(own_q, own_k, own_v, bias)
+    first, kv = finish(
+        place, guests[2], weights, offsets[-1], total, own_k, own_v, bias, None, 0, 1
+    )
+    first = lax.ppermute(first, "heads", across)
+    second, kv = finish(place, guests[3], weights, offsets[-1], total, own_k, own_v, bias, kv, 1, 1)
+    second = lax.ppermute(second, "heads", across)
+    half_mixed = own_rest(place, own_q, own_k, own_v, alone, kv, bias)
+    total = own_out(place, own_q, own_k, own_v, alone, kv, bias, half_mixed, own_weight)
+    out = other_out(user, table, first, 0, pieces, total, 0, None, True)
+    return other_out(user, table, second, 0, pieces, total, 1, out, True)
 
 
 def solution(mesh):

time: 94.8 us -> 98.1 us (1.035)
  local copies, waits for them, and re-layouts: 0.01 us -> 6.65 us
  waiting for transfers between devices: 28.6 us -> 26.7 us
  Pallas kernels: 41.7 us -> 40.2 us
    unnamed x4 -> x8, local copies, waits for them, and re-layouts: 0.01 us -> 6.65 us
    ppermute x6, waiting for transfers between devices: 13.6 us -> 9.96 us  [the longest x1 5.35 us: two_halves(): first = lax.ppermute(first, 'heads', across)]
    ppermute x4, waiting for transfers between devices: 2.23 us -> 4.09 us  [two_halves(): near = lax.ppermute(near, 'users', around)]
    pallas_call x14 -> x15, Pallas kernels: 41.7 us -> 40.2 us  [call(): pl.pallas_call(body, in_specs=in_specs, out_specs=out_specs if out_specs...]
  transfers between devices with their start and end apart: 22 -> 22, of which waited for: 7 -> 5; matrix products, arithmetic and copies ran while one was open for 0% -> 0% of each run, Pallas kernels for 40% -> 37%
where the time goes in v3:
time: 98.1 us; the launch traced here: 97.8 us
  Pallas kernels  40.2 us (41%)
  waiting for transfers between devices  26.7 us (27%)
  starting transfers between devices  24 us (24%)
  local copies, waits for them, and re-layouts  6.65 us (7%)
    pallas_call x15, Pallas kernels, call(): pl.pallas_call(body, in_specs=in_specs, out_specs=out_specs if out_specs...  40.2 us
    ppermute x1, waiting for transfers between devices, two_halves(): crossed = lax.ppermute(piece, 'heads', across)  11.9 us
    ppermute x4, starting transfers between devices, two_halves(): near = lax.ppermute(near, 'users', around)  6.86 us
    unnamed x8, local copies, waits for them, and re-layouts  6.65 us
    ppermute x1, waiting for transfers between devices, two_halves(): first = lax.ppermute(first, 'heads', across)  5.35 us
    ppermute x4, starting transfers between devices, two_halves(): guests = [lax.ppermute(x, 'heads', across) for x in sent]  5.14 us
    ppermute x3, starting transfers between devices, two_halves(): far = lax.ppermute(far, 'users', around)  4.67 us
    ppermute x4, waiting for transfers between devices, two_halves(): guests = [lax.ppermute(x, 'heads', across) for x in sent]  4.6 us
  transfers between devices with their start and end apart: 22, of which 5 were waited for; matrix products, arithmetic and copies ran while one was open for 0% of the time, Pallas kernels for 37%

profile of v3, /device:TPU:0, one launch (start us, length us, event | category | flops | bytes accessed | tf_op | source)
XLA Modules:
  0.0 97.8 jit_solution(14911795223309600069)
XLA Ops:
  0.0 1.0 %shard_map.67 = bf16[1024,256]{1,0:T(8,128)(2,1)S(1)} custom-call(s32[1]{0:T(128)} %bitcast.user_ref, s32[1]{0:T(128)} %bitcast.1.place_ref.refs_0_, bf16[1024,4096]{1,0:T(8,128)(2,1)} %w_hbm.1), custom_call_target="tpu_custom_call" | custom-call | bytes 1048576 | tf_op jit(solution)/shard_map/pallas_call | solution.py:120
  1.1 3.0 %collective-permute-start.5 = (bf16[1024,256]{1,0:T(8,128)(2,1)S(1)}, bf16[1024,256]{1,0:T(8,128)(2,1)S(1)}, u32[]{:S(2)}, u32[]{:S(2)}) collective-permute-start(bf16[1024,256]{1,0:T(8,128)(2,1)S(1)} %shard_map.67), channel_id=1, source_target_pairs={{0,1},{1,0},{2,3},{3,2},{4,5},{5,4},{6,7},{7,6},{8,9},{9,8},{10,11... | collective-permute-start | bytes 1572872 | tf_op jit(solution)/shard_map/ppermute | solution.py:514
  4.1 11.9 %collective-permute-done.5.refs_0_ = bf16[1024,256]{1,0:T(8,128)(2,1)S(1)} collective-permute-done((bf16[1024,256]{1,0:T(8,128)(2,1)S(1)}, bf16[1024,256]{1,0:T(8,128)(2,1)S(1)}, u32[]{:S(2)}, u32[]{:S(2)}) %collective-permute-start.5) | collective-permute-done | bytes 524320 | tf_op jit(solution)/shard_map/ppermute | solution.py:514
  16.0 1.8 %collective-permute-start.7 = (bf16[1024,256]{1,0:T(8,128)(2,1)S(1)}, bf16[1024,256]{1,0:T(8,128)(2,1)S(1)}, u32[]{:S(2)}, u32[]{:S(2)}) collective-permute-start(bf16[1024,256]{1,0:T(8,128)(2,1)S(1)} %collective-permute-done.5.refs_0_), channel_id=1, source_target_pairs={{0,8},{2,6},{8,16},{10,2},{16,24},{18,10},{24,28},{26,18},{28,20},... | collective-permute-start | bytes 1572872 | tf_op jit(solution)/shard_map/ppermute | solution.py:520
  17.8 1.7 %shard_map.55 = (bf16[256,2048]{1,0:T(8,128)(2,1)S(1)}, bf16[256,1024]{1,0:T(8,128)(2,1)S(1)}, bf16[256,1024]{1,0:T(8,128)(2,1)S(1)}, bf16[128,1024]{1,0:T(8,128)(2,1)S(1)}, bf16[128,1024]{1,0:T(8,128)(2,1)S(1)}) custom-call(bf16[256,4096]{1,0:T(8,128)(2,1)} %x_hbm.1), custom_call_target="tpu_custom_call" | custom-call | bytes 1048576 | tf_op jit(solution)/shard_map/pallas_call | solution.py:120
  19.6 1.6 %collective-permute-start.2 = (bf16[256,2048]{1,0:T(8,128)(2,1)S(1)}, bf16[256,2048]{1,0:T(8,128)(2,1)S(1)}, u32[]{:S(2)}, u32[]{:S(2)}) collective-permute-start(bf16[256,2048]{1,0:T(8,128)(2,1)S(1)} %get-tuple-element.22.refs_0_), channel_id=1, source_target_pairs={{0,1},{1,0},{2,3},{3,2},{4,5},{5,4},{6,7},{7,6},{8,9},{9,8},{10,11... | collective-permute-start | bytes 3145736 | tf_op jit(solution)/shard_map/ppermute | solution.py:515
  21.1 4.1 %collective-permute-done.7.refs_2_ = bf16[1024,256]{1,0:T(8,128)(2,1)S(1)} collective-permute-done((bf16[1024,256]{1,0:T(8,128)(2,1)S(1)}, bf16[1024,256]{1,0:T(8,128)(2,1)S(1)}, u32[]{:S(2)}, u32[]{:S(2)}) %collective-permute-start.7) | collective-permute-done | bytes 524320 | tf_op jit(solution)/shard_map/ppermute | solution.py:520
  25.2 1.8 %collective-permute-start.11 = (bf16[1024,256]{1,0:T(8,128)(2,1)S(1)}, bf16[1024,256]{1,0:T(8,128)(2,1)S(1)}, u32[]{:S(2)}, u32[]{:S(2)}) collective-permute-start(bf16[1024,256]{1,0:T(8,128)(2,1)S(1)} %collective-permute-done.7.refs_2_), channel_id=1, source_target_pairs={{0,8},{2,6},{8,16},{10,2},{16,24},{18,10},{24,28},{26,18},{28,20},... | collective-permute-start | bytes 1572872 | tf_op jit(solution)/shard_map/ppermute | solution.py:520
  27.0 1.6 %collective-permute-start.8 = (bf16[1024,256]{1,0:T(8,128)(2,1)S(1)}, bf16[1024,256]{1,0:T(8,128)(2,1)S(1)}, u32[]{:S(2)}, u32[]{:S(2)}) collective-permute-start(bf16[1024,256]{1,0:T(8,128)(2,1)S(1)} %collective-permute-done.6.refs_1_), channel_id=1, source_target_pairs={{0,8},{2,6},{8,16},{10,2},{16,24},{18,10},{24,28},{26,18},{28,20},... | collective-permute-start | bytes 1572872 | tf_op jit(solution)/shard_map/ppermute | solution.py:521
  28.6 1.5 %collective-permute-start.1 = (bf16[256,1024]{1,0:T(8,128)(2,1)S(1)}, bf16[256,1024]{1,0:T(8,128)(2,1)S(1)}, u32[]{:S(2)}, u32[]{:S(2)}) collective-permute-start(bf16[256,1024]{1,0:T(8,128)(2,1)S(1)} %get-tuple-element.23.refs_1_), channel_id=1, source_target_pairs={{0,1},{1,0},{2,3},{3,2},{4,5},{5,4},{6,7},{7,6},{8,9},{9,8},{10,11... | collective-permute-start | bytes 1572872 | tf_op jit(solution)/shard_map/ppermute | solution.py:515
  30.6 5.9 %shard_map.56 = (bf16[1,256,1024]{2,1,0:T(8,128)(2,1)S(1)}, bf16[2,4096,512]{2,1,0:T(8,128)(2,1)S(1)}, bf16[2,4096,512]{2,1,0:T(8,128)(2,1)S(1)}) custom-call(bf16[256,2048]{1,0:T(8,128)(2,1)S(1)} %get-tuple-element.22.refs_0_, bf16[256,1024]{1,0:T(8,128)(2,1)S(1)} %get-tuple-element.23.refs_1_, bf16[256,1024]{1,0:T(8,128)(2,1)S(1)} %get-tuple-element.24.refs_2_, ...), custom_call_target="tpu_custom_call" | custom-call | flops 2147483648 | bytes 1048576 | tf_op jit(solution)/shard_map/pallas_call | solution.py:120
  36.5 3.5 %shard_map.57 = (bf16[1,256,1024]{2,1,0:T(8,128)(2,1)S(1)}, bf16[2,4096,512]{2,1,0:T(8,128)(2,1)S(1)}) custom-call(bf16[256,2048]{1,0:T(8,128)(2,1)S(1)} %get-tuple-element.22.refs_0_, bf16[256,1024]{1,0:T(8,128)(2,1)S(1)} %get-tuple-element.23.refs_1_, bf16[256,1024]{1,0:T(8,128)(2,1)S(1)} %get-tuple-element.24.refs_2_, bf16[3,4096,1024]{2,1,0:T(8,128)(2,1)} %refs_3_.5, ...), custom_call_target="tpu_custom_call" | custom-call | flops 2147483648 | bytes 1048576 | tf_op jit(solution)/shard_map/pallas_call | solution.py:120
  40.0 1.6 %collective-permute-start.15 = (bf16[1024,256]{1,0:T(8,128)(2,1)S(1)}, bf16[1024,256]{1,0:T(8,128)(2,1)S(1)}, u32[]{:S(2)}, u32[]{:S(2)}) collective-permute-start(bf16[1024,256]{1,0:T(8,128)(2,1)S(1)} %collective-permute-done.11.refs_6_), channel_id=1, source_target_pairs={{0,8},{2,6},{8,16},{10,2},{16,24},{18,10},{24,28},{26,18},{28,20},... | collective-permute-start | bytes 1572872 | tf_op jit(solution)/shard_map/ppermute | solution.py:520
  41.7 1.5 %collective-permute-start.12 = (bf16[1024,256]{1,0:T(8,128)(2,1)S(1)}, bf16[1024,256]{1,0:T(8,128)(2,1)S(1)}, u32[]{:S(2)}, u32[]{:S(2)}) collective-permute-start(bf16[1024,256]{1,0:T(8,128)(2,1)S(1)} %collective-permute-done.8.refs_3_), channel_id=1, source_target_pairs={{0,8},{2,6},{8,16},{10,2},{16,24},{18,10},{24,28},{26,18},{28,20},... | collective-permute-start | bytes 1572872 | tf_op jit(solution)/shard_map/ppermute | solution.py:521
  43.2 2.5 %shard_map.60.refs_5_.v_ref.refs_3_ = bf16[1,256,1024]{2,1,0:T(8,128)(2,1)S(1)} custom-call(bf16[256,2048]{1,0:T(8,128)(2,1)S(1)} %get-tuple-element.22.refs_0_, bf16[256,1024]{1,0:T(8,128)(2,1)S(1)} %get-tuple-element.23.refs_1_, bf16[256,1024]{1,0:T(8,128)(2,1)S(1)} %get-tuple-element.24.refs_2_, bf16[3,4096,1024]{2,1,0:T(8,128)(2,1)} %refs_3_.5, ...), custom_call_target="tpu_custom_call" | custom-call | flops 2147483648 | bytes 1048576 | tf_op jit(solution)/shard_map/pallas_call | solution.py:120
  46.5 1.6 %collective-permute-start = (bf16[128,1024]{1,0:T(8,128)(2,1)S(1)}, bf16[128,1024]{1,0:T(8,128)(2,1)S(1)}, u32[]{:S(2)}, u32[]{:S(2)}) collective-permute-start(bf16[128,1024]{1,0:T(8,128)(2,1)S(1)} %get-tuple-element.21), channel_id=1, source_target_pairs={{0,1},{1,0},{2,3},{3,2},{4,5},{5,4},{6,7},{7,6},{8,9},{9,8},{10,11... | collective-permute-start | bytes 786440 | tf_op jit(solution)/shard_map/ppermute | solution.py:515
  48.1 4.2 %shard_map.58.refs_3_ = f32[3,256,1024]{2,1,0:T(8,128)S(1)} custom-call(bf16[256,2048]{1,0:T(8,128)(2,1)S(1)} %collective-permute-done.2.x_ref, bf16[2,4096,512]{2,1,0:T(8,128)(2,1)S(1)} %get-tuple-element.25.refs_0_, bf16[2,4096,512]{2,1,0:T(8,128)(2,1)S(1)} %get-tuple-element.26.refs_4_.refs_1_, bf16[2,4096,512]{2,1,0:T(8,128)(2,1)S(1)} %get-tuple-element.27.refs_2_.refs_4_), custom_call_target="tpu_custom_call" | custom-call | flops 3221225472 | bytes 1048576 | tf_op jit(solution)/shard_map/pallas_call | solution.py:120
  52.3 4.6 %collective-permute-done.1.x_ref = bf16[256,1024]{1,0:T(8,128)(2,1)S(1)} collective-permute-done((bf16[256,1024]{1,0:T(8,128)(2,1)S(1)}, bf16[256,1024]{1,0:T(8,128)(2,1)S(1)}, u32[]{:S(2)}, u32[]{:S(2)}) %collective-permute-start.1) | collective-permute-done | bytes 524320 | tf_op jit(solution)/shard_map/ppermute | solution.py:515
  56.9 3.5 %shard_map.59 = (f32[3,256,1024]{2,1,0:T(8,128)S(1)}, bf16[8,1024,512]{2,1,0:T(8,128)(2,1)S(1)}) custom-call(bf16[256,1024]{1,0:T(8,128)(2,1)S(1)} %collective-permute-done.1.x_ref, bf16[2,4096,512]{2,1,0:T(8,128)(2,1)S(1)} %get-tuple-element.25.refs_0_, ...), custom_call_target="tpu_custom_call", output_to_operand_aliasing={{0}: (4, {})} | custom-call | flops 1610612736 | bytes 1048576 | tf_op jit(solution)/shard_map/pallas_call | solution.py:120
  60.4 3.3 %copy-done = bf16[8,1024,512]{2,1,0:T(8,128)(2,1)} copy-done((bf16[8,1024,512]{2,1,0:T(8,128)(2,1)}, bf16[8,1024,512]{2,1,0:T(8,128)(2,1)S(1)}, u32[]{:S(2)}) %copy-start) | copy-done | bytes 8388632
  64.2 1.6 %collective-permute-start.19 = (bf16[1024,256]{1,0:T(8,128)(2,1)S(1)}, bf16[1024,256]{1,0:T(8,128)(2,1)S(1)}, u32[]{:S(2)}, u32[]{:S(2)}) collective-permute-start(bf16[1024,256]{1,0:T(8,128)(2,1)S(1)} %collective-permute-done.15.refs_10_), channel_id=1, source_target_pairs={{0,8},{2,6},{8,16},{10,2},{16,24},{18,10},{24,28},{26,18},{28,20},... | collective-permute-start | bytes 1572872 | tf_op jit(solution)/shard_map/ppermute | solution.py:525
  65.8 1.6 %collective-permute-start.16 = (bf16[1024,256]{1,0:T(8,128)(2,1)S(1)}, bf16[1024,256]{1,0:T(8,128)(2,1)S(1)}, u32[]{:S(2)}, u32[]{:S(2)}) collective-permute-start(bf16[1024,256]{1,0:T(8,128)(2,1)S(1)} %collective-permute-done.12.refs_7_), channel_id=1, source_target_pairs={{0,8},{2,6},{8,16},{10,2},{16,24},{18,10},{24,28},{26,18},{28,20},... | collective-permute-start | bytes 1572872 | tf_op jit(solution)/shard_map/ppermute | solution.py:521
  67.4 3.3 %shard_map.62 = (bf16[128,1024]{1,0:T(8,128)(2,1)S(1)}, bf16[2,256,1024]{2,1,0:T(8,128)(2,1)S(1)}) custom-call(s32[1]{0:T(128)} %bitcast.1.place_ref.refs_0_, bf16[128,1024]{1,0:T(8,128)(2,1)S(1)} %collective-permute-done.3.x_ref, bf16[2,4096,512]{2,1,0:T(8,128)(2,1)S(1)} %get-tuple-element.25.refs_0_, ...), custom_call_target="tpu_custom_call" | custom-call | flops 1073741824 | bytes 1048576 | tf_op jit(solution)/shard_map/pallas_call | solution.py:120
  70.7 1.2 %collective-permute-start.21 = (bf16[128,1024]{1,0:T(8,128)(2,1)S(1)}, bf16[128,1024]{1,0:T(8,128)(2,1)S(1)}, u32[]{:S(2)}, u32[]{:S(2)}) collective-permute-start(bf16[128,1024]{1,0:T(8,128)(2,1)S(1)} %get-tuple-element.36), channel_id=1, source_target_pairs={{0,1},{1,0},{2,3},{3,2},{4,5},{5,4},{6,7},{7,6},{8,9},{9,8},{10,11... | collective-permute-start | bytes 786440 | tf_op jit(solution)/shard_map/ppermute | solution.py:539
  72.0 5.4 %collective-permute-done.21.mixed_ref = bf16[128,1024]{1,0:T(8,128)(2,1)S(1)} collective-permute-done((bf16[128,1024]{1,0:T(8,128)(2,1)S(1)}, bf16[128,1024]{1,0:T(8,128)(2,1)S(1)}, u32[]{:S(2)}, u32[]{:S(2)}) %collective-permute-start.21) | collective-permute-done | bytes 262176 | tf_op jit(solution)/shard_map/ppermute | solution.py:539
  79.0 1.2 %shard_map.64.refs_4_ = bf16[256,1024]{1,0:T(8,128)(2,1)S(1)} custom-call(bf16[1,256,1024]{2,1,0:T(8,128)(2,1)S(1)} %get-tuple-element.33.q_ref.refs_1_, bf16[1,256,1024]{2,1,0:T(8,128)(2,1)S(1)} %get-tuple-element.29.refs_4_.k_ref.refs_2_, bf16[1,256,1024]{2,1,0:T(8,128)(2,1)S(1)} %shard_map.60.refs_5_.v_ref.refs_3_, ...), custom_call_target="tpu_custom_call" | custom-call | flops 268435456 | bytes 1048576 | tf_op jit(solution)/shard_map/pallas_call | solution.py:120
  80.2 3.5 %shard_map.63 = (bf16[128,1024]{1,0:T(8,128)(2,1)S(1)}, bf16[2,256,1024]{2,1,0:T(8,128)(2,1)S(1)}) custom-call(s32[1]{0:T(128)} %bitcast.1.place_ref.refs_0_, bf16[128,1024]{1,0:T(8,128)(2,1)S(1)} %collective-permute-done.x_ref, bf16[2,4096,512]{2,1,0:T(8,128)(2,1)S(1)} %get-tuple-element.25.refs_0_, ...), custom_call_target="tpu_custom_call", output_to_operand_aliasing={{1}: (9, {})} | custom-call | flops 1073741824 | bytes 1048576 | tf_op jit(solution)/shard_map/pallas_call | solution.py:120
  83.7 1.5 %collective-permute-start.4 = (bf16[128,1024]{1,0:T(8,128)(2,1)S(1)}, bf16[128,1024]{1,0:T(8,128)(2,1)S(1)}, u32[]{:S(2)}, u32[]{:S(2)}) collective-permute-start(bf16[128,1024]{1,0:T(8,128)(2,1)S(1)} %get-tuple-element.32), channel_id=1, source_target_pairs={{0,1},{1,0},{2,3},{3,2},{4,5},{5,4},{6,7},{7,6},{8,9},{9,8},{10,11... | collective-permute-start | bytes 786440 | tf_op jit(solution)/shard_map/ppermute | solution.py:541
  85.2 3.4 %copy-done.1 = bf16[8,1024,512]{2,1,0:T(8,128)(2,1)S(1)} copy-done((bf16[8,1024,512]{2,1,0:T(8,128)(2,1)S(1)}, bf16[8,1024,512]{2,1,0:T(8,128)(2,1)}, u32[]{:S(2)}) %copy-start.1) | copy-done | bytes 8388632
  88.6 3.5 %shard_map.66.total_ref = f32[256,4096]{1,0:T(8,128)S(1)} custom-call(s32[1]{0:T(128)} %bitcast.1.place_ref.refs_0_, bf16[1,256,1024]{2,1,0:T(8,128)(2,1)S(1)} %get-tuple-element.33.q_ref.refs_1_, bf16[1,256,1024]{2,1,0:T(8,128)(2,1)S(1)} %get-tuple-element.29.refs_4_.k_ref.refs_2_, bf16[1,256,1024]{2,1,0:T(8,128)(2,1)S(1)} %shard_map.60.refs_5_.v_ref.refs_3_, ...), custom_call_target="tpu_custom_call" | custom-call | flops 2147483648 | bytes 1048576 | tf_op jit(solution)/shard_map/pallas_call | solution.py:120
  92.2 2.8 %shard_map.68.refs_16_ = bf16[256,4096]{1,0:T(8,128)(2,1)} custom-call(s32[1]{0:T(128)} %bitcast.user_ref, s32[256]{0:T(256)S(1)} %copy-done.2, bf16[128,1024]{1,0:T(8,128)(2,1)S(1)} %collective-permute-done.21.mixed_ref, f32[256,4096]{1,0:T(8,128)S(1)} %shard_map.66.total_ref, bf16[1024,256]{1,0:T(8,128)(2,1)S(1)} %collective-permute-done.5.refs_0_, ...), custom_call_target="tpu_custom_call" | custom-call | flops 1073741824 | bytes 1048576 | tf_op jit(solution)/shard_map/pallas_call | solution.py:120
  95.0 2.7 %shard_map.69 = bf16[256,4096]{1,0:T(8,128)(2,1)} custom-call(s32[1]{0:T(128)} %bitcast.user_ref, s32[256]{0:T(256)S(1)} %copy-done.2, bf16[128,1024]{1,0:T(8,128)(2,1)S(1)} %collective-permute-done.4.mixed_ref, f32[256,4096]{1,0:T(8,128)S(1)} %shard_map.66.total_ref, ...), custom_call_target="tpu_custom_call", output_to_operand_aliasing={{}: (20, {})} | custom-call | flops 1073741824 | bytes 1048576 | tf_op jit(solution)/shard_map/pallas_call | solution.py:120
  (35 shorter events, 3.6 us)
Async XLA Ops:
  1.1 15.0 %collective-permute-start.5 = (bf16[1024,256]{1,0:T(8,128)(2,1)S(1)}, bf16[1024,256]{1,0:T(8,128)(2,1)S(1)}, u32[]{:S(2)}, u32[]{:S(2)}) collective-permute-start(bf16[1024,256]{1,0:T(8,128)(2,1)S(1)} %shard_map.67), channel_id=1, source_target_pairs={{0,1},{1,0},{2,3},{3,2},{4,5},{5,4},{6,7},{7,6},{8,9},{9,8},{10,11... | collective-permute-start | bytes 1572872 | tf_op jit(solution)/shard_map/ppermute | solution.py:514
  16.0 9.2 %collective-permute-start.7 = (bf16[1024,256]{1,0:T(8,128)(2,1)S(1)}, bf16[1024,256]{1,0:T(8,128)(2,1)S(1)}, u32[]{:S(2)}, u32[]{:S(2)}) collective-permute-start(bf16[1024,256]{1,0:T(8,128)(2,1)S(1)} %collective-permute-done.5.refs_0_), channel_id=1, source_target_pairs={{0,8},{2,6},{8,16},{10,2},{16,24},{18,10},{24,28},{26,18},{28,20},... | collective-permute-start | bytes 1572872 | tf_op jit(solution)/shard_map/ppermute | solution.py:520
  17.8 9.2 %collective-permute-start.6 = (bf16[1024,256]{1,0:T(8,128)(2,1)S(1)}, bf16[1024,256]{1,0:T(8,128)(2,1)S(1)}, u32[]{:S(2)}, u32[]{:S(2)}) collective-permute-start(bf16[1024,256]{1,0:T(8,128)(2,1)S(1)} %collective-permute-done.5.refs_0_), channel_id=1, source_target_pairs={{0,2},{2,0},{8,10},{10,8},{16,18},{18,16},{24,26},{26,24},{28,30},... | collective-permute-start | bytes 1572872 | tf_op jit(solution)/shard_map/ppermute | solution.py:517
  19.6 26.9 %collective-permute-start.2 = (bf16[256,2048]{1,0:T(8,128)(2,1)S(1)}, bf16[256,2048]{1,0:T(8,128)(2,1)S(1)}, u32[]{:S(2)}, u32[]{:S(2)}) collective-permute-start(bf16[256,2048]{1,0:T(8,128)(2,1)S(1)} %get-tuple-element.22.refs_0_), channel_id=1, source_target_pairs={{0,1},{1,0},{2,3},{3,2},{4,5},{5,4},{6,7},{7,6},{8,9},{9,8},{10,11... | collective-permute-start | bytes 3145736 | tf_op jit(solution)/shard_map/ppermute | solution.py:515
  25.2 14.8 %collective-permute-start.11 = (bf16[1024,256]{1,0:T(8,128)(2,1)S(1)}, bf16[1024,256]{1,0:T(8,128)(2,1)S(1)}, u32[]{:S(2)}, u32[]{:S(2)}) collective-permute-start(bf16[1024,256]{1,0:T(8,128)(2,1)S(1)} %collective-permute-done.7.refs_2_), channel_id=1, source_target_pairs={{0,8},{2,6},{8,16},{10,2},{16,24},{18,10},{24,28},{26,18},{28,20},... | collective-permute-start | bytes 1572872 | tf_op jit(solution)/shard_map/ppermute | solution.py:520
  27.0 14.6 %collective-permute-start.8 = (bf16[1024,256]{1,0:T(8,128)(2,1)S(1)}, bf16[1024,256]{1,0:T(8,128)(2,1)S(1)}, u32[]{:S(2)}, u32[]{:S(2)}) collective-permute-start(bf16[1024,256]{1,0:T(8,128)(2,1)S(1)} %collective-permute-done.6.refs_1_), channel_id=1, source_target_pairs={{0,8},{2,6},{8,16},{10,2},{16,24},{18,10},{24,28},{26,18},{28,20},... | collective-permute-start | bytes 1572872 | tf_op jit(solution)/shard_map/ppermute | solution.py:521
  28.6 28.3 %collective-permute-start.1 = (bf16[256,1024]{1,0:T(8,128)(2,1)S(1)}, bf16[256,1024]{1,0:T(8,128)(2,1)S(1)}, u32[]{:S(2)}, u32[]{:S(2)}) collective-permute-start(bf16[256,1024]{1,0:T(8,128)(2,1)S(1)} %get-tuple-element.23.refs_1_), channel_id=1, source_target_pairs={{0,1},{1,0},{2,3},{3,2},{4,5},{5,4},{6,7},{7,6},{8,9},{9,8},{10,11... | collective-permute-start | bytes 1572872 | tf_op jit(solution)/shard_map/ppermute | solution.py:515
  30.1 33.6 %collective-permute-start.3 = (bf16[128,1024]{1,0:T(8,128)(2,1)S(1)}, bf16[128,1024]{1,0:T(8,128)(2,1)S(1)}, u32[]{:S(2)}, u32[]{:S(2)}) collective-permute-start(bf16[128,1024]{1,0:T(8,128)(2,1)S(1)} %get-tuple-element.30), channel_id=1, source_target_pairs={{0,1},{1,0},{2,3},{3,2},{4,5},{5,4},{6,7},{7,6},{8,9},{9,8},{10,11... | collective-permute-start | bytes 786440 | tf_op jit(solution)/shard_map/ppermute | solution.py:515
  40.0 24.2 %collective-permute-start.15 = (bf16[1024,256]{1,0:T(8,128)(2,1)S(1)}, bf16[1024,256]{1,0:T(8,128)(2,1)S(1)}, u32[]{:S(2)}, u32[]{:S(2)}) collective-permute-start(bf16[1024,256]{1,0:T(8,128)(2,1)S(1)} %collective-permute-done.11.refs_6_), channel_id=1, source_target_pairs={{0,8},{2,6},{8,16},{10,2},{16,24},{18,10},{24,28},{26,18},{28,20},... | collective-permute-start | bytes 1572872 | tf_op jit(solution)/shard_map/ppermute | solution.py:520
  41.7 24.1 %collective-permute-start.12 = (bf16[1024,256]{1,0:T(8,128)(2,1)S(1)}, bf16[1024,256]{1,0:T(8,128)(2,1)S(1)}, u32[]{:S(2)}, u32[]{:S(2)}) collective-permute-start(bf16[1024,256]{1,0:T(8,128)(2,1)S(1)} %collective-permute-done.8.refs_3_), channel_id=1, source_target_pairs={{0,8},{2,6},{8,16},{10,2},{16,24},{18,10},{24,28},{26,18},{28,20},... | collective-permute-start | bytes 1572872 | tf_op jit(solution)/shard_map/ppermute | solution.py:521
  43.2 2.5 %copy-start.3 = (s32[2]{0:T(128)S(1)}, s32[2]{0:T(128)}, u32[]{:S(2)}) copy-start(s32[2]{0:T(128)} %counts_ref.1) | copy-start | bytes 28
  46.5 24.2 %collective-permute-start = (bf16[128,1024]{1,0:T(8,128)(2,1)S(1)}, bf16[128,1024]{1,0:T(8,128)(2,1)S(1)}, u32[]{:S(2)}, u32[]{:S(2)}) collective-permute-start(bf16[128,1024]{1,0:T(8,128)(2,1)S(1)} %get-tuple-element.21), channel_id=1, source_target_pairs={{0,1},{1,0},{2,3},{3,2},{4,5},{5,4},{6,7},{7,6},{8,9},{9,8},{10,11... | collective-permute-start | bytes 786440 | tf_op jit(solution)/shard_map/ppermute | solution.py:515
  56.9 20.4 %collective-permute-start.9 = (bf16[1024,256]{1,0:T(8,128)(2,1)S(1)}, bf16[1024,256]{1,0:T(8,128)(2,1)S(1)}, u32[]{:S(2)}, u32[]{:S(2)}) collective-permute-start(bf16[1024,256]{1,0:T(8,128)(2,1)S(1)} %collective-permute-done.7.refs_2_), channel_id=1, source_target_pairs={{0,2},{2,0},{8,10},{10,8},{16,18},{18,16},{24,26},{26,24},{28,30},... | collective-permute-start | bytes 1572872 | tf_op jit(solution)/shard_map/ppermute | solution.py:523
  60.4 3.3 %copy-start = (bf16[8,1024,512]{2,1,0:T(8,128)(2,1)}, bf16[8,1024,512]{2,1,0:T(8,128)(2,1)S(1)}, u32[]{:S(2)}) copy-start(bf16[8,1024,512]{2,1,0:T(8,128)(2,1)S(1)} %get-tuple-element.35.refs_8_) | copy-start | bytes 25165828
  63.7 14.1 %collective-permute-start.13 = (bf16[1024,256]{1,0:T(8,128)(2,1)S(1)}, bf16[1024,256]{1,0:T(8,128)(2,1)S(1)}, u32[]{:S(2)}, u32[]{:S(2)}) collective-permute-start(bf16[1024,256]{1,0:T(8,128)(2,1)S(1)} %collective-permute-done.11.refs_6_), channel_id=1, source_target_pairs={{0,2},{2,0},{8,10},{10,8},{16,18},{18,16},{24,26},{26,24},{28,30},... | collective-permute-start | bytes 1572872 | tf_op jit(solution)/shard_map/ppermute | solution.py:523
  64.2 13.7 %collective-permute-start.19 = (bf16[1024,256]{1,0:T(8,128)(2,1)S(1)}, bf16[1024,256]{1,0:T(8,128)(2,1)S(1)}, u32[]{:S(2)}, u32[]{:S(2)}) collective-permute-start(bf16[1024,256]{1,0:T(8,128)(2,1)S(1)} %collective-permute-done.15.refs_10_), channel_id=1, source_target_pairs={{0,8},{2,6},{8,16},{10,2},{16,24},{18,10},{24,28},{26,18},{28,20},... | collective-permute-start | bytes 1572872 | tf_op jit(solution)/shard_map/ppermute | solution.py:525
  65.8 13.2 %collective-permute-start.16 = (bf16[1024,256]{1,0:T(8,128)(2,1)S(1)}, bf16[1024,256]{1,0:T(8,128)(2,1)S(1)}, u32[]{:S(2)}, u32[]{:S(2)}) collective-permute-start(bf16[1024,256]{1,0:T(8,128)(2,1)S(1)} %collective-permute-done.12.refs_7_), channel_id=1, source_target_pairs={{0,8},{2,6},{8,16},{10,2},{16,24},{18,10},{24,28},{26,18},{28,20},... | collective-permute-start | bytes 1572872 | tf_op jit(solution)/shard_map/ppermute | solution.py:521
  70.7 6.6 %collective-permute-start.21 = (bf16[128,1024]{1,0:T(8,128)(2,1)S(1)}, bf16[128,1024]{1,0:T(8,128)(2,1)S(1)}, u32[]{:S(2)}, u32[]{:S(2)}) collective-permute-start(bf16[128,1024]{1,0:T(8,128)(2,1)S(1)} %get-tuple-element.36), channel_id=1, source_target_pairs={{0,1},{1,0},{2,3},{3,2},{4,5},{5,4},{6,7},{7,6},{8,9},{9,8},{10,11... | collective-permute-start | bytes 786440 | tf_op jit(solution)/shard_map/ppermute | solution.py:539
  77.3 6.4 %collective-permute-start.10 = (bf16[1024,256]{1,0:T(8,128)(2,1)S(1)}, bf16[1024,256]{1,0:T(8,128)(2,1)S(1)}, u32[]{:S(2)}, u32[]{:S(2)}) collective-permute-start(bf16[1024,256]{1,0:T(8,128)(2,1)S(1)} %collective-permute-done.8.refs_3_), channel_id=1, source_target_pairs={{0,2},{2,0},{8,10},{10,8},{16,18},{18,16},{24,26},{26,24},{28,30},... | collective-permute-start | bytes 1572872 | tf_op jit(solution)/shard_map/ppermute | solution.py:523
  77.3 14.8 %collective-permute-start.17 = (bf16[1024,256]{1,0:T(8,128)(2,1)S(1)}, bf16[1024,256]{1,0:T(8,128)(2,1)S(1)}, u32[]{:S(2)}, u32[]{:S(2)}) collective-permute-start(bf16[1024,256]{1,0:T(8,128)(2,1)S(1)} %collective-permute-done.15.refs_10_), channel_id=1, source_target_pairs={{0,2},{2,0},{8,10},{10,8},{16,18},{18,16},{24,26},{26,24},{28,30},... | collective-permute-start | bytes 1572872 | tf_op jit(solution)/shard_map/ppermute | solution.py:523
  77.8 14.3 %collective-permute-start.14 = (bf16[1024,256]{1,0:T(8,128)(2,1)S(1)}, bf16[1024,256]{1,0:T(8,128)(2,1)S(1)}, u32[]{:S(2)}, u32[]{:S(2)}) collective-permute-start(bf16[1024,256]{1,0:T(8,128)(2,1)S(1)} %collective-permute-done.12.refs_7_), channel_id=1, source_target_pairs={{0,2},{2,0},{8,10},{10,8},{16,18},{18,16},{24,26},{26,24},{28,30},... | collective-permute-start | bytes 1572872 | tf_op jit(solution)/shard_map/ppermute | solution.py:523
  77.9 14.2 %collective-permute-start.20 = (bf16[1024,256]{1,0:T(8,128)(2,1)S(1)}, bf16[1024,256]{1,0:T(8,128)(2,1)S(1)}, u32[]{:S(2)}, u32[]{:S(2)}) collective-permute-start(bf16[1024,256]{1,0:T(8,128)(2,1)S(1)} %collective-permute-done.19.refs_14_), channel_id=1, source_target_pairs={{0,2},{2,0},{8,10},{10,8},{16,18},{18,16},{24,26},{26,24},{28,30},... | collective-permute-start | bytes 1572872 | tf_op jit(solution)/shard_map/ppermute | solution.py:526
  79.0 13.2 %collective-permute-start.18 = (bf16[1024,256]{1,0:T(8,128)(2,1)S(1)}, bf16[1024,256]{1,0:T(8,128)(2,1)S(1)}, u32[]{:S(2)}, u32[]{:S(2)}) collective-permute-start(bf16[1024,256]{1,0:T(8,128)(2,1)S(1)} %collective-permute-done.16.refs_11_), channel_id=1, source_target_pairs={{0,2},{2,0},{8,10},{10,8},{16,18},{18,16},{24,26},{26,24},{28,30},... | collective-permute-start | bytes 1572872 | tf_op jit(solution)/shard_map/ppermute | solution.py:523
  83.7 11.2 %collective-permute-start.4 = (bf16[128,1024]{1,0:T(8,128)(2,1)S(1)}, bf16[128,1024]{1,0:T(8,128)(2,1)S(1)}, u32[]{:S(2)}, u32[]{:S(2)}) collective-permute-start(bf16[128,1024]{1,0:T(8,128)(2,1)S(1)} %get-tuple-element.32), channel_id=1, source_target_pairs={{0,1},{1,0},{2,3},{3,2},{4,5},{5,4},{6,7},{7,6},{8,9},{9,8},{10,11... | collective-permute-start | bytes 786440 | tf_op jit(solution)/shard_map/ppermute | solution.py:541
  85.2 3.4 %copy-start.1 = (bf16[8,1024,512]{2,1,0:T(8,128)(2,1)S(1)}, bf16[8,1024,512]{2,1,0:T(8,128)(2,1)}, u32[]{:S(2)}) copy-start(bf16[8,1024,512]{2,1,0:T(8,128)(2,1)} %copy-done) | copy-start | bytes 25165828
  88.6 3.6 %copy-start.2 = (s32[256]{0:T(256)S(1)}, s32[256]{0:T(256)}, u32[]{:S(2)}) copy-start(s32[256]{0:T(256)} %constant.10.clone.table_ref) | copy-start | bytes 3076

commit v4 on v3

--- a/solution.py
+++ b/solution.py
@@ -300,13 +300,13 @@
     return (out / total).astype(jnp.bfloat16)
 
 
-def finish(place, x, weights, offset, total, own_k, own_v, bias, kv, r, splits):
+def finish(place, x, weights, offset, total, own_k, own_v, bias, kv, row, splits):
     part_rows, depth = x.shape
     _, rows, width = total.shape
     wide = weights[0].shape[2]
     across = width // wide
-    here = slice(r * part_rows, (r + 1) * part_rows)
-    known = slice(0, (r + 1) * part_rows)
+    here = slice(row, row + part_rows)
+    known = slice(0, row + part_rows)
 
     def body(place_ref, x_ref, *refs):
         w_refs = refs[:len(weights)]
@@ -425,12 +425,12 @@
     )
 
 
-def other_out(user, table, mixed, first, pieces, total, r, out, last):
+def other_out(user, table, mixed, first, pieces, total, row, out, last):
     part_rows, depth = mixed.shape
     rows, model = total.shape
     wide = pieces[0].shape[-1]
     n = len(pieces)
-    here = slice(r * part_rows, (r + 1) * part_rows)
+    here = slice(row, row + part_rows)
 
     def body(user_ref, table_ref, mixed_ref, total_ref, *refs):
         piece_refs = refs[:n]
@@ -440,7 +440,7 @@
 
         def store(s):
             o_ref, buf, sem = refs[-3:]
-            dst = o_ref.at[pl.ds(r * part_rows, part_rows), columns(s)]
+            dst = o_ref.at[pl.ds(row, part_rows), columns(s)]
             return pltpu.make_async_copy(buf.at[s], dst, sem.at[s])
 
         for s in range(n):
@@ -504,10 +504,10 @@
 
     sizes = [model // 2, model // 4, model // 4]
     offsets = np.cumsum([0] + sizes)[:-1].tolist()
-    block = rows // 2
+    block = max(16, rows * 7 // 256 * 16)
     piece = load_piece(user, place, output_weight, model // users)
     boxes = [(0, rows, o, s) for o, s in zip(offsets, sizes)]
-    boxes += [(r * block, block, offsets[-1], sizes[-1]) for r in range(2)]
+    boxes += [(r, n, offsets[-1], sizes[-1]) for r, n in ((0, block), (block, rows - block))]
     loaded = load_rows(sessions, boxes)
     parts, sent = loaded[:3], [*loaded[:2], *loaded[3:]]
 
@@ -537,12 +537,14 @@
         place, guests[2], weights, offsets[-1], total, own_k, own_v, bias, None, 0, 1
     )
     first = lax.ppermute(first, "heads", across)
-    second, kv = finish(place, guests[3], weights, offsets[-1], total, own_k, own_v, bias, kv, 1, 1)
+    second, kv = finish(
+        place, guests[3], weights, offsets[-1], total, own_k, own_v, bias, kv, block, 1
+    )
     second = lax.ppermute(second, "heads", across)
     half_mixed = own_rest(place, own_q, own_k, own_v, alone, kv, bias)
     total = own_out(place, own_q, own_k, own_v, alone, kv, bias, half_mixed, own_weight)
     out = other_out(user, table, first, 0, pieces, total, 0, None, True)
-    return other_out(user, table, second, 0, pieces, total, 1, out, True)
+    return other_out(user, table, second, 0, pieces, total, block, out, True)
 
 
 def solution(mesh):

time: 98.1 us -> 99.1 us (1.010)
  the two profiles are of different devices: /device:TPU:0 before, /device:TPU:19 now
where the time goes in v4:
time: 99.1 us; the launch traced here: 98.9 us
  Pallas kernels  40.3 us (41%)
  waiting for transfers between devices  35.7 us (36%)
  starting transfers between devices  15.9 us (16%)
  local copies, waits for them, and re-layouts  6.64 us (7%)
    pallas_call x15, Pallas kernels, call(): pl.pallas_call(body, in_specs=in_specs, out_specs=out_specs if out_specs...  40.3 us
    ppermute x1, waiting for transfers between devices, two_halves(): crossed = lax.ppermute(piece, 'heads', across)  12.6 us
    ppermute x4, waiting for transfers between devices, two_halves(): guests = [lax.ppermute(x, 'heads', across) for x in sent]  11.4 us
    unnamed x8, local copies, waits for them, and re-layouts  6.64 us
    ppermute x1, waiting for transfers between devices, two_halves(): first = lax.ppermute(first, 'heads', across)  4.82 us
    ppermute x3, starting transfers between devices, two_halves(): lax.ppermute(far, 'users', beside)  4.03 us
    ppermute x3, waiting for transfers between devices, two_halves(): far = lax.ppermute(far, 'users', around)  3.73 us
    ppermute x4, waiting for transfers between devices, two_halves(): near = lax.ppermute(near, 'users', around)  3.19 us
  transfers between devices with their start and end apart: 22, of which 8 were waited for; matrix products, arithmetic and copies ran while one was open for 0% of the time, Pallas kernels for 37%

profile of v4, /device:TPU:19, one launch (start us, length us, event | category | flops | bytes accessed | tf_op | source)
XLA Modules:
  0.0 98.9 jit_solution(1208715604101926042)
XLA Ops:
  0.0 1.0 %shard_map.67 = bf16[1024,256]{1,0:T(8,128)(2,1)S(1)} custom-call(s32[1]{0:T(128)} %bitcast.user_ref, s32[1]{0:T(128)} %bitcast.1.place_ref.refs_0_, bf16[1024,4096]{1,0:T(8,128)(2,1)} %w_hbm.1), custom_call_target="tpu_custom_call" | custom-call | bytes 1048576 | tf_op jit(solution)/shard_map/pallas_call | solution.py:120
  1.4 12.6 %collective-permute-done.5.refs_0_ = bf16[1024,256]{1,0:T(8,128)(2,1)S(1)} collective-permute-done((bf16[1024,256]{1,0:T(8,128)(2,1)S(1)}, bf16[1024,256]{1,0:T(8,128)(2,1)S(1)}, u32[]{:S(2)}, u32[]{:S(2)}) %collective-permute-start.5) | collective-permute-done | bytes 524320 | tf_op jit(solution)/shard_map/ppermute | solution.py:514
  14.1 2.9 %collective-permute-start.6 = (bf16[1024,256]{1,0:T(8,128)(2,1)S(1)}, bf16[1024,256]{1,0:T(8,128)(2,1)S(1)}, u32[]{:S(2)}, u32[]{:S(2)}) collective-permute-start(bf16[1024,256]{1,0:T(8,128)(2,1)S(1)} %collective-permute-done.5.refs_0_), channel_id=1, source_target_pairs={{0,2},{2,0},{8,10},{10,8},{16,18},{18,16},{24,26},{26,24},{28,30},... | collective-permute-start | bytes 1572872 | tf_op jit(solution)/shard_map/ppermute | solution.py:517
  17.0 1.7 %shard_map.55 = (bf16[256,2048]{1,0:T(8,128)(2,1)S(1)}, bf16[256,1024]{1,0:T(8,128)(2,1)S(1)}, bf16[256,1024]{1,0:T(8,128)(2,1)S(1)}, bf16[112,1024]{1,0:T(8,128)(2,1)S(1)}, bf16[144,1024]{1,0:T(8,128)(2,1)S(1)}) custom-call(bf16[256,4096]{1,0:T(8,128)(2,1)} %x_hbm.1), custom_call_target="tpu_custom_call" | custom-call | bytes 1048576 | tf_op jit(solution)/shard_map/pallas_call | solution.py:120
  19.1 3.2 %collective-permute-done.7.refs_2_ = bf16[1024,256]{1,0:T(8,128)(2,1)S(1)} collective-permute-done((bf16[1024,256]{1,0:T(8,128)(2,1)S(1)}, bf16[1024,256]{1,0:T(8,128)(2,1)S(1)}, u32[]{:S(2)}, u32[]{:S(2)}) %collective-permute-start.7) | collective-permute-done | bytes 524320 | tf_op jit(solution)/shard_map/ppermute | solution.py:520
  22.9 1.2 %collective-permute-start.3 = (bf16[112,1024]{1,0:T(8,128)(2,1)S(1)}, bf16[112,1024]{1,0:T(8,128)(2,1)S(1)}, u32[]{:S(2)}, u32[]{:S(2)}) collective-permute-start(bf16[112,1024]{1,0:T(8,128)(2,1)S(1)} %get-tuple-element.30), channel_id=1, source_target_pairs={{0,1},{1,0},{2,3},{3,2},{4,5},{5,4},{6,7},{7,6},{8,9},{9,8},{10,11... | collective-permute-start | bytes 688136 | tf_op jit(solution)/shard_map/ppermute | solution.py:515
  24.1 5.9 %shard_map.56 = (bf16[1,256,1024]{2,1,0:T(8,128)(2,1)S(1)}, bf16[2,4096,512]{2,1,0:T(8,128)(2,1)S(1)}, bf16[2,4096,512]{2,1,0:T(8,128)(2,1)S(1)}) custom-call(bf16[256,2048]{1,0:T(8,128)(2,1)S(1)} %get-tuple-element.22.refs_0_, bf16[256,1024]{1,0:T(8,128)(2,1)S(1)} %get-tuple-element.23.refs_1_, bf16[256,1024]{1,0:T(8,128)(2,1)S(1)} %get-tuple-element.24.refs_2_, ...), custom_call_target="tpu_custom_call" | custom-call | flops 2147483648 | bytes 1048576 | tf_op jit(solution)/shard_map/pallas_call | solution.py:120
  30.0 3.5 %shard_map.57 = (bf16[1,256,1024]{2,1,0:T(8,128)(2,1)S(1)}, bf16[2,4096,512]{2,1,0:T(8,128)(2,1)S(1)}) custom-call(bf16[256,2048]{1,0:T(8,128)(2,1)S(1)} %get-tuple-element.22.refs_0_, bf16[256,1024]{1,0:T(8,128)(2,1)S(1)} %get-tuple-element.23.refs_1_, bf16[256,1024]{1,0:T(8,128)(2,1)S(1)} %get-tuple-element.24.refs_2_, bf16[3,4096,1024]{2,1,0:T(8,128)(2,1)} %refs_3_.5, ...), custom_call_target="tpu_custom_call" | custom-call | flops 2147483648 | bytes 1048576 | tf_op jit(solution)/shard_map/pallas_call | solution.py:120
  33.5 1.3 %collective-permute-start.15 = (bf16[1024,256]{1,0:T(8,128)(2,1)S(1)}, bf16[1024,256]{1,0:T(8,128)(2,1)S(1)}, u32[]{:S(2)}, u32[]{:S(2)}) collective-permute-start(bf16[1024,256]{1,0:T(8,128)(2,1)S(1)} %collective-permute-done.11.refs_6_), channel_id=1, source_target_pairs={{0,8},{2,6},{8,16},{10,2},{16,24},{18,10},{24,28},{26,18},{28,20},... | collective-permute-start | bytes 1572872 | tf_op jit(solution)/shard_map/ppermute | solution.py:520
  34.8 1.4 %collective-permute-done.8.refs_3_ = bf16[1024,256]{1,0:T(8,128)(2,1)S(1)} collective-permute-done((bf16[1024,256]{1,0:T(8,128)(2,1)S(1)}, bf16[1024,256]{1,0:T(8,128)(2,1)S(1)}, u32[]{:S(2)}, u32[]{:S(2)}) %collective-permute-start.8) | collective-permute-done | bytes 524320 | tf_op jit(solution)/shard_map/ppermute | solution.py:521
  36.4 2.5 %shard_map.60.refs_5_.v_ref.refs_3_ = bf16[1,256,1024]{2,1,0:T(8,128)(2,1)S(1)} custom-call(bf16[256,2048]{1,0:T(8,128)(2,1)S(1)} %get-tuple-element.22.refs_0_, bf16[256,1024]{1,0:T(8,128)(2,1)S(1)} %get-tuple-element.23.refs_1_, bf16[256,1024]{1,0:T(8,128)(2,1)S(1)} %get-tuple-element.24.refs_2_, bf16[3,4096,1024]{2,1,0:T(8,128)(2,1)} %refs_3_.5, ...), custom_call_target="tpu_custom_call" | custom-call | flops 2147483648 | bytes 1048576 | tf_op jit(solution)/shard_map/pallas_call | solution.py:120
  39.7 3.9 %collective-permute-done.2.x_ref = bf16[256,2048]{1,0:T(8,128)(2,1)S(1)} collective-permute-done((bf16[256,2048]{1,0:T(8,128)(2,1)S(1)}, bf16[256,2048]{1,0:T(8,128)(2,1)S(1)}, u32[]{:S(2)}, u32[]{:S(2)}) %collective-permute-start.2) | collective-permute-done | bytes 1048608 | tf_op jit(solution)/shard_map/ppermute | solution.py:515
  43.8 4.2 %shard_map.58.refs_3_ = f32[3,256,1024]{2,1,0:T(8,128)S(1)} custom-call(bf16[256,2048]{1,0:T(8,128)(2,1)S(1)} %collective-permute-done.2.x_ref, bf16[2,4096,512]{2,1,0:T(8,128)(2,1)S(1)} %get-tuple-element.25.refs_0_, bf16[2,4096,512]{2,1,0:T(8,128)(2,1)S(1)} %get-tuple-element.26.refs_4_.refs_1_, bf16[2,4096,512]{2,1,0:T(8,128)(2,1)S(1)} %get-tuple-element.27.refs_2_.refs_4_), custom_call_target="tpu_custom_call" | custom-call | flops 3221225472 | bytes 1048576 | tf_op jit(solution)/shard_map/pallas_call | solution.py:120
  48.0 6.7 %collective-permute-done.1.x_ref = bf16[256,1024]{1,0:T(8,128)(2,1)S(1)} collective-permute-done((bf16[256,1024]{1,0:T(8,128)(2,1)S(1)}, bf16[256,1024]{1,0:T(8,128)(2,1)S(1)}, u32[]{:S(2)}, u32[]{:S(2)}) %collective-permute-start.1) | collective-permute-done | bytes 524320 | tf_op jit(solution)/shard_map/ppermute | solution.py:515
  54.8 1.3 %collective-permute-start.9 = (bf16[1024,256]{1,0:T(8,128)(2,1)S(1)}, bf16[1024,256]{1,0:T(8,128)(2,1)S(1)}, u32[]{:S(2)}, u32[]{:S(2)}) collective-permute-start(bf16[1024,256]{1,0:T(8,128)(2,1)S(1)} %collective-permute-done.7.refs_2_), channel_id=1, source_target_pairs={{0,2},{2,0},{8,10},{10,8},{16,18},{18,16},{24,26},{26,24},{28,30},... | collective-permute-start | bytes 1572872 | tf_op jit(solution)/shard_map/ppermute | solution.py:523
  56.1 3.5 %shard_map.59 = (f32[3,256,1024]{2,1,0:T(8,128)S(1)}, bf16[8,1024,512]{2,1,0:T(8,128)(2,1)S(1)}) custom-call(bf16[256,1024]{1,0:T(8,128)(2,1)S(1)} %collective-permute-done.1.x_ref, bf16[2,4096,512]{2,1,0:T(8,128)(2,1)S(1)} %get-tuple-element.25.refs_0_, ...), custom_call_target="tpu_custom_call", output_to_operand_aliasing={{0}: (4, {})} | custom-call | flops 1610612736 | bytes 1048576 | tf_op jit(solution)/shard_map/pallas_call | solution.py:120
  59.6 3.3 %copy-done = bf16[8,1024,512]{2,1,0:T(8,128)(2,1)} copy-done((bf16[8,1024,512]{2,1,0:T(8,128)(2,1)}, bf16[8,1024,512]{2,1,0:T(8,128)(2,1)S(1)}, u32[]{:S(2)}) %copy-start) | copy-done | bytes 8388632
  63.3 1.9 %shard_map.62 = (bf16[112,1024]{1,0:T(8,128)(2,1)S(1)}, bf16[2,256,1024]{2,1,0:T(8,128)(2,1)S(1)}) custom-call(s32[1]{0:T(128)} %bitcast.1.place_ref.refs_0_, bf16[112,1024]{1,0:T(8,128)(2,1)S(1)} %collective-permute-done.3.x_ref, bf16[2,4096,512]{2,1,0:T(8,128)(2,1)S(1)} %get-tuple-element.25.refs_0_, ...), custom_call_target="tpu_custom_call" | custom-call | flops 939524096 | bytes 1048576 | tf_op jit(solution)/shard_map/pallas_call | solution.py:120
  65.2 0.8 collective-permute-done.x_ref
  66.0 1.0 collective-permute-start.21
  67.0 4.8 %collective-permute-done.21.mixed_ref = bf16[112,1024]{1,0:T(8,128)(2,1)S(1)} collective-permute-done((bf16[112,1024]{1,0:T(8,128)(2,1)S(1)}, bf16[112,1024]{1,0:T(8,128)(2,1)S(1)}, u32[]{:S(2)}, u32[]{:S(2)}) %collective-permute-start.21) | collective-permute-done | bytes 229408 | tf_op jit(solution)/shard_map/ppermute | solution.py:539
  71.8 2.2 %collective-permute-start.10 = (bf16[1024,256]{1,0:T(8,128)(2,1)S(1)}, bf16[1024,256]{1,0:T(8,128)(2,1)S(1)}, u32[]{:S(2)}, u32[]{:S(2)}) collective-permute-start(bf16[1024,256]{1,0:T(8,128)(2,1)S(1)} %collective-permute-done.8.refs_3_), channel_id=1, source_target_pairs={{0,2},{2,0},{8,10},{10,8},{16,18},{18,16},{24,26},{26,24},{28,30},... | collective-permute-start | bytes 1572872 | tf_op jit(solution)/shard_map/ppermute | solution.py:523
  74.6 2.3 %collective-permute-done.16.refs_11_ = bf16[1024,256]{1,0:T(8,128)(2,1)S(1)} collective-permute-done((bf16[1024,256]{1,0:T(8,128)(2,1)S(1)}, bf16[1024,256]{1,0:T(8,128)(2,1)S(1)}, u32[]{:S(2)}, u32[]{:S(2)}) %collective-permute-start.16) | collective-permute-done | bytes 524320 | tf_op jit(solution)/shard_map/ppermute | solution.py:521
  76.9 1.3 %collective-permute-start.18 = (bf16[1024,256]{1,0:T(8,128)(2,1)S(1)}, bf16[1024,256]{1,0:T(8,128)(2,1)S(1)}, u32[]{:S(2)}, u32[]{:S(2)}) collective-permute-start(bf16[1024,256]{1,0:T(8,128)(2,1)S(1)} %collective-permute-done.16.refs_11_), channel_id=1, source_target_pairs={{0,2},{2,0},{8,10},{10,8},{16,18},{18,16},{24,26},{26,24},{28,30},... | collective-permute-start | bytes 1572872 | tf_op jit(solution)/shard_map/ppermute | solution.py:523
  78.2 1.2 %shard_map.64.refs_4_ = bf16[256,1024]{1,0:T(8,128)(2,1)S(1)} custom-call(bf16[1,256,1024]{2,1,0:T(8,128)(2,1)S(1)} %get-tuple-element.33.q_ref.refs_1_, bf16[1,256,1024]{2,1,0:T(8,128)(2,1)S(1)} %get-tuple-element.29.refs_4_.k_ref.refs_2_, bf16[1,256,1024]{2,1,0:T(8,128)(2,1)S(1)} %shard_map.60.refs_5_.v_ref.refs_3_, ...), custom_call_target="tpu_custom_call" | custom-call | flops 268435456 | bytes 1048576 | tf_op jit(solution)/shard_map/pallas_call | solution.py:120
  79.4 2.2 %shard_map.63 = (bf16[144,1024]{1,0:T(8,128)(2,1)S(1)}, bf16[2,256,1024]{2,1,0:T(8,128)(2,1)S(1)}) custom-call(s32[1]{0:T(128)} %bitcast.1.place_ref.refs_0_, bf16[144,1024]{1,0:T(8,128)(2,1)S(1)} %collective-permute-done.x_ref, bf16[2,4096,512]{2,1,0:T(8,128)(2,1)S(1)} %get-tuple-element.25.refs_0_, ...), custom_call_target="tpu_custom_call", output_to_operand_aliasing={{1}: (9, {})} | custom-call | flops 1207959552 | bytes 1048576 | tf_op jit(solution)/shard_map/pallas_call | solution.py:120
  81.6 1.8 %collective-permute-start.4 = (bf16[144,1024]{1,0:T(8,128)(2,1)S(1)}, bf16[144,1024]{1,0:T(8,128)(2,1)S(1)}, u32[]{:S(2)}, u32[]{:S(2)}) collective-permute-start(bf16[144,1024]{1,0:T(8,128)(2,1)S(1)} %get-tuple-element.32), channel_id=1, source_target_pairs={{0,1},{1,0},{2,3},{3,2},{4,5},{5,4},{6,7},{7,6},{8,9},{9,8},{10,11... | collective-permute-start | bytes 884744 | tf_op jit(solution)/shard_map/ppermute | solution.py:543
  83.4 1.4 %shard_map.65.refs_7_ = bf16[256,512]{1,0:T(8,128)(2,1)S(1)} custom-call(s32[1]{0:T(128)} %bitcast.1.place_ref.refs_0_, bf16[1,256,1024]{2,1,0:T(8,128)(2,1)S(1)} %get-tuple-element.33.q_ref.refs_1_, bf16[1,256,1024]{2,1,0:T(8,128)(2,1)S(1)} %get-tuple-element.29.refs_4_.k_ref.refs_2_, bf16[1,256,1024]{2,1,0:T(8,128)(2,1)S(1)} %shard_map.60.refs_5_.v_ref.refs_3_, ...), custom_call_target="tpu_custom_call" | custom-call | flops 134217728 | bytes 1048576 | tf_op jit(solution)/shard_map/pallas_call | solution.py:120
  84.8 3.4 %copy-done.1 = bf16[8,1024,512]{2,1,0:T(8,128)(2,1)S(1)} copy-done((bf16[8,1024,512]{2,1,0:T(8,128)(2,1)S(1)}, bf16[8,1024,512]{2,1,0:T(8,128)(2,1)}, u32[]{:S(2)}) %copy-start.1) | copy-done | bytes 8388632
  88.2 4.9 %shard_map.66.total_ref = f32[256,4096]{1,0:T(8,128)S(1)} custom-call(s32[1]{0:T(128)} %bitcast.1.place_ref.refs_0_, bf16[1,256,1024]{2,1,0:T(8,128)(2,1)S(1)} %get-tuple-element.33.q_ref.refs_1_, bf16[1,256,1024]{2,1,0:T(8,128)(2,1)S(1)} %get-tuple-element.29.refs_4_.k_ref.refs_2_, bf16[1,256,1024]{2,1,0:T(8,128)(2,1)S(1)} %shard_map.60.refs_5_.v_ref.refs_3_, ...), custom_call_target="tpu_custom_call" | custom-call | flops 2147483648 | bytes 1048576 | tf_op jit(solution)/shard_map/pallas_call | solution.py:120
  93.1 2.7 %shard_map.68.refs_16_ = bf16[256,4096]{1,0:T(8,128)(2,1)} custom-call(s32[1]{0:T(128)} %bitcast.user_ref, s32[256]{0:T(256)S(1)} %copy-done.2, bf16[112,1024]{1,0:T(8,128)(2,1)S(1)} %collective-permute-done.21.mixed_ref, f32[256,4096]{1,0:T(8,128)S(1)} %shard_map.66.total_ref, bf16[1024,256]{1,0:T(8,128)(2,1)S(1)} %collective-permute-done.5.refs_0_, ...), custom_call_target="tpu_custom_call" | custom-call | flops 939524096 | bytes 1048576 | tf_op jit(solution)/shard_map/pallas_call | solution.py:120
  95.9 2.9 %shard_map.69 = bf16[256,4096]{1,0:T(8,128)(2,1)} custom-call(s32[1]{0:T(128)} %bitcast.user_ref, s32[256]{0:T(256)S(1)} %copy-done.2, bf16[144,1024]{1,0:T(8,128)(2,1)S(1)} %collective-permute-done.4.mixed_ref, f32[256,4096]{1,0:T(8,128)S(1)} %shard_map.66.total_ref, ...), custom_call_target="tpu_custom_call", output_to_operand_aliasing={{}: (20, {})} | custom-call | flops 1207959552 | bytes 1048576 | tf_op jit(solution)/shard_map/pallas_call | solution.py:120
  (35 shorter events, 3.6 us)
Async XLA Ops:
  1.1 12.9 %collective-permute-start.5 = (bf16[1024,256]{1,0:T(8,128)(2,1)S(1)}, bf16[1024,256]{1,0:T(8,128)(2,1)S(1)}, u32[]{:S(2)}, u32[]{:S(2)}) collective-permute-start(bf16[1024,256]{1,0:T(8,128)(2,1)S(1)} %shard_map.67), channel_id=1, source_target_pairs={{0,1},{1,0},{2,3},{3,2},{4,5},{5,4},{6,7},{7,6},{8,9},{9,8},{10,11... | collective-permute-start | bytes 1572872 | tf_op jit(solution)/shard_map/ppermute | solution.py:514
  13.9 8.3 %collective-permute-start.7 = (bf16[1024,256]{1,0:T(8,128)(2,1)S(1)}, bf16[1024,256]{1,0:T(8,128)(2,1)S(1)}, u32[]{:S(2)}, u32[]{:S(2)}) collective-permute-start(bf16[1024,256]{1,0:T(8,128)(2,1)S(1)} %collective-permute-done.5.refs_0_), channel_id=1, source_target_pairs={{0,8},{2,6},{8,16},{10,2},{16,24},{18,10},{24,28},{26,18},{28,20},... | collective-permute-start | bytes 1572872 | tf_op jit(solution)/shard_map/ppermute | solution.py:520
  14.1 8.3 %collective-permute-start.6 = (bf16[1024,256]{1,0:T(8,128)(2,1)S(1)}, bf16[1024,256]{1,0:T(8,128)(2,1)S(1)}, u32[]{:S(2)}, u32[]{:S(2)}) collective-permute-start(bf16[1024,256]{1,0:T(8,128)(2,1)S(1)} %collective-permute-done.5.refs_0_), channel_id=1, source_target_pairs={{0,2},{2,0},{8,10},{10,8},{16,18},{18,16},{24,26},{26,24},{28,30},... | collective-permute-start | bytes 1572872 | tf_op jit(solution)/shard_map/ppermute | solution.py:517
  18.8 24.8 %collective-permute-start.2 = (bf16[256,2048]{1,0:T(8,128)(2,1)S(1)}, bf16[256,2048]{1,0:T(8,128)(2,1)S(1)}, u32[]{:S(2)}, u32[]{:S(2)}) collective-permute-start(bf16[256,2048]{1,0:T(8,128)(2,1)S(1)} %get-tuple-element.22.refs_0_), channel_id=1, source_target_pairs={{0,1},{1,0},{2,3},{3,2},{4,5},{5,4},{6,7},{7,6},{8,9},{9,8},{10,11... | collective-permute-start | bytes 3145736 | tf_op jit(solution)/shard_map/ppermute | solution.py:515
  22.3 11.2 %collective-permute-start.11 = (bf16[1024,256]{1,0:T(8,128)(2,1)S(1)}, bf16[1024,256]{1,0:T(8,128)(2,1)S(1)}, u32[]{:S(2)}, u32[]{:S(2)}) collective-permute-start(bf16[1024,256]{1,0:T(8,128)(2,1)S(1)} %collective-permute-done.7.refs_2_), channel_id=1, source_target_pairs={{0,8},{2,6},{8,16},{10,2},{16,24},{18,10},{24,28},{26,18},{28,20},... | collective-permute-start | bytes 1572872 | tf_op jit(solution)/shard_map/ppermute | solution.py:520
  22.4 13.8 %collective-permute-start.8 = (bf16[1024,256]{1,0:T(8,128)(2,1)S(1)}, bf16[1024,256]{1,0:T(8,128)(2,1)S(1)}, u32[]{:S(2)}, u32[]{:S(2)}) collective-permute-start(bf16[1024,256]{1,0:T(8,128)(2,1)S(1)} %collective-permute-done.6.refs_1_), channel_id=1, source_target_pairs={{0,8},{2,6},{8,16},{10,2},{16,24},{18,10},{24,28},{26,18},{28,20},... | collective-permute-start | bytes 1572872 | tf_op jit(solution)/shard_map/ppermute | solution.py:521
  22.6 32.2 %collective-permute-start.1 = (bf16[256,1024]{1,0:T(8,128)(2,1)S(1)}, bf16[256,1024]{1,0:T(8,128)(2,1)S(1)}, u32[]{:S(2)}, u32[]{:S(2)}) collective-permute-start(bf16[256,1024]{1,0:T(8,128)(2,1)S(1)} %get-tuple-element.23.refs_1_), channel_id=1, source_target_pairs={{0,1},{1,0},{2,3},{3,2},{4,5},{5,4},{6,7},{7,6},{8,9},{9,8},{10,11... | collective-permute-start | bytes 1572872 | tf_op jit(solution)/shard_map/ppermute | solution.py:515
  22.9 40.0 %collective-permute-start.3 = (bf16[112,1024]{1,0:T(8,128)(2,1)S(1)}, bf16[112,1024]{1,0:T(8,128)(2,1)S(1)}, u32[]{:S(2)}, u32[]{:S(2)}) collective-permute-start(bf16[112,1024]{1,0:T(8,128)(2,1)S(1)} %get-tuple-element.30), channel_id=1, source_target_pairs={{0,1},{1,0},{2,3},{3,2},{4,5},{5,4},{6,7},{7,6},{8,9},{9,8},{10,11... | collective-permute-start | bytes 688136 | tf_op jit(solution)/shard_map/ppermute | solution.py:515
  33.5 29.4 %collective-permute-start.15 = (bf16[1024,256]{1,0:T(8,128)(2,1)S(1)}, bf16[1024,256]{1,0:T(8,128)(2,1)S(1)}, u32[]{:S(2)}, u32[]{:S(2)}) collective-permute-start(bf16[1024,256]{1,0:T(8,128)(2,1)S(1)} %collective-permute-done.11.refs_6_), channel_id=1, source_target_pairs={{0,8},{2,6},{8,16},{10,2},{16,24},{18,10},{24,28},{26,18},{28,20},... | collective-permute-start | bytes 1572872 | tf_op jit(solution)/shard_map/ppermute | solution.py:520
  36.2 26.9 %collective-permute-start.12 = (bf16[1024,256]{1,0:T(8,128)(2,1)S(1)}, bf16[1024,256]{1,0:T(8,128)(2,1)S(1)}, u32[]{:S(2)}, u32[]{:S(2)}) collective-permute-start(bf16[1024,256]{1,0:T(8,128)(2,1)S(1)} %collective-permute-done.8.refs_3_), channel_id=1, source_target_pairs={{0,8},{2,6},{8,16},{10,2},{16,24},{18,10},{24,28},{26,18},{28,20},... | collective-permute-start | bytes 1572872 | tf_op jit(solution)/shard_map/ppermute | solution.py:521
  36.4 2.5 %copy-start.3 = (s32[2]{0:T(128)S(1)}, s32[2]{0:T(128)}, u32[]{:S(2)}) copy-start(s32[2]{0:T(128)} %counts_ref.1) | copy-start | bytes 28
  43.5 22.5 %collective-permute-start = (bf16[144,1024]{1,0:T(8,128)(2,1)S(1)}, bf16[144,1024]{1,0:T(8,128)(2,1)S(1)}, u32[]{:S(2)}, u32[]{:S(2)}) collective-permute-start(bf16[144,1024]{1,0:T(8,128)(2,1)S(1)} %get-tuple-element.21), channel_id=1, source_target_pairs={{0,1},{1,0},{2,3},{3,2},{4,5},{5,4},{6,7},{7,6},{8,9},{9,8},{10,11... | collective-permute-start | bytes 884744 | tf_op jit(solution)/shard_map/ppermute | solution.py:515
  54.8 19.3 %collective-permute-start.9 = (bf16[1024,256]{1,0:T(8,128)(2,1)S(1)}, bf16[1024,256]{1,0:T(8,128)(2,1)S(1)}, u32[]{:S(2)}, u32[]{:S(2)}) collective-permute-start(bf16[1024,256]{1,0:T(8,128)(2,1)S(1)} %collective-permute-done.7.refs_2_), channel_id=1, source_target_pairs={{0,2},{2,0},{8,10},{10,8},{16,18},{18,16},{24,26},{26,24},{28,30},... | collective-permute-start | bytes 1572872 | tf_op jit(solution)/shard_map/ppermute | solution.py:523
  59.6 3.3 %copy-start = (bf16[8,1024,512]{2,1,0:T(8,128)(2,1)}, bf16[8,1024,512]{2,1,0:T(8,128)(2,1)S(1)}, u32[]{:S(2)}) copy-start(bf16[8,1024,512]{2,1,0:T(8,128)(2,1)S(1)} %get-tuple-element.35.refs_8_) | copy-start | bytes 25165828
  62.9 11.1 %collective-permute-start.13 = (bf16[1024,256]{1,0:T(8,128)(2,1)S(1)}, bf16[1024,256]{1,0:T(8,128)(2,1)S(1)}, u32[]{:S(2)}, u32[]{:S(2)}) collective-permute-start(bf16[1024,256]{1,0:T(8,128)(2,1)S(1)} %collective-permute-done.11.refs_6_), channel_id=1, source_target_pairs={{0,2},{2,0},{8,10},{10,8},{16,18},{18,16},{24,26},{26,24},{28,30},... | collective-permute-start | bytes 1572872 | tf_op jit(solution)/shard_map/ppermute | solution.py:523
  62.9 11.6 %collective-permute-start.19 = (bf16[1024,256]{1,0:T(8,128)(2,1)S(1)}, bf16[1024,256]{1,0:T(8,128)(2,1)S(1)}, u32[]{:S(2)}, u32[]{:S(2)}) collective-permute-start(bf16[1024,256]{1,0:T(8,128)(2,1)S(1)} %collective-permute-done.15.refs_10_), channel_id=1, source_target_pairs={{0,8},{2,6},{8,16},{10,2},{16,24},{18,10},{24,28},{26,18},{28,20},... | collective-permute-start | bytes 1572872 | tf_op jit(solution)/shard_map/ppermute | solution.py:525
  63.1 13.8 %collective-permute-start.16 = (bf16[1024,256]{1,0:T(8,128)(2,1)S(1)}, bf16[1024,256]{1,0:T(8,128)(2,1)S(1)}, u32[]{:S(2)}, u32[]{:S(2)}) collective-permute-start(bf16[1024,256]{1,0:T(8,128)(2,1)S(1)} %collective-permute-done.12.refs_7_), channel_id=1, source_target_pairs={{0,8},{2,6},{8,16},{10,2},{16,24},{18,10},{24,28},{26,18},{28,20},... | collective-permute-start | bytes 1572872 | tf_op jit(solution)/shard_map/ppermute | solution.py:521
  66.0 5.8 %collective-permute-start.21 = (bf16[112,1024]{1,0:T(8,128)(2,1)S(1)}, bf16[112,1024]{1,0:T(8,128)(2,1)S(1)}, u32[]{:S(2)}, u32[]{:S(2)}) collective-permute-start(bf16[112,1024]{1,0:T(8,128)(2,1)S(1)} %get-tuple-element.36), channel_id=1, source_target_pairs={{0,1},{1,0},{2,3},{3,2},{4,5},{5,4},{6,7},{7,6},{8,9},{9,8},{10,11... | collective-permute-start | bytes 688136 | tf_op jit(solution)/shard_map/ppermute | solution.py:539
  71.8 9.8 %collective-permute-start.10 = (bf16[1024,256]{1,0:T(8,128)(2,1)S(1)}, bf16[1024,256]{1,0:T(8,128)(2,1)S(1)}, u32[]{:S(2)}, u32[]{:S(2)}) collective-permute-start(bf16[1024,256]{1,0:T(8,128)(2,1)S(1)} %collective-permute-done.8.refs_3_), channel_id=1, source_target_pairs={{0,2},{2,0},{8,10},{10,8},{16,18},{18,16},{24,26},{26,24},{28,30},... | collective-permute-start | bytes 1572872 | tf_op jit(solution)/shard_map/ppermute | solution.py:523
  74.0 19.0 %collective-permute-start.17 = (bf16[1024,256]{1,0:T(8,128)(2,1)S(1)}, bf16[1024,256]{1,0:T(8,128)(2,1)S(1)}, u32[]{:S(2)}, u32[]{:S(2)}) collective-permute-start(bf16[1024,256]{1,0:T(8,128)(2,1)S(1)} %collective-permute-done.15.refs_10_), channel_id=1, source_target_pairs={{0,2},{2,0},{8,10},{10,8},{16,18},{18,16},{24,26},{26,24},{28,30},... | collective-permute-start | bytes 1572872 | tf_op jit(solution)/shard_map/ppermute | solution.py:523
  74.0 19.0 %collective-permute-start.14 = (bf16[1024,256]{1,0:T(8,128)(2,1)S(1)}, bf16[1024,256]{1,0:T(8,128)(2,1)S(1)}, u32[]{:S(2)}, u32[]{:S(2)}) collective-permute-start(bf16[1024,256]{1,0:T(8,128)(2,1)S(1)} %collective-permute-done.12.refs_7_), channel_id=1, source_target_pairs={{0,2},{2,0},{8,10},{10,8},{16,18},{18,16},{24,26},{26,24},{28,30},... | collective-permute-start | bytes 1572872 | tf_op jit(solution)/shard_map/ppermute | solution.py:523
  74.5 18.5 %collective-permute-start.20 = (bf16[1024,256]{1,0:T(8,128)(2,1)S(1)}, bf16[1024,256]{1,0:T(8,128)(2,1)S(1)}, u32[]{:S(2)}, u32[]{:S(2)}) collective-permute-start(bf16[1024,256]{1,0:T(8,128)(2,1)S(1)} %collective-permute-done.19.refs_14_), channel_id=1, source_target_pairs={{0,2},{2,0},{8,10},{10,8},{16,18},{18,16},{24,26},{26,24},{28,30},... | collective-permute-start | bytes 1572872 | tf_op jit(solution)/shard_map/ppermute | solution.py:526
  76.9 16.2 %collective-permute-start.18 = (bf16[1024,256]{1,0:T(8,128)(2,1)S(1)}, bf16[1024,256]{1,0:T(8,128)(2,1)S(1)}, u32[]{:S(2)}, u32[]{:S(2)}) collective-permute-start(bf16[1024,256]{1,0:T(8,128)(2,1)S(1)} %collective-permute-done.16.refs_11_), channel_id=1, source_target_pairs={{0,2},{2,0},{8,10},{10,8},{16,18},{18,16},{24,26},{26,24},{28,30},... | collective-permute-start | bytes 1572872 | tf_op jit(solution)/shard_map/ppermute | solution.py:523
  81.6 14.2 %collective-permute-start.4 = (bf16[144,1024]{1,0:T(8,128)(2,1)S(1)}, bf16[144,1024]{1,0:T(8,128)(2,1)S(1)}, u32[]{:S(2)}, u32[]{:S(2)}) collective-permute-start(bf16[144,1024]{1,0:T(8,128)(2,1)S(1)} %get-tuple-element.32), channel_id=1, source_target_pairs={{0,1},{1,0},{2,3},{3,2},{4,5},{5,4},{6,7},{7,6},{8,9},{9,8},{10,11... | collective-permute-start | bytes 884744 | tf_op jit(solution)/shard_map/ppermute | solution.py:543
  84.8 3.4 %copy-start.1 = (bf16[8,1024,512]{2,1,0:T(8,128)(2,1)S(1)}, bf16[8,1024,512]{2,1,0:T(8,128)(2,1)}, u32[]{:S(2)}) copy-start(bf16[8,1024,512]{2,1,0:T(8,128)(2,1)} %copy-done) | copy-start | bytes 25165828
  88.2 4.9 %copy-start.2 = (s32[256]{0:T(256)S(1)}, s32[256]{0:T(256)}, u32[]{:S(2)}) copy-start(s32[256]{0:T(256)} %constant.10.clone.table_ref) | copy-start | bytes 3076
